TPU v7x, 256 devices: a whole 4x4x8 slice. The times are simulated.
256 devices in a mesh: blk: 256 (over z, x, y, core).
Axes of the slice: x: 4, y: 4, z: 8, core: 2. Of those that a mesh axis runs over, the one named last changes fastest.
Arguments:
- adjacency: int32 [65536, 1280], P('blk'), may hold values 0 or 1
- weight: bfloat16 [65536, 1280], P('blk'), may hold values from -6 to 6
Outputs:
- closure: float32 [65536, 4352], P('blk')
All inputs are finite; a program needn't handle non-finite values. No bound on the sum of `adjacency` on one device may be relied on, other than what follows from the above.
Results may differ from a plain program's by a relative error of at most 0.0041.
Values may be sent and summed in bfloat16 or wider, within the bound.
No kernel may reach another device: no remote copies, remote signals or barrier semaphores. Data moves between devices by JAX's collectives and lax.ppermute only.
A program may use at most 64 MiB of HBM per device.

v0:
```python
import math

import jax
import jax.numpy as jnp
from jax import lax
from jax.sharding import PartitionSpec as P

B = 512


def shifted(value, axis, steps):
    count = lax.axis_size(axis)
    pairs = [(source, (source + steps) % count) for source in range(count)]
    return lax.ppermute(value, axis, pairs)


def banded(adjacency, weight):
    row_count = adjacency.shape[0]
    reach = (adjacency.shape[1] // row_count - 1) // 2
    local_row = lax.broadcasted_iota(jnp.int32, adjacency.shape, 0)
    offset = lax.broadcasted_iota(jnp.int32, adjacency.shape, 1) - local_row - reach * row_count
    keep = (jnp.abs(offset) <= B) & ((adjacency == 1) | (offset == 0))
    return jnp.where(keep, weight, jnp.zeros_like(weight))


def neighbours(block_rows, reach):
    below = []
    above = []
    upward = block_rows
    downward = block_rows
    for hop_count in range(reach):
        upward = shifted(upward, "blk", -1)
        downward = shifted(downward, "blk", 1)
        above.append(upward)
        below.append(downward)
    return below[::-1] + [block_rows] + above


def combine(block_rows, others, scale):
    row_count = block_rows.shape[0]
    width_cols = block_rows.shape[1]
    reach = (width_cols // row_count - 1) // 2
    result = jnp.zeros((row_count, (4 * reach + 1) * row_count), jnp.float32)
    for column, neighbour in enumerate(others):
        begin_col = column * row_count
        product = jnp.dot(
            block_rows[:, begin_col : begin_col + row_count],
            neighbour,
            preferred_element_type=jnp.float32,
        )
        result = result.at[:, begin_col : begin_col + width_cols].add(product)
    return result * scale


def local(adjacency, weight):
    matrix = banded(adjacency, weight)
    row_count = matrix.shape[0]
    reach = (matrix.shape[1] // row_count - 1) // 2
    first_scale = 1.0 / math.sqrt(B)
    second_scale = 1.0 / math.sqrt(2 * B)
    stacked = neighbours(matrix, 3 * reach)
    squared_rows = []
    for index in range(4 * reach + 1):
        squared = combine(
            stacked[index + reach], stacked[index : index + 2 * reach + 1], first_scale
        )
        squared_rows.append(squared.astype(jnp.bfloat16))
    return combine(squared_rows[2 * reach], squared_rows, second_scale)


def solution(mesh):
    in_specs = (P("blk", None), P("blk", None))
    out_specs = P("blk", None)
    return jax.shard_map(local, mesh=mesh, in_specs=in_specs, out_specs=out_specs, check_vma=False)
```

profile of v0, /device:TPU:0, one launch (start us, length us, event | category | flops | bytes accessed | tf_op | source)
XLA Modules:
  0.0 124.6 jit_solution(17119264481262830271)
XLA Ops:
  0.0 1.9 %fusion.81 = bf16[256,1280]{1,0:T(8,128)(2,1)S(1)} fusion(bf16[256,1280]{1,0:T(8,128)(2,1)} %param.111, s32[256,1280]{1,0:T(8,128)} %param.110), kind=kLoop, calls=%fused_computation.147 | loop fusion | flops 2949120 | bytes 2621440 | tf_op jit(solution)/shard_map/jit(_where)/select_n | solution.py:23
  2.0 8.3 %collective-permute-start.2 = (bf16[256,1280]{1,0:T(8,128)(2,1)S(1)}, bf16[256,1280]{1,0:T(8,128)(2,1)S(1)}, u32[]{:S(2)}, u32[]{:S(2)}) collective-permute-start(bf16[256,1280]{1,0:T(8,128)(2,1)S(1)} %fusion.81), channel_id=1, source_target_pairs={{0,255},{1,0},{2,1},{3,2},{4,3},{5,4},{6,5},{7,6},{8,7},{9,8},{10,... | collective-permute-start | bytes 1966088 | tf_op jit(solution)/shard_map/ppermute | solution.py:14
  19.6 7.3 %collective-permute-start.3 = (bf16[256,1280]{1,0:T(8,128)(2,1)S(1)}, bf16[256,1280]{1,0:T(8,128)(2,1)S(1)}, u32[]{:S(2)}, u32[]{:S(2)}) collective-permute-start(bf16[256,1280]{1,0:T(8,128)(2,1)S(1)} %collective-permute-done.2), channel_id=1, source_target_pairs={{0,255},{1,0},{2,1},{3,2},{4,3},{5,4},{6,5},{7,6},{8,7},{9,8},{10,... | collective-permute-start | bytes 1966088 | tf_op jit(solution)/shard_map/ppermute | solution.py:14
  29.0 4.9 %collective-permute-done.1 = bf16[256,1280]{1,0:T(8,128)(2,1)S(1)} collective-permute-done((bf16[256,1280]{1,0:T(8,128)(2,1)S(1)}, bf16[256,1280]{1,0:T(8,128)(2,1)S(1)}, u32[]{:S(2)}, u32[]{:S(2)}) %collective-permute-start.1) | collective-permute-done | bytes 655392 | tf_op jit(solution)/shard_map/ppermute | solution.py:14
  35.0 1.1 fusion.75
  38.4 7.2 %collective-permute-start.8 = (bf16[256,1280]{1,0:T(8,128)(2,1)S(1)}, bf16[256,1280]{1,0:T(8,128)(2,1)S(1)}, u32[]{:S(2)}, u32[]{:S(2)}) collective-permute-start(bf16[256,1280]{1,0:T(8,128)(2,1)S(1)} %collective-permute-done.3), channel_id=1, source_target_pairs={{0,255},{1,0},{2,1},{3,2},{4,3},{5,4},{6,5},{7,6},{8,7},{9,8},{10,... | collective-permute-start | bytes 1966088 | tf_op jit(solution)/shard_map/ppermute | solution.py:14
  45.5 1.2 fusion.71
  47.1 1.2 fusion.38
  50.5 3.2 %collective-permute-done.4 = bf16[256,1280]{1,0:T(8,128)(2,1)S(1)} collective-permute-done((bf16[256,1280]{1,0:T(8,128)(2,1)S(1)}, bf16[256,1280]{1,0:T(8,128)(2,1)S(1)}, u32[]{:S(2)}, u32[]{:S(2)}) %collective-permute-start.4) | collective-permute-done | bytes 655392 | tf_op jit(solution)/shard_map/ppermute | solution.py:14
  55.2 1.1 fusion.49
  57.3 1.2 fusion.45
  58.9 7.2 %collective-permute-start.9 = (bf16[256,1280]{1,0:T(8,128)(2,1)S(1)}, bf16[256,1280]{1,0:T(8,128)(2,1)S(1)}, u32[]{:S(2)}, u32[]{:S(2)}) collective-permute-start(bf16[256,1280]{1,0:T(8,128)(2,1)S(1)} %collective-permute-done.8), channel_id=1, source_target_pairs={{0,255},{1,0},{2,1},{3,2},{4,3},{5,4},{6,5},{7,6},{8,7},{9,8},{10,... | collective-permute-start | bytes 1966088 | tf_op jit(solution)/shard_map/ppermute | solution.py:14
  66.5 1.2 fusion.31
  74.2 1.2 fusion.52
  75.8 7.2 %collective-permute-start.10 = (bf16[256,1280]{1,0:T(8,128)(2,1)S(1)}, bf16[256,1280]{1,0:T(8,128)(2,1)S(1)}, u32[]{:S(2)}, u32[]{:S(2)}) collective-permute-start(bf16[256,1280]{1,0:T(8,128)(2,1)S(1)} %collective-permute-done.9), channel_id=1, source_target_pairs={{0,255},{1,0},{2,1},{3,2},{4,3},{5,4},{6,5},{7,6},{8,7},{9,8},{10,... | collective-permute-start | bytes 1966088 | tf_op jit(solution)/shard_map/ppermute | solution.py:14
  83.4 1.2 fusion.24
  85.7 1.1 fusion.21
  89.1 1.1 fusion.62
  91.2 1.2 fusion.58
  92.7 7.5 %collective-permute-start.11 = (bf16[256,1280]{1,0:T(8,128)(2,1)S(1)}, bf16[256,1280]{1,0:T(8,128)(2,1)S(1)}, u32[]{:S(2)}, u32[]{:S(2)}) collective-permute-start(bf16[256,1280]{1,0:T(8,128)(2,1)S(1)} %collective-permute-done.10), channel_id=1, source_target_pairs={{0,255},{1,0},{2,1},{3,2},{4,3},{5,4},{6,5},{7,6},{8,7},{9,8},{10,... | collective-permute-start | bytes 1966088 | tf_op jit(solution)/shard_map/ppermute | solution.py:14
  100.6 1.2 fusion.17
  101.7 2.8 %collective-permute-done.7 = bf16[256,1280]{1,0:T(8,128)(2,1)S(1)} collective-permute-done((bf16[256,1280]{1,0:T(8,128)(2,1)S(1)}, bf16[256,1280]{1,0:T(8,128)(2,1)S(1)}, u32[]{:S(2)}, u32[]{:S(2)}) %collective-permute-start.7) | collective-permute-done | bytes 655392 | tf_op jit(solution)/shard_map/ppermute | solution.py:14
  107.7 1.2 fusion.64
  109.3 1.2 convolution_select_fusion
  110.8 1.4 %fusion.14 = f32[256,4352]{1,0:T(8,128)S(1)} fusion(f32[256,4352]{1,0:T(8,128)S(1)} %scatter-add.196, f32[256,2304]{1,0:T(8,128)S(1)} %fusion.76, pred[]{:T(512)} %compare_reduce_fusion.6, bf16[256,2304]{1,0:T(8,128)(2,1)S(1)} %multiply_convert_fusion.8), kind=kOutput, calls=%fused_computation.23 | convolution fusion | flops 304349184 | bytes 7208961 | tf_op jit(solution)/shard_map/dot_general | solution.py:46
  112.2 1.5 %fusion.12 = f32[256,4352]{1,0:T(8,128)S(1)} fusion(f32[256,4352]{1,0:T(8,128)S(1)} %fusion.14, f32[256,2304]{1,0:T(8,128)S(1)} %fusion.50, pred[]{:T(512)} %compare_reduce_fusion.5, bf16[256,2304]{1,0:T(8,128)(2,1)S(1)} %multiply_convert_fusion.8), kind=kOutput, calls=%fused_computation.20 | convolution fusion | flops 304349184 | bytes 7208961 | tf_op jit(solution)/shard_map/dot_general | solution.py:46
  113.7 1.5 %fusion.10 = f32[256,4352]{1,0:T(8,128)S(1)} fusion(f32[256,4352]{1,0:T(8,128)S(1)} %fusion.12, f32[256,2304]{1,0:T(8,128)S(1)} %fusion.43, pred[]{:T(512)} %compare_reduce_fusion.4, bf16[256,2304]{1,0:T(8,128)(2,1)S(1)} %multiply_convert_fusion.8), kind=kOutput, calls=%fused_computation.17 | convolution fusion | flops 304349184 | bytes 7208961 | tf_op jit(solution)/shard_map/dot_general | solution.py:46
  115.2 1.4 %fusion.8 = f32[256,4352]{1,0:T(8,128)S(1)} fusion(f32[256,4352]{1,0:T(8,128)S(1)} %fusion.10, bf16[256,2304]{1,0:T(8,128)(2,1)S(1)} %multiply_convert_fusion.8, pred[]{:T(512)} %compare_reduce_fusion.3), kind=kOutput, calls=%fused_computation.14 | convolution fusion | flops 303169536 | bytes 6029313 | tf_op jit(solution)/shard_map/dot_general | solution.py:46
  116.6 1.5 %fusion.6 = f32[256,4352]{1,0:T(8,128)S(1)} fusion(f32[256,4352]{1,0:T(8,128)S(1)} %fusion.8, f32[256,2304]{1,0:T(8,128)S(1)} %fusion.36, pred[]{:T(512)} %compare_reduce_fusion.2, bf16[256,2304]{1,0:T(8,128)(2,1)S(1)} %multiply_convert_fusion.8), kind=kOutput, calls=%fused_computation.11 | convolution fusion | flops 304349184 | bytes 7208961 | tf_op jit(solution)/shard_map/dot_general | solution.py:46
  118.1 1.4 %fusion.4 = f32[256,4352]{1,0:T(8,128)S(1)} fusion(f32[256,4352]{1,0:T(8,128)S(1)} %fusion.6, f32[256,2304]{1,0:T(8,128)S(1)} %fusion.29, pred[]{:T(512)} %compare_reduce_fusion.1, bf16[256,2304]{1,0:T(8,128)(2,1)S(1)} %multiply_convert_fusion.8), kind=kOutput, calls=%fused_computation.8 | convolution fusion | flops 304349184 | bytes 7208961 | tf_op jit(solution)/shard_map/dot_general | solution.py:46
  119.6 1.6 %fusion.2 = f32[256,4352]{1,0:T(8,128)S(1)} fusion(f32[256,4352]{1,0:T(8,128)S(1)} %fusion.4, f32[256,2304]{1,0:T(8,128)S(1)} %fusion.22, pred[]{:T(512)} %compare_reduce_fusion, bf16[256,2304]{1,0:T(8,128)(2,1)S(1)} %multiply_convert_fusion.8), kind=kOutput, calls=%fused_computation.5 | convolution fusion | flops 304349184 | bytes 7208961 | tf_op jit(solution)/shard_map/dot_general | solution.py:46
  122.2 2.4 %broadcast_multiply_fusion = f32[256,4352]{1,0:T(8,128)} fusion(f32[256,4352]{1,0:T(8,128)S(1)} %fusion), kind=kLoop, calls=%fused_computation.137 | loop fusion | flops 1114112 | bytes 8912896 | tf_op jit(solution)/shard_map/mul | solution.py:52
  (70 shorter events, 37.7 us)
Async XLA Ops:
  1.9 16.6 %collective-permute-start = (bf16[256,1280]{1,0:T(8,128)(2,1)S(1)}, bf16[256,1280]{1,0:T(8,128)(2,1)S(1)}, u32[]{:S(2)}, u32[]{:S(2)}) collective-permute-start(bf16[256,1280]{1,0:T(8,128)(2,1)S(1)} %fusion.81), channel_id=1, source_target_pairs={{0,1},{1,2},{2,3},{3,4},{4,5},{5,6},{6,7},{7,8},{8,9},{9,10},{10,1... | collective-permute-start | bytes 1966088 | tf_op jit(solution)/shard_map/ppermute | solution.py:14
  2.0 16.5 %collective-permute-start.2 = (bf16[256,1280]{1,0:T(8,128)(2,1)S(1)}, bf16[256,1280]{1,0:T(8,128)(2,1)S(1)}, u32[]{:S(2)}, u32[]{:S(2)}) collective-permute-start(bf16[256,1280]{1,0:T(8,128)(2,1)S(1)} %fusion.81), channel_id=1, source_target_pairs={{0,255},{1,0},{2,1},{3,2},{4,3},{5,4},{6,5},{7,6},{8,7},{9,8},{10,... | collective-permute-start | bytes 1966088 | tf_op jit(solution)/shard_map/ppermute | solution.py:14
  18.4 15.4 %collective-permute-start.1 = (bf16[256,1280]{1,0:T(8,128)(2,1)S(1)}, bf16[256,1280]{1,0:T(8,128)(2,1)S(1)}, u32[]{:S(2)}, u32[]{:S(2)}) collective-permute-start(bf16[256,1280]{1,0:T(8,128)(2,1)S(1)} %collective-permute-done), channel_id=1, source_target_pairs={{0,1},{1,2},{2,3},{3,4},{4,5},{5,6},{6,7},{7,8},{8,9},{9,10},{10,1... | collective-permute-start | bytes 1966088 | tf_op jit(solution)/shard_map/ppermute | solution.py:14
  19.6 17.5 %collective-permute-start.3 = (bf16[256,1280]{1,0:T(8,128)(2,1)S(1)}, bf16[256,1280]{1,0:T(8,128)(2,1)S(1)}, u32[]{:S(2)}, u32[]{:S(2)}) collective-permute-start(bf16[256,1280]{1,0:T(8,128)(2,1)S(1)} %collective-permute-done.2), channel_id=1, source_target_pairs={{0,255},{1,0},{2,1},{3,2},{4,3},{5,4},{6,5},{7,6},{8,7},{9,8},{10,... | collective-permute-start | bytes 1966088 | tf_op jit(solution)/shard_map/ppermute | solution.py:14
  38.3 15.5 %collective-permute-start.4 = (bf16[256,1280]{1,0:T(8,128)(2,1)S(1)}, bf16[256,1280]{1,0:T(8,128)(2,1)S(1)}, u32[]{:S(2)}, u32[]{:S(2)}) collective-permute-start(bf16[256,1280]{1,0:T(8,128)(2,1)S(1)} %collective-permute-done.1), channel_id=1, source_target_pairs={{0,1},{1,2},{2,3},{3,4},{4,5},{5,6},{6,7},{7,8},{8,9},{9,10},{10,1... | collective-permute-start | bytes 1966088 | tf_op jit(solution)/shard_map/ppermute | solution.py:14
  38.4 20.5 %collective-permute-start.8 = (bf16[256,1280]{1,0:T(8,128)(2,1)S(1)}, bf16[256,1280]{1,0:T(8,128)(2,1)S(1)}, u32[]{:S(2)}, u32[]{:S(2)}) collective-permute-start(bf16[256,1280]{1,0:T(8,128)(2,1)S(1)} %collective-permute-done.3), channel_id=1, source_target_pairs={{0,255},{1,0},{2,1},{3,2},{4,3},{5,4},{6,5},{7,6},{8,7},{9,8},{10,... | collective-permute-start | bytes 1966088 | tf_op jit(solution)/shard_map/ppermute | solution.py:14
  54.9 16.0 %collective-permute-start.5 = (bf16[256,1280]{1,0:T(8,128)(2,1)S(1)}, bf16[256,1280]{1,0:T(8,128)(2,1)S(1)}, u32[]{:S(2)}, u32[]{:S(2)}) collective-permute-start(bf16[256,1280]{1,0:T(8,128)(2,1)S(1)} %collective-permute-done.4), channel_id=1, source_target_pairs={{0,1},{1,2},{2,3},{3,4},{4,5},{5,6},{6,7},{7,8},{8,9},{9,10},{10,1... | collective-permute-start | bytes 1966088 | tf_op jit(solution)/shard_map/ppermute | solution.py:14
  58.9 16.9 %collective-permute-start.9 = (bf16[256,1280]{1,0:T(8,128)(2,1)S(1)}, bf16[256,1280]{1,0:T(8,128)(2,1)S(1)}, u32[]{:S(2)}, u32[]{:S(2)}) collective-permute-start(bf16[256,1280]{1,0:T(8,128)(2,1)S(1)} %collective-permute-done.8), channel_id=1, source_target_pairs={{0,255},{1,0},{2,1},{3,2},{4,3},{5,4},{6,5},{7,6},{8,7},{9,8},{10,... | collective-permute-start | bytes 1966088 | tf_op jit(solution)/shard_map/ppermute | solution.py:14
  72.0 15.8 %collective-permute-start.6 = (bf16[256,1280]{1,0:T(8,128)(2,1)S(1)}, bf16[256,1280]{1,0:T(8,128)(2,1)S(1)}, u32[]{:S(2)}, u32[]{:S(2)}) collective-permute-start(bf16[256,1280]{1,0:T(8,128)(2,1)S(1)} %collective-permute-done.5), channel_id=1, source_target_pairs={{0,1},{1,2},{2,3},{3,4},{4,5},{5,6},{6,7},{7,8},{8,9},{9,10},{10,1... | collective-permute-start | bytes 1966088 | tf_op jit(solution)/shard_map/ppermute | solution.py:14
  75.8 16.9 %collective-permute-start.10 = (bf16[256,1280]{1,0:T(8,128)(2,1)S(1)}, bf16[256,1280]{1,0:T(8,128)(2,1)S(1)}, u32[]{:S(2)}, u32[]{:S(2)}) collective-permute-start(bf16[256,1280]{1,0:T(8,128)(2,1)S(1)} %collective-permute-done.9), channel_id=1, source_target_pairs={{0,255},{1,0},{2,1},{3,2},{4,3},{5,4},{6,5},{7,6},{8,7},{9,8},{10,... | collective-permute-start | bytes 1966088 | tf_op jit(solution)/shard_map/ppermute | solution.py:14
  89.0 15.5 %collective-permute-start.7 = (bf16[256,1280]{1,0:T(8,128)(2,1)S(1)}, bf16[256,1280]{1,0:T(8,128)(2,1)S(1)}, u32[]{:S(2)}, u32[]{:S(2)}) collective-permute-start(bf16[256,1280]{1,0:T(8,128)(2,1)S(1)} %collective-permute-done.6), channel_id=1, source_target_pairs={{0,1},{1,2},{2,3},{3,4},{4,5},{5,6},{6,7},{7,8},{8,9},{9,10},{10,1... | collective-permute-start | bytes 1966088 | tf_op jit(solution)/shard_map/ppermute | solution.py:14
  92.7 28.4 %collective-permute-start.11 = (bf16[256,1280]{1,0:T(8,128)(2,1)S(1)}, bf16[256,1280]{1,0:T(8,128)(2,1)S(1)}, u32[]{:S(2)}, u32[]{:S(2)}) collective-permute-start(bf16[256,1280]{1,0:T(8,128)(2,1)S(1)} %collective-permute-done.10), channel_id=1, source_target_pairs={{0,255},{1,0},{2,1},{3,2},{4,3},{5,4},{6,5},{7,6},{8,7},{9,8},{10,... | collective-permute-start | bytes 1966088 | tf_op jit(solution)/shard_map/ppermute | solution.py:14
where the time goes:
time: 125 us
  matrix products  53.5 us (43%)
  starting transfers between devices  45.3 us (36%)
  other arithmetic  11.9 us (10%)
  waiting for transfers between devices  11.6 us (9%)
  local copies, waits for them, and re-layouts  1.68 us (1%)
    dot_general x54, matrix products, combine(): jnp.dot(block_rows[:, begin_col:begin_col + row_count], neighbour, prefer...  53.5 us
    ppermute x12, starting transfers between devices, shifted(): return lax.ppermute(value, axis, pairs)  45.3 us
    ppermute x12, waiting for transfers between devices, shifted(): return lax.ppermute(value, axis, pairs)  11.6 us
    another operation x11, other arithmetic  7.41 us
  transfers between devices with their start and end apart: 12, of which 4 were waited for; matrix products, arithmetic and copies ran while one was open for 49% of the time, Pallas kernels for 0%

commit v1 on v0

v1 whole, which is shorter than its diff:
```python
import math

import jax
import jax.numpy as jnp
from jax import lax
from jax.experimental import pallas as pl
from jax.experimental.pallas import tpu as pltpu
from jax.sharding import PartitionSpec as P

B = 512
R = 256
LANES = 128
TILES = 1024 // LANES
ROWS = TILES * R + 16
FIRST_SCALE = 1.0 / math.sqrt(B)
LAST_SCALE = 1.0 / (math.sqrt(B) * math.sqrt(2 * B))
MIB = 1 << 20


def pack_kernel(adjacency_ref, weight_ref, packed_ref, far_ref):
    step = pl.program_id(0)
    count = adjacency_ref.shape[0]
    row = lax.broadcasted_iota(jnp.int32, (count, LANES), 0) + step * count
    lane = lax.broadcasted_iota(jnp.int32, (count, LANES), 1)

    def tile(index):
        columns = slice(index * LANES, (index + 1) * LANES)
        edge = adjacency_ref[:, columns] == 1
        value = weight_ref[:, columns].astype(jnp.float32)
        return edge, value

    for half in range(2):
        column = lane + half * LANES
        near_edge, near = tile(half)
        far_edge, far = tile(8 + half)
        near = jnp.where(near_edge, near, 0.0)
        far = jnp.where(far_edge, far, 0.0)
        merged = jnp.where(column >= row, near, far)
        packed_ref[pl.ds(half * R + step * count, count), :] = merged.astype(jnp.bfloat16)
        diagonal = jnp.sum(jnp.where(column == row, far, 0.0), axis=0, keepdims=True)
        previous = jnp.where(step == 0, 0.0, far_ref[half : half + 1, :])
        far_ref[half : half + 1, :] = previous + diagonal
    for index in range(2, 8):
        edge, value = tile(index)
        if index in (4, 5):
            edge = edge | (lane + (index - 4) * LANES == row)
        kept = jnp.where(edge, value, 0.0)
        packed_ref[pl.ds(index * R + step * count, count), :] = kept.astype(jnp.bfloat16)

    @pl.when(step == pl.num_programs(0) - 1)
    def _():
        place = lax.broadcasted_iota(jnp.int32, (16, LANES), 0)
        first = jnp.where(place == 0, far_ref[0:1, :], 0.0)
        both = first + jnp.where(place == 1, far_ref[1:2, :], 0.0)
        packed_ref[TILES * R :, :] = both.astype(jnp.bfloat16)


def pack(adjacency, weight):
    steps = 4
    return pl.pallas_call(
        pack_kernel,
        grid=(steps,),
        in_specs=[pl.BlockSpec((R // steps, 5 * R), lambda i: (i, 0))] * 2,
        out_specs=pl.BlockSpec((ROWS, LANES), lambda i: (0, 0)),
        out_shape=jax.ShapeDtypeStruct((ROWS, LANES), jnp.bfloat16),
        scratch_shapes=[pltpu.VMEM((8, LANES), jnp.float32)],
        compiler_params=pltpu.CompilerParams(vmem_limit_bytes=16 * MIB),
        cost_estimate=pl.CostEstimate(flops=R * 5 * R * 4, bytes_accessed=R * 5 * R * 6 + ROWS * 256, transcendentals=0),
    )(adjacency, weight)


def slot(ref, index):
    begin = index * 2 * R
    return jnp.concatenate([ref[begin : begin + R, :], ref[begin + R : begin + 2 * R, :]], axis=1)


def unpacked(ref):
    row = lax.broadcasted_iota(jnp.int32, (R, R), 0)
    column = lax.broadcasted_iota(jnp.int32, (R, R), 1)
    merged = slot(ref, 0).astype(jnp.float32)
    tail = ref[TILES * R :, :].astype(jnp.float32)
    diagonal = jnp.concatenate([tail[0:1, :], tail[1:2, :]], axis=1)
    first = jnp.where(column >= row, merged, 0.0)
    last = jnp.where(column < row, merged, jnp.where(column == row, diagonal, 0.0))
    return [
        first.astype(jnp.bfloat16),
        slot(ref, 1),
        slot(ref, 2),
        slot(ref, 3),
        last.astype(jnp.bfloat16),
    ]


def block(index):
    return pl.ds(pl.multiple_of(index * R, R), R)


def accumulate(total_ref, left, ref, first_block):
    for offset, right in enumerate(unpacked(ref)):
        where = block(first_block + offset)
        total_ref[:, where] += jnp.dot(left, right, preferred_element_type=jnp.float32)


def square_kernel(sign_ref, own, n1, p1, n2, p2, result_ref, left_ref, total_ref):
    sign = sign_ref[0]
    for offset, part in enumerate(unpacked(own)):
        left_ref[:, offset * R : (offset + 1) * R] = part
    total_ref[...] = jnp.zeros_like(total_ref)
    for reach, ref in ((0, own), (1, p1), (-1, n1), (2, p2), (-2, n2)):
        at = reach * sign
        accumulate(total_ref, left_ref[:, block(at + 2)], ref, at + 2)
    result_ref[...] = (total_ref[...] * FIRST_SCALE).astype(jnp.bfloat16)


def cube_kernel(sign_ref, left_ref, d0, n1, p1, n2, p2, n3, p3, n4, p4, cube_ref, sum_ref, total_ref):
    sign = sign_ref[0]
    known = ((0, d0), (1, p1), (-1, n1), (2, p2), (-2, n2), (3, p3), (-3, n3), (4, p4), (-4, n4))
    total_ref[...] = jnp.zeros_like(total_ref)
    for reach, ref in known:
        at = reach * sign
        accumulate(total_ref, left_ref[:, block(at + 4)], ref, at + 4)
    cube_ref[...] = total_ref[...].astype(jnp.bfloat16)
    sum_ref[...] = jnp.zeros_like(sum_ref)
    for reach, ref in known:
        at = reach * sign
        accumulate(sum_ref, cube_ref[:, block(at + 6)], ref, at + 4)


def far_kernel(sign_ref, cube_ref, sum_ref, n5, p5, p6, out_ref, last_ref):
    sign = sign_ref[0]
    out_ref[:, : 2 * R] = jnp.zeros((R, 2 * R), jnp.float32)
    out_ref[:, 15 * R :] = jnp.zeros((R, 2 * R), jnp.float32)
    out_ref[:, 2 * R : 15 * R] = sum_ref[...]
    for reach, ref in ((5, p5), (-5, n5), (6, p6)):
        at = reach * sign
        accumulate(out_ref, cube_ref[:, block(at + 6)], ref, at + 6)
    out_ref[...] = out_ref[...] * LAST_SCALE
    last_ref[...] = cube_ref[:, block(6 - 6 * sign)]


def edge_kernel(left_ref, n6, before_ref, out_ref):
    step = pl.program_id(0)
    for offset, right in enumerate(unpacked(n6)):

        @pl.when(step == offset)
        def _():
            product = jnp.dot(left_ref[...], right, preferred_element_type=jnp.float32)
            out_ref[...] = before_ref[...] + product * LAST_SCALE


def edge_call(sign, left, n6, before):
    def place(i, sign_ref):
        return (0, 6 - 6 * sign_ref[0] + i)

    def kernel(sign_ref, *refs):
        edge_kernel(*refs)

    return pl.pallas_call(
        kernel,
        grid_spec=pltpu.PrefetchScalarGridSpec(
            num_scalar_prefetch=1,
            grid=(5,),
            in_specs=[
                pl.BlockSpec((R, R), lambda i, s: (0, 0)),
                pl.BlockSpec((ROWS, LANES), lambda i, s: (0, 0)),
                pl.BlockSpec((R, R), place),
            ],
            out_specs=pl.BlockSpec((R, R), place),
        ),
        out_shape=jax.ShapeDtypeStruct(before.shape, jnp.float32),
        input_output_aliases={3: 0},
        compiler_params=pltpu.CompilerParams(vmem_limit_bytes=16 * MIB),
        cost_estimate=cost(1, 2 * 5 * R * R * 4),
    )(sign, left, n6, before)


def cost(count, more):
    return pl.CostEstimate(
        flops=count * 2 * R * R * 5 * R, bytes_accessed=count * ROWS * LANES * 2 + more, transcendentals=0
    )


def call(kernel, arrays, shapes, scratch, count, more):
    specs = [pl.BlockSpec(memory_space=pltpu.SMEM)]
    specs += [pl.BlockSpec(memory_space=pltpu.VMEM)] * (len(arrays) - 1)
    return pl.pallas_call(
        kernel,
        in_specs=specs,
        out_specs=[pl.BlockSpec(memory_space=pltpu.VMEM)] * len(shapes),
        out_shape=shapes,
        scratch_shapes=scratch,
        compiler_params=pltpu.CompilerParams(vmem_limit_bytes=40 * MIB),
        cost_estimate=cost(count, more),
    )(*arrays)


def local(adjacency, weight):
    size = lax.axis_size("blk")
    parity = lax.rem(lax.axis_index("blk"), 2)
    sign = (1 - 2 * parity).astype(jnp.int32).reshape(1)

    def hop(value, steps):
        pairs = []
        for target in range(size):
            ahead = steps if target % 2 == 0 else -steps
            pairs.append(((target + ahead) % size, target))
        return lax.ppermute(value, "blk", pairs)

    def peer(value):
        return lax.ppermute(value, "blk", [(source, source ^ 1) for source in range(size)])

    own = pack(adjacency, weight)
    p2 = hop(own, 2)
    p1 = peer(own)
    held, p1 = lax.optimization_barrier((own, p1))
    n2 = hop(held, -2)
    p4 = hop(p2, 2)
    n1 = peer(p2)
    n4 = hop(n2, -2)
    p3 = peer(n2)
    f32, bf16 = jnp.float32, jnp.bfloat16
    (square,) = call(
        square_kernel,
        (sign, own, n1, p1, n2, p2),
        [jax.ShapeDtypeStruct((R, 9 * R), bf16)],
        [pltpu.VMEM((R, 5 * R), bf16), pltpu.VMEM((R, 9 * R), f32)],
        5,
        9 * R * R * 2,
    )
    p6 = hop(p4, 2)
    n3 = peer(p4)
    n6 = hop(n4, -2)
    p5 = peer(n4)
    cube, total = call(
        cube_kernel,
        (sign, square, own, n1, p1, n2, p2, n3, p3, n4, p4),
        [jax.ShapeDtypeStruct((R, 13 * R), bf16), jax.ShapeDtypeStruct((R, 13 * R), f32)],
        [pltpu.VMEM((R, 13 * R), f32)],
        18,
        28 * R * R * 2,
    )
    n5 = peer(p6)
    before, last = call(
        far_kernel,
        (sign, cube, total, n5, p5, p6),
        [jax.ShapeDtypeStruct((R, 17 * R), f32), jax.ShapeDtypeStruct((R, R), bf16)],
        [],
        3,
        30 * R * R * 4,
    )
    return edge_call(sign, last, n6, before)


def solution(mesh):
    in_specs = (P("blk", None), P("blk", None))
    out_specs = P("blk", None)
    return jax.shard_map(local, mesh=mesh, in_specs=in_specs, out_specs=out_specs, check_vma=False)
```

time: 125 us -> 86.8 us (0.69)
  the two profiles are of different devices: /device:TPU:0 before, /device:TPU:1 now
where the time goes in v1:
time: 86.8 us; the launch traced here: 86.5 us
  starting transfers between devices  53.5 us (62%)
  Pallas kernels  17.7 us (20%)
  waiting for transfers between devices  12.9 us (15%)
  local copies, waits for them, and re-layouts  2.4 us (3%)
    ppermute x6, starting transfers between devices, peer(): lax.ppermute(value, 'blk', [(source, source ^ 1) for source in range(size)])  30.1 us
    ppermute x6, starting transfers between devices, hop(): return lax.ppermute(value, 'blk', pairs)  23.4 us
    pallas_call x3, Pallas kernels, call(): pl.pallas_call(kernel, in_specs=specs, out_specs=[pl.BlockSpec(memory_spa...  12.5 us
    ppermute x6, waiting for transfers between devices, hop(): return lax.ppermute(value, 'blk', pairs)  11.3 us
    pallas_call x1, Pallas kernels, edge_call(): pl.pallas_call(kernel, grid_spec=pltpu.PrefetchScalarGridSpec(num_scalar_...  4.86 us
    unnamed x4, local copies, waits for them, and re-layouts  2.4 us
  transfers between devices with their start and end apart: 12, of which 4 were waited for; matrix products, arithmetic and copies ran while one was open for 0% of the time, Pallas kernels for 14%

profile of v1, /device:TPU:1, one launch (start us, length us, event | category | flops | bytes accessed | tf_op | source)
XLA Modules:
  0.0 86.5 jit_solution(14068620414769729221)
XLA Ops:
  0.0 0.0 copy-start
  0.0 1.3 %copy-done = s32[256,1280]{1,0:T(8,128)S(1)} copy-done((s32[256,1280]{1,0:T(8,128)S(1)}, s32[256,1280]{1,0:T(8,128)}, u32[]{:S(2)}) %copy-start) | copy-done | bytes 1310744
  1.3 1.1 %copy-done.1 = bf16[256,1280]{1,0:T(8,128)(2,1)S(1)} copy-done((bf16[256,1280]{1,0:T(8,128)(2,1)S(1)}, bf16[256,1280]{1,0:T(8,128)(2,1)}, u32[]{:S(2)}) %copy-start.1) | copy-done | bytes 655384
  2.4 0.3 shard_map.28.own.d0
  2.7 3.3 %collective-permute-start.2 = (bf16[2064,128]{1,0:T(8,128)(2,1)S(1)}, bf16[2064,128]{1,0:T(8,128)(2,1)S(1)}, u32[]{:S(2)}, u32[]{:S(2)}) collective-permute-start(bf16[2064,128]{1,0:T(8,128)(2,1)S(1)} %shard_map.28.own.d0), channel_id=1, source_target_pairs={{0,1},{1,0},{2,3},{3,2},{4,5},{5,4},{6,7},{7,6},{8,9},{9,8},{10,11... | collective-permute-start | bytes 1585160 | tf_op jit(solution)/shard_map/ppermute | solution.py:210
  6.0 0.0 collective-permute-start
  6.0 1.5 %collective-permute-done.2.p1 = bf16[2064,128]{1,0:T(8,128)(2,1)S(1)} collective-permute-done((bf16[2064,128]{1,0:T(8,128)(2,1)S(1)}, bf16[2064,128]{1,0:T(8,128)(2,1)S(1)}, u32[]{:S(2)}, u32[]{:S(2)}) %collective-permute-start.2) | collective-permute-done | bytes 528416 | tf_op jit(solution)/shard_map/ppermute | solution.py:210
  7.6 8.5 %collective-permute-start.3 = (bf16[2064,128]{1,0:T(8,128)(2,1)S(1)}, bf16[2064,128]{1,0:T(8,128)(2,1)S(1)}, u32[]{:S(2)}, u32[]{:S(2)}) collective-permute-start(bf16[2064,128]{1,0:T(8,128)(2,1)S(1)} %shard_map.28.own.d0), channel_id=1, source_target_pairs={{254,0},{3,1},{0,2},{5,3},{2,4},{7,5},{4,6},{9,7},{6,8},{11,9},{8,... | collective-permute-start | bytes 1585160 | tf_op jit(solution)/shard_map/ppermute | solution.py:207
  16.1 5.1 %collective-permute-done.p2 = bf16[2064,128]{1,0:T(8,128)(2,1)S(1)} collective-permute-done((bf16[2064,128]{1,0:T(8,128)(2,1)S(1)}, bf16[2064,128]{1,0:T(8,128)(2,1)S(1)}, u32[]{:S(2)}, u32[]{:S(2)}) %collective-permute-start) | collective-permute-done | bytes 528416 | tf_op jit(solution)/shard_map/ppermute | solution.py:207
  21.1 0.0 collective-permute-start.4
  21.1 5.8 %collective-permute-done.3.n2 = bf16[2064,128]{1,0:T(8,128)(2,1)S(1)} collective-permute-done((bf16[2064,128]{1,0:T(8,128)(2,1)S(1)}, bf16[2064,128]{1,0:T(8,128)(2,1)S(1)}, u32[]{:S(2)}, u32[]{:S(2)}) %collective-permute-start.3) | collective-permute-done | bytes 528416 | tf_op jit(solution)/shard_map/ppermute | solution.py:207
  26.9 7.3 %collective-permute-start.7 = (bf16[2064,128]{1,0:T(8,128)(2,1)S(1)}, bf16[2064,128]{1,0:T(8,128)(2,1)}, u32[]{:S(2)}, u32[]{:S(2)}) collective-permute-start(bf16[2064,128]{1,0:T(8,128)(2,1)S(1)} %collective-permute-done.3.n2), channel_id=1, source_target_pairs={{254,0},{3,1},{0,2},{5,3},{2,4},{7,5},{4,6},{9,7},{6,8},{11,9},{8,... | collective-permute-start | bytes 1585160 | tf_op jit(solution)/shard_map/ppermute | solution.py:207
  34.2 0.5 collective-permute-done.4.p4
  34.7 0.0 collective-permute-start.8
  34.7 19.7 %collective-permute-start.1 = (bf16[2064,128]{1,0:T(8,128)(2,1)S(1)}, bf16[2064,128]{1,0:T(8,128)(2,1)S(1)}, u32[]{:S(2)}, u32[]{:S(2)}) collective-permute-start(bf16[2064,128]{1,0:T(8,128)(2,1)S(1)} %collective-permute-done.p2), channel_id=1, source_target_pairs={{0,1},{1,0},{2,3},{3,2},{4,5},{5,4},{6,7},{7,6},{8,9},{9,8},{10,11... | collective-permute-start | bytes 1585160 | tf_op jit(solution)/shard_map/ppermute | solution.py:210
  54.5 0.0 collective-permute-start.6
  54.5 0.5 collective-permute-start.5
  55.0 0.0 collective-permute-done.7.n4
  55.0 0.0 collective-permute-start.10
  55.0 0.0 collective-permute-done.8.p6
  55.0 6.5 %collective-permute-start.9 = (bf16[2064,128]{1,0:T(8,128)(2,1)S(1)}, bf16[2064,128]{1,0:T(8,128)(2,1)}, u32[]{:S(2)}, u32[]{:S(2)}) collective-permute-start(bf16[2064,128]{1,0:T(8,128)(2,1)S(1)} %collective-permute-done.8.p6), channel_id=1, source_target_pairs={{0,1},{1,0},{2,3},{3,2},{4,5},{5,4},{6,7},{7,6},{8,9},{9,8},{10,11... | collective-permute-start | bytes 1585160 | tf_op jit(solution)/shard_map/ppermute | solution.py:210
  61.5 0.0 collective-permute-done.1.n1
  61.5 7.5 %collective-permute-start.11 = (bf16[2064,128]{1,0:T(8,128)(2,1)}, bf16[2064,128]{1,0:T(8,128)(2,1)}, u32[]{:S(2)}, u32[]{:S(2)}) collective-permute-start(bf16[2064,128]{1,0:T(8,128)(2,1)} %collective-permute-done.7.n4), channel_id=1, source_target_pairs={{254,0},{3,1},{0,2},{5,3},{2,4},{7,5},{4,6},{9,7},{6,8},{11,9},{8,... | collective-permute-start | bytes 1585160 | tf_op jit(solution)/shard_map/ppermute | solution.py:207
  69.1 1.6 %shard_map.29.left_ref = bf16[256,2304]{1,0:T(8,128)(2,1)S(1)} custom-call(s32[1]{0:T(128)} %bitcast.sign_ref, bf16[2064,128]{1,0:T(8,128)(2,1)S(1)} %shard_map.28.own.d0, bf16[2064,128]{1,0:T(8,128)(2,1)S(1)} %collective-permute-done.1.n1, bf16[2064,128]{1,0:T(8,128)(2,1)S(1)} %collective-permute-done.2.p1, ...), custom_call_target="tpu_custom_call" | custom-call | flops 838860800 | bytes 3821568 | tf_op jit(solution)/shard_map/pallas_call | solution.py:186
  70.7 0.0 collective-permute-done.6.p3
  70.7 0.0 collective-permute-done.5.n3
  70.7 6.0 %shard_map.30 = (bf16[256,3328]{1,0:T(8,128)(2,1)S(1)}, f32[256,3328]{1,0:T(8,128)S(1)}) custom-call(s32[1]{0:T(128)} %bitcast.sign_ref, bf16[256,2304]{1,0:T(8,128)(2,1)S(1)} %shard_map.29.left_ref, bf16[2064,128]{1,0:T(8,128)(2,1)S(1)} %shard_map.28.own.d0, bf16[2064,128]{1,0:T(8,128)(2,1)S(1)} %collective-permute-done.1.n1, ...), custom_call_target="tpu_custom_call" | custom-call | flops 3019898880 | bytes 13180928 | tf_op jit(solution)/shard_map/pallas_call | solution.py:186
  76.8 0.0 collective-permute-done.10.p5
  76.8 0.0 collective-permute-done.9.n5
  76.8 4.8 %shard_map.31 = (f32[256,4352]{1,0:T(8,128)}, bf16[256,256]{1,0:T(8,128)(2,1)S(1)}) custom-call(s32[1]{0:T(128)} %bitcast.sign_ref, bf16[256,3328]{1,0:T(8,128)(2,1)S(1)} %get-tuple-element.13.cube_ref, f32[256,3328]{1,0:T(8,128)S(1)} %get-tuple-element.14.sum_ref, bf16[2064,128]{1,0:T(8,128)(2,1)} %collective-permute-done.9.n5, ...), custom_call_target="tpu_custom_call" | custom-call | flops 503316480 | bytes 9449472 | tf_op jit(solution)/shard_map/pallas_call | solution.py:186
  81.6 0.0 collective-permute-done.11.refs_1_
  81.6 4.9 %shard_map.32 = f32[256,4352]{1,0:T(8,128)} custom-call(s32[1]{0:T(128)} %bitcast.sign_ref, bf16[256,256]{1,0:T(8,128)(2,1)S(1)} %get-tuple-element.15.refs_0_, bf16[2064,128]{1,0:T(8,128)(2,1)} %collective-permute-done.11.refs_1_, f32[256,4352]{1,0:T(8,128)} %get-tuple-element.16.refs_2_), custom_call_target="tpu_custom_call", output_to_operand_aliasing={{}: (3, {})} | custom-call | flops 167772160 | bytes 3149824 | tf_op jit(solution)/shard_map/pallas_call | solution.py:158
  (1 shorter events, 0.0 us)
Async XLA Ops:
  0.0 1.3 %copy-start = (s32[256,1280]{1,0:T(8,128)S(1)}, s32[256,1280]{1,0:T(8,128)}, u32[]{:S(2)}) copy-start(s32[256,1280]{1,0:T(8,128)} %adjacency_ref.1) | copy-start | bytes 3932164
  1.3 1.1 %copy-start.1 = (bf16[256,1280]{1,0:T(8,128)(2,1)S(1)}, bf16[256,1280]{1,0:T(8,128)(2,1)}, u32[]{:S(2)}) copy-start(bf16[256,1280]{1,0:T(8,128)(2,1)} %weight_ref.1) | copy-start | bytes 1966084
  2.7 4.9 %collective-permute-start.2 = (bf16[2064,128]{1,0:T(8,128)(2,1)S(1)}, bf16[2064,128]{1,0:T(8,128)(2,1)S(1)}, u32[]{:S(2)}, u32[]{:S(2)}) collective-permute-start(bf16[2064,128]{1,0:T(8,128)(2,1)S(1)} %shard_map.28.own.d0), channel_id=1, source_target_pairs={{0,1},{1,0},{2,3},{3,2},{4,5},{5,4},{6,7},{7,6},{8,9},{9,8},{10,11... | collective-permute-start | bytes 1585160 | tf_op jit(solution)/shard_map/ppermute | solution.py:210
  6.0 15.1 %collective-permute-start = (bf16[2064,128]{1,0:T(8,128)(2,1)S(1)}, bf16[2064,128]{1,0:T(8,128)(2,1)S(1)}, u32[]{:S(2)}, u32[]{:S(2)}) collective-permute-start(bf16[2064,128]{1,0:T(8,128)(2,1)S(1)} %shard_map.28.own.d0), channel_id=1, source_target_pairs={{2,0},{255,1},{4,2},{1,3},{6,4},{3,5},{8,6},{5,7},{10,8},{7,9},{12... | collective-permute-start | bytes 1585160 | tf_op jit(solution)/shard_map/ppermute | solution.py:207
  7.6 19.3 %collective-permute-start.3 = (bf16[2064,128]{1,0:T(8,128)(2,1)S(1)}, bf16[2064,128]{1,0:T(8,128)(2,1)S(1)}, u32[]{:S(2)}, u32[]{:S(2)}) collective-permute-start(bf16[2064,128]{1,0:T(8,128)(2,1)S(1)} %shard_map.28.own.d0), channel_id=1, source_target_pairs={{254,0},{3,1},{0,2},{5,3},{2,4},{7,5},{4,6},{9,7},{6,8},{11,9},{8,... | collective-permute-start | bytes 1585160 | tf_op jit(solution)/shard_map/ppermute | solution.py:207
  21.1 13.6 %collective-permute-start.4 = (bf16[2064,128]{1,0:T(8,128)(2,1)S(1)}, bf16[2064,128]{1,0:T(8,128)(2,1)}, u32[]{:S(2)}, u32[]{:S(2)}) collective-permute-start(bf16[2064,128]{1,0:T(8,128)(2,1)S(1)} %collective-permute-done.p2), channel_id=1, source_target_pairs={{2,0},{255,1},{4,2},{1,3},{6,4},{3,5},{8,6},{5,7},{10,8},{7,9},{12... | collective-permute-start | bytes 1585160 | tf_op jit(solution)/shard_map/ppermute | solution.py:207
  26.9 28.1 %collective-permute-start.7 = (bf16[2064,128]{1,0:T(8,128)(2,1)S(1)}, bf16[2064,128]{1,0:T(8,128)(2,1)}, u32[]{:S(2)}, u32[]{:S(2)}) collective-permute-start(bf16[2064,128]{1,0:T(8,128)(2,1)S(1)} %collective-permute-done.3.n2), channel_id=1, source_target_pairs={{254,0},{3,1},{0,2},{5,3},{2,4},{7,5},{4,6},{9,7},{6,8},{11,9},{8,... | collective-permute-start | bytes 1585160 | tf_op jit(solution)/shard_map/ppermute | solution.py:207
  34.7 20.3 %collective-permute-start.8 = (bf16[2064,128]{1,0:T(8,128)(2,1)}, bf16[2064,128]{1,0:T(8,128)(2,1)S(1)}, u32[]{:S(2)}, u32[]{:S(2)}) collective-permute-start(bf16[2064,128]{1,0:T(8,128)(2,1)} %collective-permute-done.4.p4), channel_id=1, source_target_pairs={{2,0},{255,1},{4,2},{1,3},{6,4},{3,5},{8,6},{5,7},{10,8},{7,9},{12... | collective-permute-start | bytes 1585160 | tf_op jit(solution)/shard_map/ppermute | solution.py:207
  34.7 26.8 %collective-permute-start.1 = (bf16[2064,128]{1,0:T(8,128)(2,1)S(1)}, bf16[2064,128]{1,0:T(8,128)(2,1)S(1)}, u32[]{:S(2)}, u32[]{:S(2)}) collective-permute-start(bf16[2064,128]{1,0:T(8,128)(2,1)S(1)} %collective-permute-done.p2), channel_id=1, source_target_pairs={{0,1},{1,0},{2,3},{3,2},{4,5},{5,4},{6,7},{7,6},{8,9},{9,8},{10,11... | collective-permute-start | bytes 1585160 | tf_op jit(solution)/shard_map/ppermute | solution.py:210
  54.5 16.2 %collective-permute-start.6 = (bf16[2064,128]{1,0:T(8,128)(2,1)S(1)}, bf16[2064,128]{1,0:T(8,128)(2,1)}, u32[]{:S(2)}, u32[]{:S(2)}) collective-permute-start(bf16[2064,128]{1,0:T(8,128)(2,1)S(1)} %collective-permute-done.3.n2), channel_id=1, source_target_pairs={{0,1},{1,0},{2,3},{3,2},{4,5},{5,4},{6,7},{7,6},{8,9},{9,8},{10,11... | collective-permute-start | bytes 1585160 | tf_op jit(solution)/shard_map/ppermute | solution.py:210
  54.5 16.3 %collective-permute-start.5 = (bf16[2064,128]{1,0:T(8,128)(2,1)}, bf16[2064,128]{1,0:T(8,128)(2,1)}, u32[]{:S(2)}, u32[]{:S(2)}) collective-permute-start(bf16[2064,128]{1,0:T(8,128)(2,1)} %collective-permute-done.4.p4), channel_id=1, source_target_pairs={{0,1},{1,0},{2,3},{3,2},{4,5},{5,4},{6,7},{7,6},{8,9},{9,8},{10,11... | collective-permute-start | bytes 1585160 | tf_op jit(solution)/shard_map/ppermute | solution.py:210
  55.0 21.8 %collective-permute-start.10 = (bf16[2064,128]{1,0:T(8,128)(2,1)}, bf16[2064,128]{1,0:T(8,128)(2,1)}, u32[]{:S(2)}, u32[]{:S(2)}) collective-permute-start(bf16[2064,128]{1,0:T(8,128)(2,1)} %collective-permute-done.7.n4), channel_id=1, source_target_pairs={{0,1},{1,0},{2,3},{3,2},{4,5},{5,4},{6,7},{7,6},{8,9},{9,8},{10,11... | collective-permute-start | bytes 1585160 | tf_op jit(solution)/shard_map/ppermute | solution.py:210
  55.0 21.8 %collective-permute-start.9 = (bf16[2064,128]{1,0:T(8,128)(2,1)S(1)}, bf16[2064,128]{1,0:T(8,128)(2,1)}, u32[]{:S(2)}, u32[]{:S(2)}) collective-permute-start(bf16[2064,128]{1,0:T(8,128)(2,1)S(1)} %collective-permute-done.8.p6), channel_id=1, source_target_pairs={{0,1},{1,0},{2,3},{3,2},{4,5},{5,4},{6,7},{7,6},{8,9},{9,8},{10,11... | collective-permute-start | bytes 1585160 | tf_op jit(solution)/shard_map/ppermute | solution.py:210
  61.5 20.1 %collective-permute-start.11 = (bf16[2064,128]{1,0:T(8,128)(2,1)}, bf16[2064,128]{1,0:T(8,128)(2,1)}, u32[]{:S(2)}, u32[]{:S(2)}) collective-permute-start(bf16[2064,128]{1,0:T(8,128)(2,1)} %collective-permute-done.7.n4), channel_id=1, source_target_pairs={{254,0},{3,1},{0,2},{5,3},{2,4},{7,5},{4,6},{9,7},{6,8},{11,9},{8,... | collective-permute-start | bytes 1585160 | tf_op jit(solution)/shard_map/ppermute | solution.py:207

commit v2 on v1

v2 whole, which is shorter than its diff:
```python
import functools
import math

import jax
import jax.numpy as jnp
from jax import lax
from jax.experimental import pallas as pl
from jax.experimental.pallas import tpu as pltpu
from jax.sharding import PartitionSpec as P

B = 512
R = 256
LANES = 128
TILES = 1024 // LANES
ROWS = TILES * R + 16
FIRST_SCALE = 1.0 / math.sqrt(B)
LAST_SCALE = 1.0 / (math.sqrt(B) * math.sqrt(2 * B))
MIB = 1 << 20
CHUNKS = 4


def pack_kernel(adjacency_hbm, weight_hbm, packed_ref, edges, weights, semaphores):
    count = R // CHUNKS
    copies = []
    for chunk in range(CHUNKS):
        rows = slice(chunk * count, (chunk + 1) * count)
        for index, (source, target) in enumerate(((adjacency_hbm, edges), (weight_hbm, weights))):
            copy = pltpu.make_async_copy(source.at[rows, :], target.at[rows, :], semaphores.at[index, chunk])
            copy.start()
            copies.append(copy)
    lane = lax.broadcasted_iota(jnp.int32, (count, LANES), 1)
    diagonals = [jnp.zeros((1, LANES), jnp.float32)] * 2
    for chunk in range(CHUNKS):
        copies[2 * chunk].wait()
        copies[2 * chunk + 1].wait()
        rows = slice(chunk * count, (chunk + 1) * count)
        row = lax.broadcasted_iota(jnp.int32, (count, LANES), 0) + chunk * count

        def tile(index):
            columns = slice(index * LANES, (index + 1) * LANES)
            return edges[rows, columns] == 1, weights[rows, columns].astype(jnp.float32)

        def store(index, value):
            begin = index * R + chunk * count
            packed_ref[begin : begin + count, :] = value.astype(jnp.bfloat16)

        for half in range(2):
            column = lane + half * LANES
            near_edge, near = tile(half)
            far_edge, far = tile(8 + half)
            near = jnp.where(near_edge, near, 0.0)
            far = jnp.where(far_edge, far, 0.0)
            store(half, jnp.where(column >= row, near, far))
            diagonal = jnp.where(column == row, far, 0.0)
            diagonals[half] = diagonals[half] + jnp.sum(diagonal, axis=0, keepdims=True)
        for index in range(2, 8):
            edge, value = tile(index)
            if index in (4, 5):
                edge = edge | (lane + (index - 4) * LANES == row)
            store(index, jnp.where(edge, value, 0.0))
    place = lax.broadcasted_iota(jnp.int32, (16, LANES), 0)
    tail = jnp.where(place == 0, diagonals[0], jnp.where(place == 1, diagonals[1], 0.0))
    packed_ref[TILES * R :, :] = tail.astype(jnp.bfloat16)


def pack(adjacency, weight):
    return pl.pallas_call(
        pack_kernel,
        in_specs=[pl.BlockSpec(memory_space=pltpu.HBM)] * 2,
        out_specs=pl.BlockSpec(memory_space=pltpu.VMEM),
        out_shape=jax.ShapeDtypeStruct((ROWS, LANES), jnp.bfloat16),
        scratch_shapes=[
            pltpu.VMEM((R, 5 * R), jnp.int32),
            pltpu.VMEM((R, 5 * R), jnp.bfloat16),
            pltpu.SemaphoreType.DMA((2, CHUNKS)),
        ],
        compiler_params=pltpu.CompilerParams(vmem_limit_bytes=56 * MIB),
        cost_estimate=pl.CostEstimate(flops=R * 5 * R * 4, bytes_accessed=R * 5 * R * 6 + ROWS * 256, transcendentals=0),
    )(adjacency, weight)


def slot(ref, index):
    begin = index * 2 * R
    return jnp.concatenate([ref[begin : begin + R, :], ref[begin + R : begin + 2 * R, :]], axis=1)


def unpacked(ref):
    row = lax.broadcasted_iota(jnp.int32, (R, R), 0)
    column = lax.broadcasted_iota(jnp.int32, (R, R), 1)
    merged = slot(ref, 0).astype(jnp.float32)
    tail = ref[TILES * R :, :].astype(jnp.float32)
    diagonal = jnp.concatenate([tail[0:1, :], tail[1:2, :]], axis=1)
    first = jnp.where(column >= row, merged, 0.0)
    last = jnp.where(column < row, merged, jnp.where(column == row, diagonal, 0.0))
    return [
        first.astype(jnp.bfloat16),
        slot(ref, 1),
        slot(ref, 2),
        slot(ref, 3),
        last.astype(jnp.bfloat16),
    ]


def block(index):
    return pl.ds(pl.multiple_of(index * R, R), R)


def accumulate(total_ref, left, ref, first_block):
    for offset, right in enumerate(unpacked(ref)):
        where = block(first_block + offset)
        total_ref[:, where] += jnp.dot(left, right, preferred_element_type=jnp.float32)


def near_kernel(sign_ref, own, p1, left_ref, total_ref):
    sign = sign_ref[0]
    for offset, part in enumerate(unpacked(own)):
        left_ref[:, offset * R : (offset + 1) * R] = part
    total_ref[...] = jnp.zeros_like(total_ref)
    for reach, ref in ((0, own), (1, p1)):
        at = reach * sign
        accumulate(total_ref, left_ref[:, block(at + 2)], ref, at + 2)


def add_kernel(reaches, span, sign_ref, left_ref, *refs):
    sign = sign_ref[0]
    before_ref, total_ref = refs[-2:]
    total_ref[...] = before_ref[...]
    for reach, ref in zip(reaches, refs[:-2], strict=True):
        at = reach * sign
        accumulate(total_ref, left_ref[:, block(at + span)], ref, at + span)


def square_kernel(sign_ref, left_ref, d0, n1, p1, n2, p2, before_ref, square_ref, total_ref, work_ref):
    sign = sign_ref[0]
    work_ref[...] = before_ref[...]
    for reach, ref in ((-1, n1), (-2, n2)):
        at = reach * sign
        accumulate(work_ref, left_ref[:, block(at + 2)], ref, at + 2)
    square_ref[...] = (work_ref[...] * FIRST_SCALE).astype(jnp.bfloat16)
    total_ref[...] = jnp.zeros_like(total_ref)
    for reach, ref in ((0, d0), (1, p1), (-1, n1), (2, p2), (-2, n2)):
        at = reach * sign
        accumulate(total_ref, square_ref[:, block(at + 4)], ref, at + 4)


def cube_kernel(sign_ref, left_ref, d0, n1, p1, n2, p2, n3, p3, n4, p4, before_ref, cube_ref, sum_ref, work_ref):
    sign = sign_ref[0]
    work_ref[...] = before_ref[...]
    for reach, ref in ((-3, n3), (-4, n4)):
        at = reach * sign
        accumulate(work_ref, left_ref[:, block(at + 4)], ref, at + 4)
    cube_ref[...] = work_ref[...].astype(jnp.bfloat16)
    sum_ref[...] = jnp.zeros_like(sum_ref)
    known = ((0, d0), (1, p1), (-1, n1), (2, p2), (-2, n2), (3, p3), (-3, n3), (4, p4), (-4, n4))
    for reach, ref in known:
        at = reach * sign
        accumulate(sum_ref, cube_ref[:, block(at + 6)], ref, at + 4)


def far_kernel(sign_ref, cube_ref, sum_ref, p5, p6, out_hbm, partial_ref, last_ref, total_ref, semaphores):
    sign = sign_ref[0]
    half = (1 - sign) // 2
    total_ref[:, : 2 * R] = jnp.zeros((R, 2 * R), jnp.float32)
    total_ref[:, 15 * R :] = jnp.zeros((R, 2 * R), jnp.float32)
    total_ref[:, 2 * R : 15 * R] = sum_ref[...]
    last_ref[:, :R] = cube_ref[:, block(6 - 5 * sign)]
    last_ref[:, R:] = cube_ref[:, block(6 - 6 * sign)]
    for reach, ref in ((5, p5), (6, p6)):
        at = reach * sign
        accumulate(total_ref, cube_ref[:, block(at + 6)], ref, at + 6)
    count = R // CHUNKS
    copies = []
    for chunk in range(CHUNKS):
        rows = slice(chunk * count, (chunk + 1) * count)
        total_ref[rows, :] = total_ref[rows, :] * LAST_SCALE
        columns = pl.ds(pl.multiple_of((1 - half) * 6 * R, R), 11 * R)
        place = (rows, columns)
        copy = pltpu.make_async_copy(total_ref.at[place], out_hbm.at[place], semaphores.at[chunk])
        copy.start()
        copies.append(copy)
    partial_ref[...] = total_ref[:, pl.ds(pl.multiple_of(half * 11 * R, R), 6 * R)]
    for copy in copies:
        copy.wait()


def far_call(sign, cube, total, p5, p6):
    return pl.pallas_call(
        far_kernel,
        in_specs=[pl.BlockSpec(memory_space=pltpu.SMEM)] + [pl.BlockSpec(memory_space=pltpu.VMEM)] * 4,
        out_specs=[pl.BlockSpec(memory_space=pltpu.HBM)] + [pl.BlockSpec(memory_space=pltpu.VMEM)] * 2,
        out_shape=[
            jax.ShapeDtypeStruct((R, 17 * R), jnp.float32),
            jax.ShapeDtypeStruct((R, 6 * R), jnp.float32),
            jax.ShapeDtypeStruct((R, 2 * R), jnp.bfloat16),
        ],
        scratch_shapes=[pltpu.VMEM((R, 17 * R), jnp.float32), pltpu.SemaphoreType.DMA((CHUNKS,))],
        compiler_params=pltpu.CompilerParams(vmem_limit_bytes=20 * MIB),
        cost_estimate=COST,
    )(sign, cube, total, p5, p6)


def edge_kernel(sign_ref, left_ref, n5, n6, partial_ref, before_hbm, out_hbm, result_ref, semaphores):
    del before_hbm
    half = (1 - sign_ref[0]) // 2
    result_ref[...] = partial_ref[...]
    for reach, ref in ((5, n5), (6, n6)):
        left = left_ref[:, (reach - 5) * R : (reach - 4) * R]
        begin = (6 - reach) * (1 - half) + (reach - 5) * half
        for offset, right in enumerate(unpacked(ref)):
            product = jnp.dot(left, right, preferred_element_type=jnp.float32)
            result_ref[:, block(begin + offset)] += product * LAST_SCALE
    copies = []
    for offset in range(3):
        columns = slice(offset * 2 * R, (offset + 1) * 2 * R)
        place = pl.ds(pl.multiple_of((half * 11 + 2 * offset) * R, R), 2 * R)
        copy = pltpu.make_async_copy(result_ref.at[:, columns], out_hbm.at[:, place], semaphores.at[offset])
        copy.start()
        copies.append(copy)
    for copy in copies:
        copy.wait()


def edge_call(sign, left, n5, n6, partial, before):
    vmem = pl.BlockSpec(memory_space=pltpu.VMEM)
    hbm = pl.BlockSpec(memory_space=pltpu.HBM)
    return pl.pallas_call(
        edge_kernel,
        in_specs=[pl.BlockSpec(memory_space=pltpu.SMEM), vmem, vmem, vmem, vmem, hbm],
        out_specs=hbm,
        out_shape=jax.ShapeDtypeStruct(before.shape, jnp.float32),
        scratch_shapes=[pltpu.VMEM((R, 6 * R), jnp.float32), pltpu.SemaphoreType.DMA((3,))],
        input_output_aliases={5: 0},
        compiler_params=pltpu.CompilerParams(vmem_limit_bytes=16 * MIB),
        cost_estimate=COST,
    )(sign, left, n5, n6, partial, before)


COST = pl.CostEstimate(flops=0, bytes_accessed=int(20 * MIB), transcendentals=0)


def call(kernel, arrays, shapes, scratch):
    specs = [pl.BlockSpec(memory_space=pltpu.SMEM)]
    specs += [pl.BlockSpec(memory_space=pltpu.VMEM)] * (len(arrays) - 1)
    return pl.pallas_call(
        kernel,
        in_specs=specs,
        out_specs=[pl.BlockSpec(memory_space=pltpu.VMEM)] * len(shapes),
        out_shape=shapes,
        scratch_shapes=scratch,
        compiler_params=pltpu.CompilerParams(vmem_limit_bytes=24 * MIB),
        cost_estimate=COST,
    )(*arrays)


def local(adjacency, weight):
    size = lax.axis_size("blk")
    parity = lax.rem(lax.axis_index("blk"), 2)
    sign = (1 - 2 * parity).astype(jnp.int32).reshape(1)

    def hop(value, steps):
        pairs = []
        for target in range(size):
            ahead = steps if target % 2 == 0 else -steps
            pairs.append(((target + ahead) % size, target))
        return lax.ppermute(value, "blk", pairs)

    def peer(value):
        return lax.ppermute(value, "blk", [(source, source ^ 1) for source in range(size)])

    tie = lax.optimization_barrier
    f32, bf16 = jnp.float32, jnp.bfloat16
    own = pack(adjacency, weight)
    p2 = hop(own, 2)
    p1 = peer(own)
    held, p1 = tie((own, p1))
    n2 = hop(held, -2)
    left, total = call(
        near_kernel,
        (sign, own, p1),
        [jax.ShapeDtypeStruct((R, 5 * R), bf16), jax.ShapeDtypeStruct((R, 9 * R), f32)],
        [],
    )
    p2, total = tie((p2, total))
    p4 = hop(p2, 2)
    n1 = peer(p2)
    (total,) = call(
        functools.partial(add_kernel, (2,), 2),
        (sign, left, p2, total),
        [jax.ShapeDtypeStruct((R, 9 * R), f32)],
        [],
    )
    n2, total = tie((n2, total))
    n4 = hop(n2, -2)
    p3 = peer(n2)
    square, total = call(
        square_kernel,
        (sign, left, own, n1, p1, n2, p2, total),
        [jax.ShapeDtypeStruct((R, 9 * R), bf16), jax.ShapeDtypeStruct((R, 13 * R), f32)],
        [pltpu.VMEM((R, 9 * R), f32)],
    )
    p4, total = tie((p4, total))
    p6 = hop(p4, 2)
    n3 = peer(p4)
    (total,) = call(
        functools.partial(add_kernel, (3, 4), 4),
        (sign, square, p3, p4, total),
        [jax.ShapeDtypeStruct((R, 13 * R), f32)],
        [],
    )
    n4, total = tie((n4, total))
    n6 = hop(n4, -2)
    p5 = peer(n4)
    cube, total = call(
        cube_kernel,
        (sign, square, own, n1, p1, n2, p2, n3, p3, n4, p4, total),
        [jax.ShapeDtypeStruct((R, 13 * R), bf16), jax.ShapeDtypeStruct((R, 13 * R), f32)],
        [pltpu.VMEM((R, 13 * R), f32)],
    )
    p6, cube = tie((p6, cube))
    n5 = peer(p6)
    before, partial, last = far_call(sign, cube, total, p5, p6)
    n6, last = tie((n6, last))
    return edge_call(sign, last, n5, n6, partial, before)


def solution(mesh):
    in_specs = (P("blk", None), P("blk", None))
    out_specs = P("blk", None)
    return jax.shard_map(local, mesh=mesh, in_specs=in_specs, out_specs=out_specs, check_vma=False)
```

time: 86.8 us -> 70.5 us (0.81)
  starting transfers between devices: 53.5 us -> 43.5 us
  Pallas kernels: 17.7 us -> 14.2 us
  waiting for transfers between devices: 12.9 us -> 11.2 us
  local copies, waits for them, and re-layouts: 2.4 us -> 1.08 us
    ppermute x6, starting transfers between devices: 23.4 us -> 8.5 us  [hop(): return lax.ppermute(value, 'blk', pairs)]
    pallas_call x3 -> x5, Pallas kernels: 12.5 us -> 7.32 us  [call(): pl.pallas_call(kernel, in_specs=specs, out_specs=[pl.BlockSpec(memory_spa...]
    ppermute x6, starting transfers between devices: 30.1 us -> 35 us  [peer(): lax.ppermute(value, 'blk', [(source, source ^ 1) for source in range(size)])]
    ppermute x6, waiting for transfers between devices: 11.3 us -> 9.46 us  [hop(): return lax.ppermute(value, 'blk', pairs)]
    pallas_call x2 -> x3, Pallas kernels: 5.15 us -> 6.84 us  [the longest x1 2.61 us: far_call(): pl.pallas_call(far_kernel, in_specs=[pl.BlockSpec(memory_space=pltpu.SMEM...]
    unnamed x4, local copies, waits for them, and re-layouts: 2.4 us -> 1.08 us
  transfers between devices with their start and end apart: 12 -> 12, of which waited for: 4 -> 5; matrix products, arithmetic and copies ran while one was open for 0% -> 0% of each run, Pallas kernels for 14% -> 14%
where the time goes in v2:
time: 70.5 us; the launch traced here: 70.3 us
  starting transfers between devices  43.5 us (62%)
  Pallas kernels  14.2 us (20%)
  waiting for transfers between devices  11.2 us (16%)
  local copies, waits for them, and re-layouts  1.08 us (2%)
    ppermute x6, starting transfers between devices, peer(): lax.ppermute(value, 'blk', [(source, source ^ 1) for source in range(size)])  35 us
    ppermute x6, waiting for transfers between devices, hop(): return lax.ppermute(value, 'blk', pairs)  9.46 us
    ppermute x6, starting transfers between devices, hop(): return lax.ppermute(value, 'blk', pairs)  8.5 us
    pallas_call x5, Pallas kernels, call(): pl.pallas_call(kernel, in_specs=specs, out_specs=[pl.BlockSpec(memory_spa...  7.32 us
    pallas_call x1, Pallas kernels, far_call(): pl.pallas_call(far_kernel, in_specs=[pl.BlockSpec(memory_space=pltpu.SMEM...  2.61 us
    pallas_call x1, Pallas kernels, pack(): pl.pallas_call(pack_kernel, in_specs=[pl.BlockSpec(memory_space=pltpu.HBM...  2.39 us
    pallas_call x1, Pallas kernels, edge_call(): pl.pallas_call(edge_kernel, in_specs=[pl.BlockSpec(memory_space=pltpu.SME...  1.84 us
    ppermute x6, waiting for transfers between devices, peer(): lax.ppermute(value, 'blk', [(source, source ^ 1) for source in range(size)])  1.76 us
  transfers between devices with their start and end apart: 12, of which 5 were waited for; matrix products, arithmetic and copies ran while one was open for 0% of the time, Pallas kernels for 14%

profile of v2, /device:TPU:1, one launch (start us, length us, event | category | flops | bytes accessed | tf_op | source)
XLA Modules:
  0.0 70.3 jit_solution(17727657604120166432)
XLA Ops:
  0.0 2.4 %shard_map.28.own.d0 = bf16[2064,128]{1,0:T(8,128)(2,1)} custom-call(s32[256,1280]{1,0:T(8,128)} %adjacency_hbm.1, bf16[256,1280]{1,0:T(8,128)(2,1)} %weight_hbm.1), custom_call_target="tpu_custom_call" | custom-call | flops 1310720 | bytes 2494464 | tf_op jit(solution)/shard_map/pallas_call | solution.py:67
  2.4 3.3 %collective-permute-start = (bf16[2064,128]{1,0:T(8,128)(2,1)}, bf16[2064,128]{1,0:T(8,128)(2,1)S(1)}, u32[]{:S(2)}, u32[]{:S(2)}) collective-permute-start(bf16[2064,128]{1,0:T(8,128)(2,1)} %shard_map.28.own.d0), channel_id=1, source_target_pairs={{0,1},{1,0},{2,3},{3,2},{4,5},{5,4},{6,7},{7,6},{8,9},{9,8},{10,11... | collective-permute-start | bytes 1585160 | tf_op jit(solution)/shard_map/ppermute | solution.py:268
  5.7 0.0 collective-permute-start.2
  5.7 1.8 %collective-permute-done.p1 = bf16[2064,128]{1,0:T(8,128)(2,1)S(1)} collective-permute-done((bf16[2064,128]{1,0:T(8,128)(2,1)}, bf16[2064,128]{1,0:T(8,128)(2,1)S(1)}, u32[]{:S(2)}, u32[]{:S(2)}) %collective-permute-start) | collective-permute-done | bytes 528416 | tf_op jit(solution)/shard_map/ppermute | solution.py:268
  7.5 8.5 %collective-permute-start.1 = (bf16[2064,128]{1,0:T(8,128)(2,1)}, bf16[2064,128]{1,0:T(8,128)(2,1)S(1)}, u32[]{:S(2)}, u32[]{:S(2)}) collective-permute-start(bf16[2064,128]{1,0:T(8,128)(2,1)} %shard_map.28.own.d0), channel_id=1, source_target_pairs={{254,0},{3,1},{0,2},{5,3},{2,4},{7,5},{4,6},{9,7},{6,8},{11,9},{8,... | collective-permute-start | bytes 1585160 | tf_op jit(solution)/shard_map/ppermute | solution.py:265
  16.0 1.1 %copy-done = bf16[2064,128]{1,0:T(8,128)(2,1)S(1)} copy-done((bf16[2064,128]{1,0:T(8,128)(2,1)S(1)}, bf16[2064,128]{1,0:T(8,128)(2,1)}, u32[]{:S(2)}) %copy-start) | copy-done | bytes 528408
  17.0 0.7 shard_map.29
  17.7 3.3 %collective-permute-done.2.refs_0_.p2 = bf16[2064,128]{1,0:T(8,128)(2,1)S(1)} collective-permute-done((bf16[2064,128]{1,0:T(8,128)(2,1)}, bf16[2064,128]{1,0:T(8,128)(2,1)S(1)}, u32[]{:S(2)}, u32[]{:S(2)}) %collective-permute-start.2) | collective-permute-done | bytes 528416 | tf_op jit(solution)/shard_map/ppermute | solution.py:265
  21.0 5.0 %collective-permute-start.4 = (bf16[2064,128]{1,0:T(8,128)(2,1)S(1)}, bf16[2064,128]{1,0:T(8,128)(2,1)S(1)}, u32[]{:S(2)}, u32[]{:S(2)}) collective-permute-start(bf16[2064,128]{1,0:T(8,128)(2,1)S(1)} %collective-permute-done.2.refs_0_.p2), channel_id=1, source_target_pairs={{0,1},{1,0},{2,3},{3,2},{4,5},{5,4},{6,7},{7,6},{8,9},{9,8},{10,11... | collective-permute-start | bytes 1585160 | tf_op jit(solution)/shard_map/ppermute | solution.py:268
  26.1 0.0 collective-permute-start.6
  26.1 0.4 shard_map.30.before_ref
  26.5 0.4 collective-permute-done.1.n2
  26.9 7.5 %collective-permute-start.5 = (bf16[2064,128]{1,0:T(8,128)(2,1)S(1)}, bf16[2064,128]{1,0:T(8,128)(2,1)S(1)}, u32[]{:S(2)}, u32[]{:S(2)}) collective-permute-start(bf16[2064,128]{1,0:T(8,128)(2,1)S(1)} %collective-permute-done.1.n2), channel_id=1, source_target_pairs={{0,1},{1,0},{2,3},{3,2},{4,5},{5,4},{6,7},{7,6},{8,9},{9,8},{10,11... | collective-permute-start | bytes 1585160 | tf_op jit(solution)/shard_map/ppermute | solution.py:268
  34.4 0.0 collective-permute-start.3
  34.4 0.0 collective-permute-done.4.n1
  34.4 2.3 %shard_map.31 = (bf16[256,2304]{1,0:T(8,128)(2,1)S(1)}, f32[256,3328]{1,0:T(8,128)S(1)}) custom-call(s32[1]{0:T(128)} %bitcast.sign_ref, bf16[256,1280]{1,0:T(8,128)(2,1)S(1)} %get-tuple-element.30.left_ref, bf16[2064,128]{1,0:T(8,128)(2,1)S(1)} %copy-done.1, bf16[2064,128]{1,0:T(8,128)(2,1)S(1)} %collective-permute-done.4.n1, ...), custom_call_target="tpu_custom_call" | custom-call | bytes 20971520 | tf_op jit(solution)/shard_map/pallas_call | solution.py:244
  36.7 3.5 %collective-permute-done.6.refs_1_.p4 = bf16[2064,128]{1,0:T(8,128)(2,1)S(1)} collective-permute-done((bf16[2064,128]{1,0:T(8,128)(2,1)S(1)}, bf16[2064,128]{1,0:T(8,128)(2,1)S(1)}, u32[]{:S(2)}, u32[]{:S(2)}) %collective-permute-start.6) | collective-permute-done | bytes 528416 | tf_op jit(solution)/shard_map/ppermute | solution.py:265
  40.2 5.8 %collective-permute-start.9 = (bf16[2064,128]{1,0:T(8,128)(2,1)S(1)}, bf16[2064,128]{1,0:T(8,128)(2,1)S(1)}, u32[]{:S(2)}, u32[]{:S(2)}) collective-permute-start(bf16[2064,128]{1,0:T(8,128)(2,1)S(1)} %collective-permute-done.6.refs_1_.p4), channel_id=1, source_target_pairs={{0,1},{1,0},{2,3},{3,2},{4,5},{5,4},{6,7},{7,6},{8,9},{9,8},{10,11... | collective-permute-start | bytes 1585160 | tf_op jit(solution)/shard_map/ppermute | solution.py:268
  46.0 0.0 collective-permute-start.8
  46.0 0.0 collective-permute-done.5.refs_0_.p3
  46.0 0.8 %shard_map.32.before_ref = f32[256,3328]{1,0:T(8,128)S(1)} custom-call(s32[1]{0:T(128)} %bitcast.sign_ref, bf16[256,2304]{1,0:T(8,128)(2,1)S(1)} %get-tuple-element.36.left_ref, bf16[2064,128]{1,0:T(8,128)(2,1)S(1)} %collective-permute-done.5.refs_0_.p3, bf16[2064,128]{1,0:T(8,128)(2,1)S(1)} %collective-permute-done.6.refs_1_.p4, ...), custom_call_target="tpu_custom_call" | custom-call | bytes 20971520 | tf_op jit(solution)/shard_map/pallas_call | solution.py:244
  46.8 0.0 collective-permute-done.3.n4
  46.8 8.0 %collective-permute-start.10 = (bf16[2064,128]{1,0:T(8,128)(2,1)S(1)}, bf16[2064,128]{1,0:T(8,128)(2,1)S(1)}, u32[]{:S(2)}, u32[]{:S(2)}) collective-permute-start(bf16[2064,128]{1,0:T(8,128)(2,1)S(1)} %collective-permute-done.3.n4), channel_id=1, source_target_pairs={{0,1},{1,0},{2,3},{3,2},{4,5},{5,4},{6,7},{7,6},{8,9},{9,8},{10,11... | collective-permute-start | bytes 1585160 | tf_op jit(solution)/shard_map/ppermute | solution.py:268
  54.9 0.0 collective-permute-start.7
  54.9 0.0 collective-permute-done.9.n3
  54.9 3.2 %shard_map.33 = (bf16[256,3328]{1,0:T(8,128)(2,1)S(1)}, f32[256,3328]{1,0:T(8,128)S(1)}) custom-call(s32[1]{0:T(128)} %bitcast.sign_ref, bf16[256,2304]{1,0:T(8,128)(2,1)S(1)} %get-tuple-element.36.left_ref, bf16[2064,128]{1,0:T(8,128)(2,1)S(1)} %copy-done.1, bf16[2064,128]{1,0:T(8,128)(2,1)S(1)} %collective-permute-done.4.n1, ...), custom_call_target="tpu_custom_call" | custom-call | bytes 20971520 | tf_op jit(solution)/shard_map/pallas_call | solution.py:244
  58.0 2.2 %collective-permute-done.8.p6 = bf16[2064,128]{1,0:T(8,128)(2,1)S(1)} collective-permute-done((bf16[2064,128]{1,0:T(8,128)(2,1)S(1)}, bf16[2064,128]{1,0:T(8,128)(2,1)S(1)}, u32[]{:S(2)}, u32[]{:S(2)}) %collective-permute-start.8) | collective-permute-done | bytes 528416 | tf_op jit(solution)/shard_map/ppermute | solution.py:265
  60.3 5.4 %collective-permute-start.11 = (bf16[2064,128]{1,0:T(8,128)(2,1)S(1)}, bf16[2064,128]{1,0:T(8,128)(2,1)S(1)}, u32[]{:S(2)}, u32[]{:S(2)}) collective-permute-start(bf16[2064,128]{1,0:T(8,128)(2,1)S(1)} %collective-permute-done.8.p6), channel_id=1, source_target_pairs={{0,1},{1,0},{2,3},{3,2},{4,5},{5,4},{6,7},{7,6},{8,9},{9,8},{10,11... | collective-permute-start | bytes 1585160 | tf_op jit(solution)/shard_map/ppermute | solution.py:268
  65.6 0.0 collective-permute-done.10.p5
  65.6 2.6 %shard_map.34 = (f32[256,4352]{1,0:T(8,128)}, f32[256,1536]{1,0:T(8,128)S(1)}, bf16[256,512]{1,0:T(8,128)(2,1)S(1)}) custom-call(s32[1]{0:T(128)} %bitcast.sign_ref, bf16[256,3328]{1,0:T(8,128)(2,1)S(1)} %get-tuple-element.43.cube_ref, f32[256,3328]{1,0:T(8,128)S(1)} %get-tuple-element.44.sum_ref, bf16[2064,128]{1,0:T(8,128)(2,1)S(1)} %collective-permute-done.10.p5, ...), custom_call_target="tpu_custom_call" | custom-call | bytes 20971520 | tf_op jit(solution)/shard_map/pallas_call | solution.py:187
  68.3 0.0 collective-permute-done.7.n6
  68.3 1.8 %shard_map.35 = f32[256,4352]{1,0:T(8,128)} custom-call(s32[1]{0:T(128)} %bitcast.sign_ref, bf16[256,512]{1,0:T(8,128)(2,1)S(1)} %get-tuple-element.47.left_ref, bf16[2064,128]{1,0:T(8,128)(2,1)S(1)} %collective-permute-done.11.n5, bf16[2064,128]{1,0:T(8,128)(2,1)S(1)} %collective-permute-done.7.n6, ...), custom_call_target="tpu_custom_call", output_to_operand_aliasing={{}: (5, {})} | custom-call | bytes 20971520 | tf_op jit(solution)/shard_map/pallas_call | solution.py:226
  (4 shorter events, 0.0 us)
Async XLA Ops:
  2.4 5.1 %collective-permute-start = (bf16[2064,128]{1,0:T(8,128)(2,1)}, bf16[2064,128]{1,0:T(8,128)(2,1)S(1)}, u32[]{:S(2)}, u32[]{:S(2)}) collective-permute-start(bf16[2064,128]{1,0:T(8,128)(2,1)} %shard_map.28.own.d0), channel_id=1, source_target_pairs={{0,1},{1,0},{2,3},{3,2},{4,5},{5,4},{6,7},{7,6},{8,9},{9,8},{10,11... | collective-permute-start | bytes 1585160 | tf_op jit(solution)/shard_map/ppermute | solution.py:268
  5.7 15.3 %collective-permute-start.2 = (bf16[2064,128]{1,0:T(8,128)(2,1)}, bf16[2064,128]{1,0:T(8,128)(2,1)S(1)}, u32[]{:S(2)}, u32[]{:S(2)}) collective-permute-start(bf16[2064,128]{1,0:T(8,128)(2,1)} %shard_map.28.own.d0), channel_id=1, source_target_pairs={{2,0},{255,1},{4,2},{1,3},{6,4},{3,5},{8,6},{5,7},{10,8},{7,9},{12... | collective-permute-start | bytes 1585160 | tf_op jit(solution)/shard_map/ppermute | solution.py:265
  7.5 19.4 %collective-permute-start.1 = (bf16[2064,128]{1,0:T(8,128)(2,1)}, bf16[2064,128]{1,0:T(8,128)(2,1)S(1)}, u32[]{:S(2)}, u32[]{:S(2)}) collective-permute-start(bf16[2064,128]{1,0:T(8,128)(2,1)} %shard_map.28.own.d0), channel_id=1, source_target_pairs={{254,0},{3,1},{0,2},{5,3},{2,4},{7,5},{4,6},{9,7},{6,8},{11,9},{8,... | collective-permute-start | bytes 1585160 | tf_op jit(solution)/shard_map/ppermute | solution.py:265
  16.0 1.1 %copy-start = (bf16[2064,128]{1,0:T(8,128)(2,1)S(1)}, bf16[2064,128]{1,0:T(8,128)(2,1)}, u32[]{:S(2)}) copy-start(bf16[2064,128]{1,0:T(8,128)(2,1)} %shard_map.28.own.d0) | copy-start | bytes 1585156
  21.0 13.4 %collective-permute-start.4 = (bf16[2064,128]{1,0:T(8,128)(2,1)S(1)}, bf16[2064,128]{1,0:T(8,128)(2,1)S(1)}, u32[]{:S(2)}, u32[]{:S(2)}) collective-permute-start(bf16[2064,128]{1,0:T(8,128)(2,1)S(1)} %collective-permute-done.2.refs_0_.p2), channel_id=1, source_target_pairs={{0,1},{1,0},{2,3},{3,2},{4,5},{5,4},{6,7},{7,6},{8,9},{9,8},{10,11... | collective-permute-start | bytes 1585160 | tf_op jit(solution)/shard_map/ppermute | solution.py:268
  26.1 14.1 %collective-permute-start.6 = (bf16[2064,128]{1,0:T(8,128)(2,1)S(1)}, bf16[2064,128]{1,0:T(8,128)(2,1)S(1)}, u32[]{:S(2)}, u32[]{:S(2)}) collective-permute-start(bf16[2064,128]{1,0:T(8,128)(2,1)S(1)} %collective-permute-done.2.refs_0_.p2), channel_id=1, source_target_pairs={{2,0},{255,1},{4,2},{1,3},{6,4},{3,5},{8,6},{5,7},{10,8},{7,9},{12... | collective-permute-start | bytes 1585160 | tf_op jit(solution)/shard_map/ppermute | solution.py:265
  26.1 8.3 %copy-start.1 = (bf16[2064,128]{1,0:T(8,128)(2,1)S(1)}, bf16[2064,128]{1,0:T(8,128)(2,1)}, u32[]{:S(2)}) copy-start(bf16[2064,128]{1,0:T(8,128)(2,1)} %shard_map.28.own.d0) | copy-start | bytes 1585156
  26.9 19.1 %collective-permute-start.5 = (bf16[2064,128]{1,0:T(8,128)(2,1)S(1)}, bf16[2064,128]{1,0:T(8,128)(2,1)S(1)}, u32[]{:S(2)}, u32[]{:S(2)}) collective-permute-start(bf16[2064,128]{1,0:T(8,128)(2,1)S(1)} %collective-permute-done.1.n2), channel_id=1, source_target_pairs={{0,1},{1,0},{2,3},{3,2},{4,5},{5,4},{6,7},{7,6},{8,9},{9,8},{10,11... | collective-permute-start | bytes 1585160 | tf_op jit(solution)/shard_map/ppermute | solution.py:268
  34.4 12.4 %collective-permute-start.3 = (bf16[2064,128]{1,0:T(8,128)(2,1)S(1)}, bf16[2064,128]{1,0:T(8,128)(2,1)S(1)}, u32[]{:S(2)}, u32[]{:S(2)}) collective-permute-start(bf16[2064,128]{1,0:T(8,128)(2,1)S(1)} %collective-permute-done.1.n2), channel_id=1, source_target_pairs={{254,0},{3,1},{0,2},{5,3},{2,4},{7,5},{4,6},{9,7},{6,8},{11,9},{8,... | collective-permute-start | bytes 1585160 | tf_op jit(solution)/shard_map/ppermute | solution.py:265
  40.2 14.7 %collective-permute-start.9 = (bf16[2064,128]{1,0:T(8,128)(2,1)S(1)}, bf16[2064,128]{1,0:T(8,128)(2,1)S(1)}, u32[]{:S(2)}, u32[]{:S(2)}) collective-permute-start(bf16[2064,128]{1,0:T(8,128)(2,1)S(1)} %collective-permute-done.6.refs_1_.p4), channel_id=1, source_target_pairs={{0,1},{1,0},{2,3},{3,2},{4,5},{5,4},{6,7},{7,6},{8,9},{9,8},{10,11... | collective-permute-start | bytes 1585160 | tf_op jit(solution)/shard_map/ppermute | solution.py:268
  46.0 14.2 %collective-permute-start.8 = (bf16[2064,128]{1,0:T(8,128)(2,1)S(1)}, bf16[2064,128]{1,0:T(8,128)(2,1)S(1)}, u32[]{:S(2)}, u32[]{:S(2)}) collective-permute-start(bf16[2064,128]{1,0:T(8,128)(2,1)S(1)} %collective-permute-done.6.refs_1_.p4), channel_id=1, source_target_pairs={{2,0},{255,1},{4,2},{1,3},{6,4},{3,5},{8,6},{5,7},{10,8},{7,9},{12... | collective-permute-start | bytes 1585160 | tf_op jit(solution)/shard_map/ppermute | solution.py:265
  46.8 18.8 %collective-permute-start.10 = (bf16[2064,128]{1,0:T(8,128)(2,1)S(1)}, bf16[2064,128]{1,0:T(8,128)(2,1)S(1)}, u32[]{:S(2)}, u32[]{:S(2)}) collective-permute-start(bf16[2064,128]{1,0:T(8,128)(2,1)S(1)} %collective-permute-done.3.n4), channel_id=1, source_target_pairs={{0,1},{1,0},{2,3},{3,2},{4,5},{5,4},{6,7},{7,6},{8,9},{9,8},{10,11... | collective-permute-start | bytes 1585160 | tf_op jit(solution)/shard_map/ppermute | solution.py:268
  54.9 13.4 %collective-permute-start.7 = (bf16[2064,128]{1,0:T(8,128)(2,1)S(1)}, bf16[2064,128]{1,0:T(8,128)(2,1)S(1)}, u32[]{:S(2)}, u32[]{:S(2)}) collective-permute-start(bf16[2064,128]{1,0:T(8,128)(2,1)S(1)} %collective-permute-done.3.n4), channel_id=1, source_target_pairs={{254,0},{3,1},{0,2},{5,3},{2,4},{7,5},{4,6},{9,7},{6,8},{11,9},{8,... | collective-permute-start | bytes 1585160 | tf_op jit(solution)/shard_map/ppermute | solution.py:265
  60.3 8.0 %collective-permute-start.11 = (bf16[2064,128]{1,0:T(8,128)(2,1)S(1)}, bf16[2064,128]{1,0:T(8,128)(2,1)S(1)}, u32[]{:S(2)}, u32[]{:S(2)}) collective-permute-start(bf16[2064,128]{1,0:T(8,128)(2,1)S(1)} %collective-permute-done.8.p6), channel_id=1, source_target_pairs={{0,1},{1,0},{2,3},{3,2},{4,5},{5,4},{6,7},{7,6},{8,9},{9,8},{10,11... | collective-permute-start | bytes 1585160 | tf_op jit(solution)/shard_map/ppermute | solution.py:268

commit v3 on v2

v3 whole, which is shorter than its diff:
```python
import math

import jax
import jax.numpy as jnp
from jax import lax
from jax.experimental import pallas as pl
from jax.experimental.pallas import tpu as pltpu
from jax.sharding import PartitionSpec as P

B = 512
R = 256
LANES = 128
TILES = 1024 // LANES
ROWS = TILES * R + 16
FIRST_SCALE = 1.0 / math.sqrt(B)
LAST_SCALE = 1.0 / (math.sqrt(B) * math.sqrt(2 * B))
MIB = 1 << 20
CHUNKS = 4


def pack_kernel(adjacency_hbm, weight_hbm, packed_ref, edges, weights, semaphores):
    count = R // CHUNKS
    copies = []
    for chunk in range(CHUNKS):
        rows = slice(chunk * count, (chunk + 1) * count)
        for index, (source, target) in enumerate(((adjacency_hbm, edges), (weight_hbm, weights))):
            copy = pltpu.make_async_copy(source.at[rows, :], target.at[rows, :], semaphores.at[index, chunk])
            copy.start()
            copies.append(copy)
    lane = lax.broadcasted_iota(jnp.int32, (count, LANES), 1)
    diagonals = [jnp.zeros((1, LANES), jnp.float32)] * 2
    for chunk in range(CHUNKS):
        copies[2 * chunk].wait()
        copies[2 * chunk + 1].wait()
        rows = slice(chunk * count, (chunk + 1) * count)
        row = lax.broadcasted_iota(jnp.int32, (count, LANES), 0) + chunk * count

        def tile(index):
            columns = slice(index * LANES, (index + 1) * LANES)
            return edges[rows, columns] == 1, weights[rows, columns].astype(jnp.float32)

        def store(index, value):
            begin = index * R + chunk * count
            packed_ref[begin : begin + count, :] = value.astype(jnp.bfloat16)

        for half in range(2):
            column = lane + half * LANES
            near_edge, near = tile(half)
            far_edge, far = tile(8 + half)
            near = jnp.where(near_edge, near, 0.0)
            far = jnp.where(far_edge, far, 0.0)
            store(half, jnp.where(column >= row, near, far))
            diagonal = jnp.where(column == row, far, 0.0)
            diagonals[half] = diagonals[half] + jnp.sum(diagonal, axis=0, keepdims=True)
        for index in range(2, 8):
            edge, value = tile(index)
            if index in (4, 5):
                edge = edge | (lane + (index - 4) * LANES == row)
            store(index, jnp.where(edge, value, 0.0))
    place = lax.broadcasted_iota(jnp.int32, (16, LANES), 0)
    tail = jnp.where(place == 0, diagonals[0], jnp.where(place == 1, diagonals[1], 0.0))
    packed_ref[TILES * R :, :] = tail.astype(jnp.bfloat16)


def pack(adjacency, weight):
    return pl.pallas_call(
        pack_kernel,
        in_specs=[pl.BlockSpec(memory_space=pltpu.HBM)] * 2,
        out_specs=pl.BlockSpec(memory_space=pltpu.VMEM),
        out_shape=jax.ShapeDtypeStruct((ROWS, LANES), jnp.bfloat16),
        scratch_shapes=[
            pltpu.VMEM((R, 5 * R), jnp.int32),
            pltpu.VMEM((R, 5 * R), jnp.bfloat16),
            pltpu.SemaphoreType.DMA((2, CHUNKS)),
        ],
        compiler_params=pltpu.CompilerParams(vmem_limit_bytes=56 * MIB),
        cost_estimate=pl.CostEstimate(flops=R * 5 * R * 4, bytes_accessed=R * 5 * R * 6 + ROWS * 256, transcendentals=0),
    )(adjacency, weight)


def slot(ref, index):
    begin = index * 2 * R
    return jnp.concatenate([ref[begin : begin + R, :], ref[begin + R : begin + 2 * R, :]], axis=1)


def unpacked(ref):
    row = lax.broadcasted_iota(jnp.int32, (R, R), 0)
    column = lax.broadcasted_iota(jnp.int32, (R, R), 1)
    merged = slot(ref, 0).astype(jnp.float32)
    tail = ref[TILES * R :, :].astype(jnp.float32)
    diagonal = jnp.concatenate([tail[0:1, :], tail[1:2, :]], axis=1)
    first = jnp.where(column >= row, merged, 0.0)
    last = jnp.where(column < row, merged, jnp.where(column == row, diagonal, 0.0))
    return [
        first.astype(jnp.bfloat16),
        slot(ref, 1),
        slot(ref, 2),
        slot(ref, 3),
        last.astype(jnp.bfloat16),
    ]


def block(index):
    return pl.ds(pl.multiple_of(index * R, R), R)


def accumulate(total_ref, left, ref, first_block):
    for offset, right in enumerate(unpacked(ref)):
        where = block(first_block + offset)
        total_ref[:, where] += jnp.dot(left, right, preferred_element_type=jnp.float32)


def near_kernel(sign_ref, own, p0, left_ref, total_ref):
    sign = sign_ref[0]
    for offset, part in enumerate(unpacked(own)):
        left_ref[:, offset * R : (offset + 1) * R] = part
    total_ref[...] = jnp.zeros_like(total_ref)
    for at, ref in ((0, own), (sign, p0)):
        accumulate(total_ref, left_ref[:, block(at + 2)], ref, at + 2)


def square_kernel(sign_ref, left_ref, own, p0, u1, v1, xu1, xv1, before_ref, square_ref, total_ref, work_ref):
    sign = sign_ref[0]
    work_ref[...] = before_ref[...]
    for at, ref in ((-2, u1), (2, v1)):
        accumulate(work_ref, left_ref[:, block(at + 2)], ref, at + 2)

    @pl.when(sign > 0)
    def _():
        accumulate(work_ref, left_ref[:, block(1)], xu1, 1)

    @pl.when(sign < 0)
    def _():
        accumulate(work_ref, left_ref[:, block(3)], xv1, 3)

    square_ref[...] = (work_ref[...] * FIRST_SCALE).astype(jnp.bfloat16)
    total_ref[...] = jnp.zeros_like(total_ref)
    for at, ref in ((0, own), (sign, p0), (-2, u1), (2, v1), (sign - 2, xu1), (sign + 2, xv1)):
        accumulate(total_ref, square_ref[:, block(at + 4)], ref, at + 4)


def cube_kernel(
    sign_ref, left_ref, own, p0, u1, v1, xu1, xv1, u2, v2, xu2, xv2, f3, xf3, before_ref,
    out_hbm, partial_ref, last_ref, work_ref, cube_ref, sum_ref, semaphores,
):
    sign = sign_ref[0]
    half = (1 - sign) // 2
    work_ref[...] = before_ref[...]
    for at, ref in ((-4, u2), (4, v2)):
        accumulate(work_ref, left_ref[:, block(at + 4)], ref, at + 4)

    @pl.when(sign > 0)
    def _():
        accumulate(work_ref, left_ref[:, block(1)], xu2, 1)

    @pl.when(sign < 0)
    def _():
        accumulate(work_ref, left_ref[:, block(7)], xv2, 7)

    cube_ref[...] = (work_ref[...] * LAST_SCALE).astype(jnp.bfloat16)
    last_ref[...] = cube_ref[:, block(6 - 6 * sign)]
    sum_ref[...] = jnp.zeros_like(sum_ref)
    known = ((0, own), (sign, p0), (-2, u1), (2, v1), (sign - 2, xu1), (sign + 2, xv1))
    known += ((-4, u2), (4, v2), (sign - 4, xu2), (sign + 4, xv2), (6 * sign, f3), (-5 * sign, xf3))
    for at, ref in known:
        accumulate(sum_ref, cube_ref[:, block(at + 6)], ref, at + 6)
    count = R // CHUNKS
    copies = []
    for chunk in range(CHUNKS):
        rows = slice(chunk * count, (chunk + 1) * count)
        place = (rows, pl.ds(pl.multiple_of((1 - half) * 5 * R, R), 12 * R))
        copy = pltpu.make_async_copy(sum_ref.at[place], out_hbm.at[place], semaphores.at[chunk])
        copy.start()
        copies.append(copy)
    partial_ref[...] = sum_ref[:, pl.ds(pl.multiple_of(half * 12 * R, R), 5 * R)]
    for copy in copies:
        copy.wait()


def cube_call(*arrays):
    return pl.pallas_call(
        cube_kernel,
        in_specs=[pl.BlockSpec(memory_space=pltpu.SMEM)] + [pl.BlockSpec(memory_space=pltpu.VMEM)] * (len(arrays) - 1),
        out_specs=[pl.BlockSpec(memory_space=pltpu.HBM)] + [pl.BlockSpec(memory_space=pltpu.VMEM)] * 2,
        out_shape=[
            jax.ShapeDtypeStruct((R, 17 * R), jnp.float32),
            jax.ShapeDtypeStruct((R, 5 * R), jnp.float32),
            jax.ShapeDtypeStruct((R, R), jnp.bfloat16),
        ],
        scratch_shapes=[
            pltpu.VMEM((R, 13 * R), jnp.float32),
            pltpu.VMEM((R, 13 * R), jnp.bfloat16),
            pltpu.VMEM((R, 17 * R), jnp.float32),
            pltpu.SemaphoreType.DMA((CHUNKS,)),
        ],
        compiler_params=pltpu.CompilerParams(vmem_limit_bytes=30 * MIB),
        cost_estimate=COST,
    )(*arrays)


def edge_kernel(sign_ref, left_ref, b3, partial_ref, before_hbm, out_hbm, result_ref, semaphores):
    del before_hbm
    half = (1 - sign_ref[0]) // 2
    copies = []
    for offset, right in enumerate(unpacked(b3)):
        columns = slice(offset * R, (offset + 1) * R)
        product = jnp.dot(left_ref[...], right, preferred_element_type=jnp.float32)
        result_ref[:, columns] = partial_ref[:, columns] + product
        copy = pltpu.make_async_copy(
            result_ref.at[:, columns], out_hbm.at[:, block(half * 12 + offset)], semaphores.at[offset]
        )
        copy.start()
        copies.append(copy)
    for copy in copies:
        copy.wait()


def edge_call(sign, left, b3, partial, before):
    vmem = pl.BlockSpec(memory_space=pltpu.VMEM)
    hbm = pl.BlockSpec(memory_space=pltpu.HBM)
    return pl.pallas_call(
        edge_kernel,
        in_specs=[pl.BlockSpec(memory_space=pltpu.SMEM), vmem, vmem, vmem, hbm],
        out_specs=hbm,
        out_shape=jax.ShapeDtypeStruct(before.shape, jnp.float32),
        scratch_shapes=[pltpu.VMEM((R, 5 * R), jnp.float32), pltpu.SemaphoreType.DMA((5,))],
        input_output_aliases={4: 0},
        compiler_params=pltpu.CompilerParams(vmem_limit_bytes=16 * MIB),
        cost_estimate=COST,
    )(sign, left, b3, partial, before)


COST = pl.CostEstimate(flops=0, bytes_accessed=int(0.1 * MIB), transcendentals=0)


def call(kernel, arrays, shapes, scratch):
    specs = [pl.BlockSpec(memory_space=pltpu.SMEM)]
    specs += [pl.BlockSpec(memory_space=pltpu.VMEM)] * (len(arrays) - 1)
    return pl.pallas_call(
        kernel,
        in_specs=specs,
        out_specs=[pl.BlockSpec(memory_space=pltpu.VMEM)] * len(shapes),
        out_shape=shapes,
        scratch_shapes=scratch,
        compiler_params=pltpu.CompilerParams(vmem_limit_bytes=24 * MIB),
        cost_estimate=COST,
    )(*arrays)


def local(adjacency, weight):
    size = lax.axis_size("blk")
    parity = lax.rem(lax.axis_index("blk"), 2)
    sign = (1 - 2 * parity).astype(jnp.int32).reshape(1)

    def hop(value, steps):
        pairs = []
        for target in range(size):
            ahead = steps if target % 2 == 0 else -steps
            pairs.append(((target + ahead) % size, target))
        return lax.ppermute(value, "blk", pairs)

    def shifted(value, steps):
        return lax.ppermute(value, "blk", [((target + steps) % size, target) for target in range(size)])

    def peer(value):
        return lax.ppermute(value, "blk", [(source, source ^ 1) for source in range(size)])

    tie = lax.optimization_barrier
    f32, bf16 = jnp.float32, jnp.bfloat16
    own = pack(adjacency, weight)
    u1 = shifted(own, -2)
    v1 = shifted(own, 2)
    p0 = peer(own)
    left, total = call(
        near_kernel,
        (sign, own, p0),
        [jax.ShapeDtypeStruct((R, 5 * R), bf16), jax.ShapeDtypeStruct((R, 9 * R), f32)],
        [],
    )
    held, total = tie((own, total))
    f3 = hop(held, 6)
    u2 = shifted(u1, -2)
    v2 = shifted(v1, 2)
    xu1 = peer(u1)
    xv1 = peer(v1)
    f3, total = tie((f3, total))
    square, total = call(
        square_kernel,
        (sign, left, own, p0, u1, v1, xu1, xv1, total),
        [jax.ShapeDtypeStruct((R, 9 * R), bf16), jax.ShapeDtypeStruct((R, 13 * R), f32)],
        [pltpu.VMEM((R, 9 * R), f32)],
    )
    held, u2, v2, total = tie((held, u2, v2, total))
    b3 = hop(held, -6)
    xu2 = peer(u2)
    xv2 = peer(v2)
    xf3 = peer(f3)
    before, partial, last = cube_call(
        sign, square, own, p0, u1, v1, xu1, xv1, u2, v2, xu2, xv2, f3, xf3, total
    )
    return edge_call(sign, last, b3, partial, before)


def solution(mesh):
    in_specs = (P("blk", None), P("blk", None))
    out_specs = P("blk", None)
    return jax.shard_map(local, mesh=mesh, in_specs=in_specs, out_specs=out_specs, check_vma=False)
```

time: 70.5 us -> 61.5 us (0.87)
  the two profiles are of different devices: /device:TPU:1 before, /device:TPU:17 now
where the time goes in v3:
time: 61.5 us; the launch traced here: 61.2 us
  waiting for transfers between devices  27.8 us (45%)
  starting transfers between devices  16.8 us (27%)
  Pallas kernels  16.5 us (27%)
    ppermute x4, waiting for transfers between devices, shifted(): lax.ppermute(value, 'blk', [((target + steps) % size, target) for target...  22.5 us
    ppermute x2, starting transfers between devices, hop(): return lax.ppermute(value, 'blk', pairs)  11.2 us
    pallas_call x1, Pallas kernels, cube_call(): pl.pallas_call(cube_kernel, in_specs=[pl.BlockSpec(memory_space=pltpu.SME...  7.29 us
    pallas_call x2, Pallas kernels, call(): pl.pallas_call(kernel, in_specs=specs, out_specs=[pl.BlockSpec(memory_spa...  5.47 us
    ppermute x2, waiting for transfers between devices, hop(): return lax.ppermute(value, 'blk', pairs)  4.99 us
    ppermute x4, starting transfers between devices, shifted(): lax.ppermute(value, 'blk', [((target + steps) % size, target) for target...  2.95 us
    ppermute x6, starting transfers between devices, peer(): lax.ppermute(value, 'blk', [(source, source ^ 1) for source in range(size)])  2.59 us
    pallas_call x1, Pallas kernels, pack(): pl.pallas_call(pack_kernel, in_specs=[pl.BlockSpec(memory_space=pltpu.HBM...  2.39 us
  transfers between devices with their start and end apart: 12, of which 5 were waited for; matrix products, arithmetic and copies ran while one was open for 0% of the time, Pallas kernels for 21%

profile of v3, /device:TPU:17, one launch (start us, length us, event | category | flops | bytes accessed | tf_op | source)
XLA Modules:
  0.0 61.2 jit_solution(14002142413477670921)
XLA Ops:
  0.0 2.4 %shard_map.28.own = bf16[2064,128]{1,0:T(8,128)(2,1)} custom-call(s32[256,1280]{1,0:T(8,128)} %adjacency_hbm.1, bf16[256,1280]{1,0:T(8,128)(2,1)} %weight_hbm.1), custom_call_target="tpu_custom_call" | custom-call | flops 1310720 | bytes 2494464 | tf_op jit(solution)/shard_map/pallas_call | solution.py:66
  2.4 0.8 %collective-permute-start = (bf16[2064,128]{1,0:T(8,128)(2,1)}, bf16[2064,128]{1,0:T(8,128)(2,1)S(1)}, u32[]{:S(2)}, u32[]{:S(2)}) collective-permute-start(bf16[2064,128]{1,0:T(8,128)(2,1)} %shard_map.28.own), channel_id=1, source_target_pairs={{0,1},{1,0},{2,3},{3,2},{4,5},{5,4},{6,7},{7,6},{8,9},{9,8},{10,11... | collective-permute-start | bytes 1585160 | tf_op jit(solution)/shard_map/ppermute | solution.py:266
  3.2 1.0 %collective-permute-start.1 = (bf16[2064,128]{1,0:T(8,128)(2,1)}, bf16[2064,128]{1,0:T(8,128)(2,1)S(1)}, u32[]{:S(2)}, u32[]{:S(2)}) collective-permute-start(bf16[2064,128]{1,0:T(8,128)(2,1)} %shard_map.28.own), channel_id=1, source_target_pairs={{254,0},{255,1},{0,2},{1,3},{2,4},{3,5},{4,6},{5,7},{6,8},{7,9},{8... | collective-permute-start | bytes 1585160 | tf_op jit(solution)/shard_map/ppermute | solution.py:263
  4.2 0.5 collective-permute-start.2
  4.6 0.3 collective-permute-done.p0
  4.9 1.7 %shard_map.29 = (bf16[256,1280]{1,0:T(8,128)(2,1)S(1)}, f32[256,2304]{1,0:T(8,128)S(1)}) custom-call(s32[1]{0:T(128)} %bitcast.sign_ref, bf16[2064,128]{1,0:T(8,128)(2,1)} %shard_map.28.own, bf16[2064,128]{1,0:T(8,128)(2,1)S(1)} %collective-permute-done.p0), custom_call_target="tpu_custom_call" | custom-call | bytes 104857 | tf_op jit(solution)/shard_map/pallas_call | solution.py:239
  6.6 1.2 %collective-permute-start.5 = (bf16[2064,128]{1,0:T(8,128)(2,1)}, bf16[2064,128]{1,0:T(8,128)(2,1)S(1)}, u32[]{:S(2)}, u32[]{:S(2)}) collective-permute-start(bf16[2064,128]{1,0:T(8,128)(2,1)} %shard_map.28.own), channel_id=1, source_target_pairs={{6,0},{251,1},{8,2},{253,3},{10,4},{255,5},{12,6},{1,7},{14,8},{3,... | collective-permute-start | bytes 1585160 | tf_op jit(solution)/shard_map/ppermute | solution.py:260
  7.8 14.8 %collective-permute-done.1.u1 = bf16[2064,128]{1,0:T(8,128)(2,1)S(1)} collective-permute-done((bf16[2064,128]{1,0:T(8,128)(2,1)}, bf16[2064,128]{1,0:T(8,128)(2,1)S(1)}, u32[]{:S(2)}, u32[]{:S(2)}) %collective-permute-start.1) | collective-permute-done | bytes 528416 | tf_op jit(solution)/shard_map/ppermute | solution.py:263
  22.6 0.9 %collective-permute-start.3 = (bf16[2064,128]{1,0:T(8,128)(2,1)S(1)}, bf16[2064,128]{1,0:T(8,128)(2,1)S(1)}, u32[]{:S(2)}, u32[]{:S(2)}) collective-permute-start(bf16[2064,128]{1,0:T(8,128)(2,1)S(1)} %collective-permute-done.1.u1), channel_id=1, source_target_pairs={{0,1},{1,0},{2,3},{3,2},{4,5},{5,4},{6,7},{7,6},{8,9},{9,8},{10,11... | collective-permute-start | bytes 1585160 | tf_op jit(solution)/shard_map/ppermute | solution.py:266
  23.5 0.0 collective-permute-done.2.v1
  23.5 0.0 collective-permute-start.4
  23.5 1.0 %collective-permute-start.6 = (bf16[2064,128]{1,0:T(8,128)(2,1)S(1)}, bf16[2064,128]{1,0:T(8,128)(2,1)S(1)}, u32[]{:S(2)}, u32[]{:S(2)}) collective-permute-start(bf16[2064,128]{1,0:T(8,128)(2,1)S(1)} %collective-permute-done.1.u1), channel_id=1, source_target_pairs={{254,0},{255,1},{0,2},{1,3},{2,4},{3,5},{4,6},{5,7},{6,8},{7,9},{8... | collective-permute-start | bytes 1585160 | tf_op jit(solution)/shard_map/ppermute | solution.py:263
  24.5 0.5 collective-permute-start.7
  25.0 5.0 %collective-permute-done.5.f3 = bf16[2064,128]{1,0:T(8,128)(2,1)S(1)} collective-permute-done((bf16[2064,128]{1,0:T(8,128)(2,1)}, bf16[2064,128]{1,0:T(8,128)(2,1)S(1)}, u32[]{:S(2)}, u32[]{:S(2)}) %collective-permute-start.5) | collective-permute-done | bytes 528416 | tf_op jit(solution)/shard_map/ppermute | solution.py:260
  29.9 0.0 collective-permute-done.3.xu1
  29.9 0.0 collective-permute-done.4.xv1
  30.0 3.8 %shard_map.30 = (bf16[256,2304]{1,0:T(8,128)(2,1)S(1)}, f32[256,3328]{1,0:T(8,128)S(1)}) custom-call(s32[1]{0:T(128)} %bitcast.sign_ref, bf16[256,1280]{1,0:T(8,128)(2,1)S(1)} %get-tuple-element.20.left_ref, bf16[2064,128]{1,0:T(8,128)(2,1)} %shard_map.28.own, bf16[2064,128]{1,0:T(8,128)(2,1)S(1)} %collective-permute-done.p0, ...), custom_call_target="tpu_custom_call" | custom-call | bytes 104857 | tf_op jit(solution)/shard_map/pallas_call | solution.py:239
  33.7 2.8 %collective-permute-done.6.u2 = bf16[2064,128]{1,0:T(8,128)(2,1)S(1)} collective-permute-done((bf16[2064,128]{1,0:T(8,128)(2,1)S(1)}, bf16[2064,128]{1,0:T(8,128)(2,1)S(1)}, u32[]{:S(2)}, u32[]{:S(2)}) %collective-permute-start.6) | collective-permute-done | bytes 528416 | tf_op jit(solution)/shard_map/ppermute | solution.py:263
  36.6 4.9 %collective-permute-done.7.v2 = bf16[2064,128]{1,0:T(8,128)(2,1)S(1)} collective-permute-done((bf16[2064,128]{1,0:T(8,128)(2,1)S(1)}, bf16[2064,128]{1,0:T(8,128)(2,1)S(1)}, u32[]{:S(2)}, u32[]{:S(2)}) %collective-permute-start.7) | collective-permute-done | bytes 528416 | tf_op jit(solution)/shard_map/ppermute | solution.py:263
  41.4 0.4 collective-permute-start.8
  41.9 0.1 collective-permute-start.9
  41.9 0.4 collective-permute-start.10
  42.4 10.1 %collective-permute-start.11 = (bf16[2064,128]{1,0:T(8,128)(2,1)}, bf16[2064,128]{1,0:T(8,128)(2,1)S(1)}, u32[]{:S(2)}, u32[]{:S(2)}) collective-permute-start(bf16[2064,128]{1,0:T(8,128)(2,1)} %shard_map.28.own), channel_id=1, source_target_pairs={{250,0},{7,1},{252,2},{9,3},{254,4},{11,5},{0,6},{13,7},{2,8},{15,... | collective-permute-start | bytes 1585160 | tf_op jit(solution)/shard_map/ppermute | solution.py:260
  52.4 0.0 collective-permute-done.8.xu2
  52.4 0.0 collective-permute-done.9.xv2
  52.4 0.0 collective-permute-done.10.xf3
  52.4 7.3 %shard_map.31 = (f32[256,4352]{1,0:T(8,128)}, f32[256,1280]{1,0:T(8,128)S(1)}, bf16[256,256]{1,0:T(8,128)(2,1)S(1)}) custom-call(s32[1]{0:T(128)} %bitcast.sign_ref, bf16[256,2304]{1,0:T(8,128)(2,1)S(1)} %get-tuple-element.25.left_ref, bf16[2064,128]{1,0:T(8,128)(2,1)} %shard_map.28.own, bf16[2064,128]{1,0:T(8,128)(2,1)S(1)} %collective-permute-done.p0, ...), custom_call_target="tpu_custom_call" | custom-call | bytes 104857 | tf_op jit(solution)/shard_map/pallas_call | solution.py:181
  59.7 0.0 collective-permute-done.11.b3
  59.7 1.3 %shard_map.32 = f32[256,4352]{1,0:T(8,128)} custom-call(s32[1]{0:T(128)} %bitcast.sign_ref, bf16[256,256]{1,0:T(8,128)(2,1)S(1)} %get-tuple-element.31.left_ref, bf16[2064,128]{1,0:T(8,128)(2,1)S(1)} %collective-permute-done.11.b3, f32[256,1280]{1,0:T(8,128)S(1)} %get-tuple-element.33.partial_ref, ...), custom_call_target="tpu_custom_call", output_to_operand_aliasing={{}: (4, {})} | custom-call | bytes 104857 | tf_op jit(solution)/shard_map/pallas_call | solution.py:221
Async XLA Ops:
  2.4 2.5 %collective-permute-start = (bf16[2064,128]{1,0:T(8,128)(2,1)}, bf16[2064,128]{1,0:T(8,128)(2,1)S(1)}, u32[]{:S(2)}, u32[]{:S(2)}) collective-permute-start(bf16[2064,128]{1,0:T(8,128)(2,1)} %shard_map.28.own), channel_id=1, source_target_pairs={{0,1},{1,0},{2,3},{3,2},{4,5},{5,4},{6,7},{7,6},{8,9},{9,8},{10,11... | collective-permute-start | bytes 1585160 | tf_op jit(solution)/shard_map/ppermute | solution.py:266
  3.2 19.4 %collective-permute-start.1 = (bf16[2064,128]{1,0:T(8,128)(2,1)}, bf16[2064,128]{1,0:T(8,128)(2,1)S(1)}, u32[]{:S(2)}, u32[]{:S(2)}) collective-permute-start(bf16[2064,128]{1,0:T(8,128)(2,1)} %shard_map.28.own), channel_id=1, source_target_pairs={{254,0},{255,1},{0,2},{1,3},{2,4},{3,5},{4,6},{5,7},{6,8},{7,9},{8... | collective-permute-start | bytes 1585160 | tf_op jit(solution)/shard_map/ppermute | solution.py:263
  4.2 19.3 %collective-permute-start.2 = (bf16[2064,128]{1,0:T(8,128)(2,1)}, bf16[2064,128]{1,0:T(8,128)(2,1)S(1)}, u32[]{:S(2)}, u32[]{:S(2)}) collective-permute-start(bf16[2064,128]{1,0:T(8,128)(2,1)} %shard_map.28.own), channel_id=1, source_target_pairs={{2,0},{3,1},{4,2},{5,3},{6,4},{7,5},{8,6},{9,7},{10,8},{11,9},{12,... | collective-permute-start | bytes 1585160 | tf_op jit(solution)/shard_map/ppermute | solution.py:263
  6.6 23.3 %collective-permute-start.5 = (bf16[2064,128]{1,0:T(8,128)(2,1)}, bf16[2064,128]{1,0:T(8,128)(2,1)S(1)}, u32[]{:S(2)}, u32[]{:S(2)}) collective-permute-start(bf16[2064,128]{1,0:T(8,128)(2,1)} %shard_map.28.own), channel_id=1, source_target_pairs={{6,0},{251,1},{8,2},{253,3},{10,4},{255,5},{12,6},{1,7},{14,8},{3,... | collective-permute-start | bytes 1585160 | tf_op jit(solution)/shard_map/ppermute | solution.py:260
  22.6 7.3 %collective-permute-start.3 = (bf16[2064,128]{1,0:T(8,128)(2,1)S(1)}, bf16[2064,128]{1,0:T(8,128)(2,1)S(1)}, u32[]{:S(2)}, u32[]{:S(2)}) collective-permute-start(bf16[2064,128]{1,0:T(8,128)(2,1)S(1)} %collective-permute-done.1.u1), channel_id=1, source_target_pairs={{0,1},{1,0},{2,3},{3,2},{4,5},{5,4},{6,7},{7,6},{8,9},{9,8},{10,11... | collective-permute-start | bytes 1585160 | tf_op jit(solution)/shard_map/ppermute | solution.py:266
  23.5 6.5 %collective-permute-start.4 = (bf16[2064,128]{1,0:T(8,128)(2,1)S(1)}, bf16[2064,128]{1,0:T(8,128)(2,1)S(1)}, u32[]{:S(2)}, u32[]{:S(2)}) collective-permute-start(bf16[2064,128]{1,0:T(8,128)(2,1)S(1)} %collective-permute-done.2.v1), channel_id=1, source_target_pairs={{0,1},{1,0},{2,3},{3,2},{4,5},{5,4},{6,7},{7,6},{8,9},{9,8},{10,11... | collective-permute-start | bytes 1585160 | tf_op jit(solution)/shard_map/ppermute | solution.py:266
  23.5 13.1 %collective-permute-start.6 = (bf16[2064,128]{1,0:T(8,128)(2,1)S(1)}, bf16[2064,128]{1,0:T(8,128)(2,1)S(1)}, u32[]{:S(2)}, u32[]{:S(2)}) collective-permute-start(bf16[2064,128]{1,0:T(8,128)(2,1)S(1)} %collective-permute-done.1.u1), channel_id=1, source_target_pairs={{254,0},{255,1},{0,2},{1,3},{2,4},{3,5},{4,6},{5,7},{6,8},{7,9},{8... | collective-permute-start | bytes 1585160 | tf_op jit(solution)/shard_map/ppermute | solution.py:263
  24.5 16.9 %collective-permute-start.7 = (bf16[2064,128]{1,0:T(8,128)(2,1)S(1)}, bf16[2064,128]{1,0:T(8,128)(2,1)S(1)}, u32[]{:S(2)}, u32[]{:S(2)}) collective-permute-start(bf16[2064,128]{1,0:T(8,128)(2,1)S(1)} %collective-permute-done.2.v1), channel_id=1, source_target_pairs={{2,0},{3,1},{4,2},{5,3},{6,4},{7,5},{8,6},{9,7},{10,8},{11,9},{12,... | collective-permute-start | bytes 1585160 | tf_op jit(solution)/shard_map/ppermute | solution.py:263
  41.4 11.0 %collective-permute-start.8 = (bf16[2064,128]{1,0:T(8,128)(2,1)S(1)}, bf16[2064,128]{1,0:T(8,128)(2,1)S(1)}, u32[]{:S(2)}, u32[]{:S(2)}) collective-permute-start(bf16[2064,128]{1,0:T(8,128)(2,1)S(1)} %collective-permute-done.6.u2), channel_id=1, source_target_pairs={{0,1},{1,0},{2,3},{3,2},{4,5},{5,4},{6,7},{7,6},{8,9},{9,8},{10,11... | collective-permute-start | bytes 1585160 | tf_op jit(solution)/shard_map/ppermute | solution.py:266
  41.9 10.6 %collective-permute-start.9 = (bf16[2064,128]{1,0:T(8,128)(2,1)S(1)}, bf16[2064,128]{1,0:T(8,128)(2,1)S(1)}, u32[]{:S(2)}, u32[]{:S(2)}) collective-permute-start(bf16[2064,128]{1,0:T(8,128)(2,1)S(1)} %collective-permute-done.7.v2), channel_id=1, source_target_pairs={{0,1},{1,0},{2,3},{3,2},{4,5},{5,4},{6,7},{7,6},{8,9},{9,8},{10,11... | collective-permute-start | bytes 1585160 | tf_op jit(solution)/shard_map/ppermute | solution.py:266
  41.9 10.5 %collective-permute-start.10 = (bf16[2064,128]{1,0:T(8,128)(2,1)S(1)}, bf16[2064,128]{1,0:T(8,128)(2,1)S(1)}, u32[]{:S(2)}, u32[]{:S(2)}) collective-permute-start(bf16[2064,128]{1,0:T(8,128)(2,1)S(1)} %collective-permute-done.5.f3), channel_id=1, source_target_pairs={{0,1},{1,0},{2,3},{3,2},{4,5},{5,4},{6,7},{7,6},{8,9},{9,8},{10,11... | collective-permute-start | bytes 1585160 | tf_op jit(solution)/shard_map/ppermute | solution.py:266
  42.4 17.4 %collective-permute-start.11 = (bf16[2064,128]{1,0:T(8,128)(2,1)}, bf16[2064,128]{1,0:T(8,128)(2,1)S(1)}, u32[]{:S(2)}, u32[]{:S(2)}) collective-permute-start(bf16[2064,128]{1,0:T(8,128)(2,1)} %shard_map.28.own), channel_id=1, source_target_pairs={{250,0},{7,1},{252,2},{9,3},{254,4},{11,5},{0,6},{13,7},{2,8},{15,... | collective-permute-start | bytes 1585160 | tf_op jit(solution)/shard_map/ppermute | solution.py:260

commit v4 on v3

v4 whole, which is shorter than its diff:
```python
import math

import jax
import jax.numpy as jnp
from jax import lax
from jax.experimental import pallas as pl
from jax.experimental.pallas import tpu as pltpu
from jax.sharding import PartitionSpec as P

B = 512
R = 256
LANES = 128
TILES = 1024 // LANES
ROWS = TILES * R + 16
FIRST_SCALE = 1.0 / math.sqrt(B)
LAST_SCALE = 1.0 / (math.sqrt(B) * math.sqrt(2 * B))
MIB = 1 << 20


def pack_kernel(adjacency_hbm, weight_hbm, packed_hbm, edges, weights, packed, in_semaphores, out_semaphores):
    copies = {}
    for part in (0, 4, 1, 2, 3):
        columns = slice(part * R, (part + 1) * R)
        for index, (source, target) in enumerate(((adjacency_hbm, edges), (weight_hbm, weights))):
            semaphore = in_semaphores.at[index, part]
            copies[index, part] = pltpu.make_async_copy(source.at[:, columns], target.at[:, columns], semaphore)
            copies[index, part].start()
    row = lax.broadcasted_iota(jnp.int32, (R, LANES), 0)
    lane = lax.broadcasted_iota(jnp.int32, (R, LANES), 1)
    leaving = []

    def leave(rows, index):
        copy = pltpu.make_async_copy(packed.at[rows, :], packed_hbm.at[rows, :], out_semaphores.at[index])
        copy.start()
        leaving.append(copy)

    def arrive(part):
        copies[0, part].wait()
        copies[1, part].wait()

    def tile(index):
        columns = slice(index * LANES, (index + 1) * LANES)
        return edges[:, columns] == 1, weights[:, columns].astype(jnp.float32)

    arrive(0)
    arrive(4)
    place = lax.broadcasted_iota(jnp.int32, (16, LANES), 0)
    tail = jnp.zeros((16, LANES), jnp.float32)
    for half in range(2):
        column = lane + half * LANES
        near_edge, near = tile(half)
        far_edge, far = tile(8 + half)
        near = jnp.where(near_edge, near, 0.0)
        far = jnp.where(far_edge, far, 0.0)
        packed[half * R : (half + 1) * R, :] = jnp.where(column >= row, near, far).astype(jnp.bfloat16)
        diagonal = jnp.sum(jnp.where(column == row, far, 0.0), axis=0, keepdims=True)
        tail = jnp.where(place == half, diagonal, tail)
    packed[TILES * R :, :] = tail.astype(jnp.bfloat16)
    leave(slice(0, 2 * R), 0)
    leave(slice(TILES * R, ROWS), 4)
    for part in (1, 2, 3):
        arrive(part)
        for half in range(2):
            index = 2 * part + half
            edge, value = tile(index)
            if part == 2:
                edge = edge | (lane + half * LANES == row)
            packed[index * R : (index + 1) * R, :] = jnp.where(edge, value, 0.0).astype(jnp.bfloat16)
        leave(slice(2 * part * R, 2 * (part + 1) * R), part)
    for copy in leaving:
        copy.wait()


def pack(adjacency, weight):
    hbm = pl.BlockSpec(memory_space=pltpu.HBM)
    return pl.pallas_call(
        pack_kernel,
        in_specs=[hbm, hbm],
        out_specs=hbm,
        out_shape=jax.ShapeDtypeStruct((ROWS, LANES), jnp.bfloat16),
        scratch_shapes=[
            pltpu.VMEM((R, 5 * R), jnp.int32),
            pltpu.VMEM((R, 5 * R), jnp.bfloat16),
            pltpu.VMEM((ROWS, LANES), jnp.bfloat16),
            pltpu.SemaphoreType.DMA((2, 5)),
            pltpu.SemaphoreType.DMA((5,)),
        ],
        compiler_params=pltpu.CompilerParams(vmem_limit_bytes=56 * MIB),
        cost_estimate=pl.CostEstimate(flops=R * 5 * R * 4, bytes_accessed=R * 5 * R * 6 + ROWS * 256, transcendentals=0),
    )(adjacency, weight)


def slot(ref, index):
    begin = index * 2 * R
    return jnp.concatenate([ref[begin : begin + R, :], ref[begin + R : begin + 2 * R, :]], axis=1)


def unpacked(ref):
    row = lax.broadcasted_iota(jnp.int32, (R, R), 0)
    column = lax.broadcasted_iota(jnp.int32, (R, R), 1)
    merged = slot(ref, 0).astype(jnp.float32)
    tail = ref[TILES * R :, :].astype(jnp.float32)
    diagonal = jnp.concatenate([tail[0:1, :], tail[1:2, :]], axis=1)
    first = jnp.where(column >= row, merged, 0.0)
    last = jnp.where(column < row, merged, jnp.where(column == row, diagonal, 0.0))
    return [
        first.astype(jnp.bfloat16),
        slot(ref, 1),
        slot(ref, 2),
        slot(ref, 3),
        last.astype(jnp.bfloat16),
    ]


def block(index):
    return pl.ds(pl.multiple_of(index * R, R), R)


def accumulate(total_ref, left, ref, first_block):
    for offset, right in enumerate(unpacked(ref)):
        where = block(first_block + offset)
        total_ref[:, where] += jnp.dot(left, right, preferred_element_type=jnp.float32)


def near_kernel(sign_ref, own, p0, left_ref, total_ref):
    sign = sign_ref[0]
    for offset, part in enumerate(unpacked(own)):
        left_ref[:, offset * R : (offset + 1) * R] = part
    total_ref[...] = jnp.zeros_like(total_ref)
    for at, ref in ((0, own), (sign, p0)):
        accumulate(total_ref, left_ref[:, block(at + 2)], ref, at + 2)


def square_kernel(sign_ref, left_ref, own, p0, v1, u1, xv1, xu1, before_ref, square_ref, total_ref, work_ref):
    sign = sign_ref[0]
    work_ref[...] = before_ref[...]
    for at, ref in ((-2, u1), (2, v1)):
        accumulate(work_ref, left_ref[:, block(at + 2)], ref, at + 2)

    @pl.when(sign > 0)
    def _():
        accumulate(work_ref, left_ref[:, block(1)], xu1, 1)

    @pl.when(sign < 0)
    def _():
        accumulate(work_ref, left_ref[:, block(3)], xv1, 3)

    square_ref[...] = (work_ref[...] * FIRST_SCALE).astype(jnp.bfloat16)
    total_ref[...] = jnp.zeros_like(total_ref)
    for at, ref in ((0, own), (sign, p0), (-2, u1), (2, v1), (sign - 2, xu1), (sign + 2, xv1)):
        accumulate(total_ref, square_ref[:, block(at + 4)], ref, at + 4)


def piece(ref, index):
    if index in (1, 2, 3):
        return slot(ref, index)
    row = lax.broadcasted_iota(jnp.int32, (R, R), 0)
    column = lax.broadcasted_iota(jnp.int32, (R, R), 1)
    merged = slot(ref, 0).astype(jnp.float32)
    if index == 0:
        return jnp.where(column >= row, merged, 0.0).astype(jnp.bfloat16)
    tail = ref[TILES * R :, :].astype(jnp.float32)
    diagonal = jnp.concatenate([tail[0:1, :], tail[1:2, :]], axis=1)
    return jnp.where(column < row, merged, jnp.where(column == row, diagonal, 0.0)).astype(jnp.bfloat16)


def band_dot(lefts, rows, at):
    places = [place for place in sorted(rows) if abs(at - place) <= 2]
    left = jnp.concatenate([lefts[place][...] for place in places], axis=1)
    right = jnp.concatenate([piece(rows[place], at - place + 2) for place in places], axis=0)
    return jnp.dot(left, right, preferred_element_type=jnp.float32)


def columns_of(ref, place, span):
    return ref.at[:, (place + span) * R : (place + span + 1) * R]


def both_cores(sign_ref, body):
    for sign in (1, -1):
        pl.when(sign_ref[0] == sign)(lambda sign=sign: body(sign))


def forward_kernel(sign_ref, left_ref, own, p0, v1, u1, xv1, xu1, v2, u2, f3, before_ref, cube_ref, rest_ref, sum_ref):
    def body(sign):
        rows = {0: own, sign: p0, -2: u1, 2: v1, sign - 2: xu1, sign + 2: xv1, -4: u2, 4: v2, 6 * sign: f3}
        outer = {place: rows[place] for place in (-4, 4)}
        for at in range(-6, 7):
            value = columns_of(before_ref, at, 6)[...]
            if abs(at) >= 2:
                value = value + band_dot({p: columns_of(left_ref, p, 4) for p in outer}, outer, at)
            if -6 < at * sign < 0:
                columns_of(rest_ref, at * sign, 5)[...] = value
            else:
                columns_of(cube_ref, at, 6)[...] = (value * LAST_SCALE).astype(jnp.bfloat16)
        ready = {place * sign: rows[place * sign] for place in (0, 1, 2, 3, 4, 6)}
        for at in range(-2, 9):
            lefts = {place: columns_of(cube_ref, place, 6) for place in ready}
            columns_of(sum_ref, at * sign, 8)[...] = band_dot(lefts, ready, at * sign)

    both_cores(sign_ref, body)


def edge_kernel(sign_ref, cube_ref, b3, product_ref):
    left = cube_ref[:, block(6 - 6 * sign_ref[0])]
    for index in range(5):
        right = piece(b3, index)
        product_ref[:, index * R : (index + 1) * R] = jnp.dot(left, right, preferred_element_type=jnp.float32)


def last_kernel(
    sign_ref, left_ref, v1, u1, xv1, xu1, v2, u2, xv2, xu2, xf3, edge_ref, cube_ref, rest_ref, sum_ref,
    out_hbm, late_ref, result_ref, semaphores,
):
    def body(sign):
        rows = {-2: u1, 2: v1, sign - 2: xu1, sign + 2: xv1, -4: u2, 4: v2, sign - 4: xu2, sign + 4: xv2}
        rows[-5 * sign] = xf3
        copies = []

        def leave(at, ref):
            place = columns_of(out_hbm, at, 8)
            copy = pltpu.make_async_copy(columns_of(ref, at, 8), place, semaphores.at[at + 8])
            copy.start()
            copies.append(copy)

        for at in (2, 8):
            leave(at * sign, sum_ref)
        third = {-3 * sign: rows[-3 * sign]}
        lefts = {5 * sign: columns_of(cube_ref, 5 * sign, 6)}
        for at in range(-5, 0):
            value = columns_of(rest_ref, at, 5)[...]
            value = value + band_dot({-3 * sign: columns_of(left_ref, -3 * sign, 4)}, third, at * sign)
            columns_of(late_ref, at, 5)[...] = (value * LAST_SCALE).astype(jnp.bfloat16)
            lefts[at * sign] = columns_of(late_ref, at, 5)
        ready = {place: rows[place] for place in lefts}
        for at in (3, 4, 5, 6, 7, 1, 0, -1, -2, -3, -4, -5, -6, -7, -8):
            if at > -8:
                value = band_dot(lefts, ready, at * sign)
            else:
                value = jnp.zeros((R, R), jnp.float32)
            if at <= -4:
                value = value + columns_of(edge_ref, at * sign + 6 * sign, 2)[...]
            if at >= -2:
                value = value + columns_of(sum_ref, at * sign, 8)[...]
            columns_of(result_ref, at * sign, 8)[...] = value
            leave(at * sign, result_ref)
        for copy in copies:
            copy.wait()

    both_cores(sign_ref, body)


def last_call(*arrays):
    return pl.pallas_call(
        last_kernel,
        in_specs=[pl.BlockSpec(memory_space=pltpu.SMEM)] + [pl.BlockSpec(memory_space=pltpu.VMEM)] * (len(arrays) - 1),
        out_specs=pl.BlockSpec(memory_space=pltpu.HBM),
        out_shape=jax.ShapeDtypeStruct((R, 17 * R), jnp.float32),
        scratch_shapes=[
            pltpu.VMEM((R, 5 * R), jnp.bfloat16),
            pltpu.VMEM((R, 17 * R), jnp.float32),
            pltpu.SemaphoreType.DMA((17,)),
        ],
        compiler_params=pltpu.CompilerParams(vmem_limit_bytes=30 * MIB),
        cost_estimate=COST,
    )(*arrays)


COST = pl.CostEstimate(flops=0, bytes_accessed=int(0.1 * MIB), transcendentals=0)


def call(kernel, arrays, shapes, scratch):
    specs = [pl.BlockSpec(memory_space=pltpu.SMEM)]
    specs += [pl.BlockSpec(memory_space=pltpu.VMEM)] * (len(arrays) - 1)
    return pl.pallas_call(
        kernel,
        in_specs=specs,
        out_specs=[pl.BlockSpec(memory_space=pltpu.VMEM)] * len(shapes),
        out_shape=shapes,
        scratch_shapes=scratch,
        compiler_params=pltpu.CompilerParams(vmem_limit_bytes=24 * MIB),
        cost_estimate=COST,
    )(*arrays)


def local(adjacency, weight):
    size = lax.axis_size("blk")
    parity = lax.rem(lax.axis_index("blk"), 2)
    sign = (1 - 2 * parity).astype(jnp.int32).reshape(1)

    def hop(value, steps):
        pairs = []
        for target in range(size):
            ahead = steps if target % 2 == 0 else -steps
            pairs.append(((target + ahead) % size, target))
        return lax.ppermute(value, "blk", pairs)

    def shifted(value, steps):
        return lax.ppermute(value, "blk", [((target + steps) % size, target) for target in range(size)])

    def peer(value):
        return lax.ppermute(value, "blk", [(source, source ^ 1) for source in range(size)])

    tie = lax.optimization_barrier
    f32, bf16 = jnp.float32, jnp.bfloat16
    own = pack(adjacency, weight)
    u1 = shifted(own, -2)
    v1 = shifted(own, 2)
    p0 = peer(own)
    left, total = call(
        near_kernel,
        (sign, own, p0),
        [jax.ShapeDtypeStruct((R, 5 * R), bf16), jax.ShapeDtypeStruct((R, 9 * R), f32)],
        [],
    )
    held, total = tie((own, total))
    f3 = hop(held, 6)
    u2 = shifted(u1, -2)
    v2 = shifted(v1, 2)
    xu1 = peer(u1)
    xv1 = peer(v1)
    f3, total = tie((f3, total))
    square, total = call(
        square_kernel,
        (sign, left, own, p0, v1, u1, xv1, xu1, total),
        [jax.ShapeDtypeStruct((R, 9 * R), bf16), jax.ShapeDtypeStruct((R, 13 * R), f32)],
        [pltpu.VMEM((R, 9 * R), f32)],
    )
    held, total = tie((held, total))
    b3 = hop(held, -6)
    u2, v2, total = tie((u2, v2, total))
    xu2 = peer(u2)
    xv2 = peer(v2)
    xf3 = peer(f3)
    cube, rest, total = call(
        forward_kernel,
        (sign, square, own, p0, v1, u1, xv1, xu1, v2, u2, f3, total),
        [
            jax.ShapeDtypeStruct((R, 13 * R), bf16),
            jax.ShapeDtypeStruct((R, 5 * R), f32),
            jax.ShapeDtypeStruct((R, 17 * R), f32),
        ],
        [],
    )
    (edge,) = call(edge_kernel, (sign, cube, b3), [jax.ShapeDtypeStruct((R, 5 * R), f32)], [])
    return last_call(sign, square, v1, u1, xv1, xu1, v2, u2, xv2, xu2, xf3, edge, cube, rest, total)


def solution(mesh):
    in_specs = (P("blk", None), P("blk", None))
    out_specs = P("blk", None)
    return jax.shard_map(local, mesh=mesh, in_specs=in_specs, out_specs=out_specs, check_vma=False)
```

time: 61.5 us -> 56.1 us (0.912)
  the two profiles are of different devices: /device:TPU:17 before, /device:TPU:1 now
where the time goes in v4:
time: 56.1 us; the launch traced here: 55.9 us
  starting transfers between devices  26 us (46%)
  waiting for transfers between devices  16.1 us (29%)
  Pallas kernels  13.5 us (24%)
    ppermute x4, starting transfers between devices, shifted(): lax.ppermute(value, 'blk', [((target + steps) % size, target) for target...  15.4 us
    ppermute x4, waiting for transfers between devices, shifted(): lax.ppermute(value, 'blk', [((target + steps) % size, target) for target...  14.2 us
    pallas_call x4, Pallas kernels, call(): pl.pallas_call(kernel, in_specs=specs, out_specs=[pl.BlockSpec(memory_spa...  8.51 us
    ppermute x6, starting transfers between devices, peer(): lax.ppermute(value, 'blk', [(source, source ^ 1) for source in range(size)])  7.27 us
    ppermute x2, starting transfers between devices, hop(): return lax.ppermute(value, 'blk', pairs)  3.38 us
    pallas_call x1, Pallas kernels, last_call(): pl.pallas_call(last_kernel, in_specs=[pl.BlockSpec(memory_space=pltpu.SME...  2.68 us
    pallas_call x1, Pallas kernels, pack(): pl.pallas_call(pack_kernel, in_specs=[hbm, hbm], out_specs=hbm, out_shape...  2.31 us
    ppermute x2, waiting for transfers between devices, hop(): return lax.ppermute(value, 'blk', pairs)  1.93 us
  transfers between devices with their start and end apart: 12, of which 3 were waited for; matrix products, arithmetic and copies ran while one was open for 0% of the time, Pallas kernels for 15%

profile of v4, /device:TPU:1, one launch (start us, length us, event | category | flops | bytes accessed | tf_op | source)
XLA Modules:
  0.0 55.9 jit_solution(15636802951982733635)
XLA Ops:
  0.0 2.3 %shard_map.28.own = bf16[2064,128]{1,0:T(8,128)(2,1)} custom-call(s32[256,1280]{1,0:T(8,128)} %adjacency_hbm.1, bf16[256,1280]{1,0:T(8,128)(2,1)} %weight_hbm.1), custom_call_target="tpu_custom_call" | custom-call | flops 1310720 | bytes 2494464 | tf_op jit(solution)/shard_map/pallas_call | solution.py:76
  2.3 3.3 %collective-permute-start = (bf16[2064,128]{1,0:T(8,128)(2,1)}, bf16[2064,128]{1,0:T(8,128)(2,1)S(1)}, u32[]{:S(2)}, u32[]{:S(2)}) collective-permute-start(bf16[2064,128]{1,0:T(8,128)(2,1)} %shard_map.28.own), channel_id=1, source_target_pairs={{0,1},{1,0},{2,3},{3,2},{4,5},{5,4},{6,7},{7,6},{8,9},{9,8},{10,11... | collective-permute-start | bytes 1585160 | tf_op jit(solution)/shard_map/ppermute | solution.py:301
  5.6 0.0 collective-permute-start.2
  5.7 8.5 %collective-permute-start.1 = (bf16[2064,128]{1,0:T(8,128)(2,1)}, bf16[2064,128]{1,0:T(8,128)(2,1)S(1)}, u32[]{:S(2)}, u32[]{:S(2)}) collective-permute-start(bf16[2064,128]{1,0:T(8,128)(2,1)} %shard_map.28.own), channel_id=1, source_target_pairs={{2,0},{3,1},{4,2},{5,3},{6,4},{7,5},{8,6},{9,7},{10,8},{11,9},{12,... | collective-permute-start | bytes 1585160 | tf_op jit(solution)/shard_map/ppermute | solution.py:298
  14.1 0.0 collective-permute-done.p0
  14.1 1.7 %shard_map.29 = (bf16[256,1280]{1,0:T(8,128)(2,1)S(1)}, f32[256,2304]{1,0:T(8,128)S(1)}) custom-call(s32[1]{0:T(128)} %bitcast.sign_ref, bf16[2064,128]{1,0:T(8,128)(2,1)} %shard_map.28.own, bf16[2064,128]{1,0:T(8,128)(2,1)S(1)} %collective-permute-done.p0), custom_call_target="tpu_custom_call" | custom-call | bytes 104857 | tf_op jit(solution)/shard_map/pallas_call | solution.py:274
  15.9 0.1 collective-permute-start.5
  16.0 10.7 %collective-permute-done.2.u1 = bf16[2064,128]{1,0:T(8,128)(2,1)S(1)} collective-permute-done((bf16[2064,128]{1,0:T(8,128)(2,1)}, bf16[2064,128]{1,0:T(8,128)(2,1)S(1)}, u32[]{:S(2)}, u32[]{:S(2)}) %collective-permute-start.2) | collective-permute-done | bytes 528416 | tf_op jit(solution)/shard_map/ppermute | solution.py:298
  26.6 1.0 %collective-permute-start.4 = (bf16[2064,128]{1,0:T(8,128)(2,1)S(1)}, bf16[2064,128]{1,0:T(8,128)(2,1)S(1)}, u32[]{:S(2)}, u32[]{:S(2)}) collective-permute-start(bf16[2064,128]{1,0:T(8,128)(2,1)S(1)} %collective-permute-done.2.u1), channel_id=1, source_target_pairs={{0,1},{1,0},{2,3},{3,2},{4,5},{5,4},{6,7},{7,6},{8,9},{9,8},{10,11... | collective-permute-start | bytes 1585160 | tf_op jit(solution)/shard_map/ppermute | solution.py:301
  27.6 0.0 collective-permute-done.1.v1
  27.6 0.0 collective-permute-start.3
  27.6 0.0 collective-permute-start.6
  27.6 6.9 %collective-permute-start.7 = (bf16[2064,128]{1,0:T(8,128)(2,1)S(1)}, bf16[2064,128]{1,0:T(8,128)(2,1)S(1)}, u32[]{:S(2)}, u32[]{:S(2)}) collective-permute-start(bf16[2064,128]{1,0:T(8,128)(2,1)S(1)} %collective-permute-done.1.v1), channel_id=1, source_target_pairs={{2,0},{3,1},{4,2},{5,3},{6,4},{7,5},{8,6},{9,7},{10,8},{11,9},{12,... | collective-permute-start | bytes 1585160 | tf_op jit(solution)/shard_map/ppermute | solution.py:298
  34.5 0.0 collective-permute-done.5.f3
  34.5 1.1 %collective-permute-start.10 = (bf16[2064,128]{1,0:T(8,128)(2,1)S(1)}, bf16[2064,128]{1,0:T(8,128)(2,1)S(1)}, u32[]{:S(2)}, u32[]{:S(2)}) collective-permute-start(bf16[2064,128]{1,0:T(8,128)(2,1)S(1)} %collective-permute-done.5.f3), channel_id=1, source_target_pairs={{0,1},{1,0},{2,3},{3,2},{4,5},{5,4},{6,7},{7,6},{8,9},{9,8},{10,11... | collective-permute-start | bytes 1585160 | tf_op jit(solution)/shard_map/ppermute | solution.py:301
  35.6 0.0 collective-permute-done.4.xu1
  35.6 0.0 collective-permute-done.3.xv1
  35.6 3.7 %shard_map.30 = (bf16[256,2304]{1,0:T(8,128)(2,1)S(1)}, f32[256,3328]{1,0:T(8,128)S(1)}) custom-call(s32[1]{0:T(128)} %bitcast.sign_ref, bf16[256,1280]{1,0:T(8,128)(2,1)S(1)} %get-tuple-element.21.left_ref, bf16[2064,128]{1,0:T(8,128)(2,1)} %shard_map.28.own, bf16[2064,128]{1,0:T(8,128)(2,1)S(1)} %collective-permute-done.p0, ...), custom_call_target="tpu_custom_call" | custom-call | bytes 104857 | tf_op jit(solution)/shard_map/pallas_call | solution.py:274
  39.3 3.3 %collective-permute-start.11 = (bf16[2064,128]{1,0:T(8,128)(2,1)}, bf16[2064,128]{1,0:T(8,128)(2,1)S(1)}, u32[]{:S(2)}, u32[]{:S(2)}) collective-permute-start(bf16[2064,128]{1,0:T(8,128)(2,1)} %shard_map.28.own), channel_id=1, source_target_pairs={{250,0},{7,1},{252,2},{9,3},{254,4},{11,5},{0,6},{13,7},{2,8},{15,... | collective-permute-start | bytes 1585160 | tf_op jit(solution)/shard_map/ppermute | solution.py:295
  42.6 3.5 %collective-permute-done.6.u2 = bf16[2064,128]{1,0:T(8,128)(2,1)S(1)} collective-permute-done((bf16[2064,128]{1,0:T(8,128)(2,1)S(1)}, bf16[2064,128]{1,0:T(8,128)(2,1)S(1)}, u32[]{:S(2)}, u32[]{:S(2)}) %collective-permute-start.6) | collective-permute-done | bytes 528416 | tf_op jit(solution)/shard_map/ppermute | solution.py:298
  46.1 0.0 collective-permute-done.7.v2
  46.1 1.9 %collective-permute-start.8 = (bf16[2064,128]{1,0:T(8,128)(2,1)S(1)}, bf16[2064,128]{1,0:T(8,128)(2,1)S(1)}, u32[]{:S(2)}, u32[]{:S(2)}) collective-permute-start(bf16[2064,128]{1,0:T(8,128)(2,1)S(1)} %collective-permute-done.7.v2), channel_id=1, source_target_pairs={{0,1},{1,0},{2,3},{3,2},{4,5},{5,4},{6,7},{7,6},{8,9},{9,8},{10,11... | collective-permute-start | bytes 1585160 | tf_op jit(solution)/shard_map/ppermute | solution.py:301
  48.0 0.0 collective-permute-start.9
  48.0 2.7 %shard_map.31 = (bf16[256,3328]{1,0:T(8,128)(2,1)S(1)}, f32[256,1280]{1,0:T(8,128)S(1)}, f32[256,4352]{1,0:T(8,128)S(1)}) custom-call(s32[1]{0:T(128)} %bitcast.sign_ref, bf16[256,2304]{1,0:T(8,128)(2,1)S(1)} %get-tuple-element.26.left_ref, bf16[2064,128]{1,0:T(8,128)(2,1)} %shard_map.28.own, bf16[2064,128]{1,0:T(8,128)(2,1)S(1)} %collective-permute-done.p0, ...), custom_call_target="tpu_custom_call" | custom-call | bytes 104857 | tf_op jit(solution)/shard_map/pallas_call | solution.py:274
  50.8 1.9 %collective-permute-done.11.b3 = bf16[2064,128]{1,0:T(8,128)(2,1)S(1)} collective-permute-done((bf16[2064,128]{1,0:T(8,128)(2,1)}, bf16[2064,128]{1,0:T(8,128)(2,1)S(1)}, u32[]{:S(2)}, u32[]{:S(2)}) %collective-permute-start.11) | collective-permute-done | bytes 528416 | tf_op jit(solution)/shard_map/ppermute | solution.py:295
  52.7 0.3 shard_map.32.edge_ref
  53.0 0.0 collective-permute-done.10.xf3
  53.0 0.0 collective-permute-done.8.xv2
  53.0 0.0 collective-permute-done.9.xu2
  53.1 2.7 %shard_map.33 = f32[256,4352]{1,0:T(8,128)} custom-call(s32[1]{0:T(128)} %bitcast.sign_ref, bf16[256,2304]{1,0:T(8,128)(2,1)S(1)} %get-tuple-element.26.left_ref, bf16[2064,128]{1,0:T(8,128)(2,1)S(1)} %collective-permute-done.1.v1, bf16[2064,128]{1,0:T(8,128)(2,1)S(1)} %collective-permute-done.2.u1, bf16[2064,128]{1,0:T(8,128)(2,1)S(1)} %collective-permute-done.3.xv1, ...), custom_call_target="tpu_custom_call" | custom-call | bytes 104857 | tf_op jit(solution)/shard_map/pallas_call | solution.py:253
Async XLA Ops:
  2.3 11.8 %collective-permute-start = (bf16[2064,128]{1,0:T(8,128)(2,1)}, bf16[2064,128]{1,0:T(8,128)(2,1)S(1)}, u32[]{:S(2)}, u32[]{:S(2)}) collective-permute-start(bf16[2064,128]{1,0:T(8,128)(2,1)} %shard_map.28.own), channel_id=1, source_target_pairs={{0,1},{1,0},{2,3},{3,2},{4,5},{5,4},{6,7},{7,6},{8,9},{9,8},{10,11... | collective-permute-start | bytes 1585160 | tf_op jit(solution)/shard_map/ppermute | solution.py:301
  5.6 21.0 %collective-permute-start.2 = (bf16[2064,128]{1,0:T(8,128)(2,1)}, bf16[2064,128]{1,0:T(8,128)(2,1)S(1)}, u32[]{:S(2)}, u32[]{:S(2)}) collective-permute-start(bf16[2064,128]{1,0:T(8,128)(2,1)} %shard_map.28.own), channel_id=1, source_target_pairs={{254,0},{255,1},{0,2},{1,3},{2,4},{3,5},{4,6},{5,7},{6,8},{7,9},{8... | collective-permute-start | bytes 1585160 | tf_op jit(solution)/shard_map/ppermute | solution.py:298
  5.7 22.0 %collective-permute-start.1 = (bf16[2064,128]{1,0:T(8,128)(2,1)}, bf16[2064,128]{1,0:T(8,128)(2,1)S(1)}, u32[]{:S(2)}, u32[]{:S(2)}) collective-permute-start(bf16[2064,128]{1,0:T(8,128)(2,1)} %shard_map.28.own), channel_id=1, source_target_pairs={{2,0},{3,1},{4,2},{5,3},{6,4},{7,5},{8,6},{9,7},{10,8},{11,9},{12,... | collective-permute-start | bytes 1585160 | tf_op jit(solution)/shard_map/ppermute | solution.py:298
  15.9 18.7 %collective-permute-start.5 = (bf16[2064,128]{1,0:T(8,128)(2,1)}, bf16[2064,128]{1,0:T(8,128)(2,1)S(1)}, u32[]{:S(2)}, u32[]{:S(2)}) collective-permute-start(bf16[2064,128]{1,0:T(8,128)(2,1)} %shard_map.28.own), channel_id=1, source_target_pairs={{6,0},{251,1},{8,2},{253,3},{10,4},{255,5},{12,6},{1,7},{14,8},{3,... | collective-permute-start | bytes 1585160 | tf_op jit(solution)/shard_map/ppermute | solution.py:295
  26.6 9.0 %collective-permute-start.4 = (bf16[2064,128]{1,0:T(8,128)(2,1)S(1)}, bf16[2064,128]{1,0:T(8,128)(2,1)S(1)}, u32[]{:S(2)}, u32[]{:S(2)}) collective-permute-start(bf16[2064,128]{1,0:T(8,128)(2,1)S(1)} %collective-permute-done.2.u1), channel_id=1, source_target_pairs={{0,1},{1,0},{2,3},{3,2},{4,5},{5,4},{6,7},{7,6},{8,9},{9,8},{10,11... | collective-permute-start | bytes 1585160 | tf_op jit(solution)/shard_map/ppermute | solution.py:301
  27.6 8.0 %collective-permute-start.3 = (bf16[2064,128]{1,0:T(8,128)(2,1)S(1)}, bf16[2064,128]{1,0:T(8,128)(2,1)S(1)}, u32[]{:S(2)}, u32[]{:S(2)}) collective-permute-start(bf16[2064,128]{1,0:T(8,128)(2,1)S(1)} %collective-permute-done.1.v1), channel_id=1, source_target_pairs={{0,1},{1,0},{2,3},{3,2},{4,5},{5,4},{6,7},{7,6},{8,9},{9,8},{10,11... | collective-permute-start | bytes 1585160 | tf_op jit(solution)/shard_map/ppermute | solution.py:301
  27.6 18.5 %collective-permute-start.6 = (bf16[2064,128]{1,0:T(8,128)(2,1)S(1)}, bf16[2064,128]{1,0:T(8,128)(2,1)S(1)}, u32[]{:S(2)}, u32[]{:S(2)}) collective-permute-start(bf16[2064,128]{1,0:T(8,128)(2,1)S(1)} %collective-permute-done.2.u1), channel_id=1, source_target_pairs={{254,0},{255,1},{0,2},{1,3},{2,4},{3,5},{4,6},{5,7},{6,8},{7,9},{8... | collective-permute-start | bytes 1585160 | tf_op jit(solution)/shard_map/ppermute | solution.py:298
  27.6 18.5 %collective-permute-start.7 = (bf16[2064,128]{1,0:T(8,128)(2,1)S(1)}, bf16[2064,128]{1,0:T(8,128)(2,1)S(1)}, u32[]{:S(2)}, u32[]{:S(2)}) collective-permute-start(bf16[2064,128]{1,0:T(8,128)(2,1)S(1)} %collective-permute-done.1.v1), channel_id=1, source_target_pairs={{2,0},{3,1},{4,2},{5,3},{6,4},{7,5},{8,6},{9,7},{10,8},{11,9},{12,... | collective-permute-start | bytes 1585160 | tf_op jit(solution)/shard_map/ppermute | solution.py:298
  34.5 18.5 %collective-permute-start.10 = (bf16[2064,128]{1,0:T(8,128)(2,1)S(1)}, bf16[2064,128]{1,0:T(8,128)(2,1)S(1)}, u32[]{:S(2)}, u32[]{:S(2)}) collective-permute-start(bf16[2064,128]{1,0:T(8,128)(2,1)S(1)} %collective-permute-done.5.f3), channel_id=1, source_target_pairs={{0,1},{1,0},{2,3},{3,2},{4,5},{5,4},{6,7},{7,6},{8,9},{9,8},{10,11... | collective-permute-start | bytes 1585160 | tf_op jit(solution)/shard_map/ppermute | solution.py:301
  39.3 13.4 %collective-permute-start.11 = (bf16[2064,128]{1,0:T(8,128)(2,1)}, bf16[2064,128]{1,0:T(8,128)(2,1)S(1)}, u32[]{:S(2)}, u32[]{:S(2)}) collective-permute-start(bf16[2064,128]{1,0:T(8,128)(2,1)} %shard_map.28.own), channel_id=1, source_target_pairs={{250,0},{7,1},{252,2},{9,3},{254,4},{11,5},{0,6},{13,7},{2,8},{15,... | collective-permute-start | bytes 1585160 | tf_op jit(solution)/shard_map/ppermute | solution.py:295
  46.1 6.9 %collective-permute-start.8 = (bf16[2064,128]{1,0:T(8,128)(2,1)S(1)}, bf16[2064,128]{1,0:T(8,128)(2,1)S(1)}, u32[]{:S(2)}, u32[]{:S(2)}) collective-permute-start(bf16[2064,128]{1,0:T(8,128)(2,1)S(1)} %collective-permute-done.7.v2), channel_id=1, source_target_pairs={{0,1},{1,0},{2,3},{3,2},{4,5},{5,4},{6,7},{7,6},{8,9},{9,8},{10,11... | collective-permute-start | bytes 1585160 | tf_op jit(solution)/shard_map/ppermute | solution.py:301
  48.0 5.0 %collective-permute-start.9 = (bf16[2064,128]{1,0:T(8,128)(2,1)S(1)}, bf16[2064,128]{1,0:T(8,128)(2,1)S(1)}, u32[]{:S(2)}, u32[]{:S(2)}) collective-permute-start(bf16[2064,128]{1,0:T(8,128)(2,1)S(1)} %collective-permute-done.6.u2), channel_id=1, source_target_pairs={{0,1},{1,0},{2,3},{3,2},{4,5},{5,4},{6,7},{7,6},{8,9},{9,8},{10,11... | collective-permute-start | bytes 1585160 | tf_op jit(solution)/shard_map/ppermute | solution.py:301

commit v5 on v4

--- a/solution.py
+++ b/solution.py
@@ -85,7 +85,7 @@
             pltpu.SemaphoreType.DMA((2, 5)),
             pltpu.SemaphoreType.DMA((5,)),
         ],
-        compiler_params=pltpu.CompilerParams(vmem_limit_bytes=56 * MIB),
+        compiler_params=pltpu.CompilerParams(vmem_limit_bytes=53 * MIB),
         cost_estimate=pl.CostEstimate(flops=R * 5 * R * 4, bytes_accessed=R * 5 * R * 6 + ROWS * 256, transcendentals=0),
     )(adjacency, weight)
 
@@ -226,23 +226,27 @@
             leave(at * sign, sum_ref)
         third = {-3 * sign: rows[-3 * sign]}
         lefts = {5 * sign: columns_of(cube_ref, 5 * sign, 6)}
-        for at in range(-5, 0):
-            value = columns_of(rest_ref, at, 5)[...]
-            value = value + band_dot({-3 * sign: columns_of(left_ref, -3 * sign, 4)}, third, at * sign)
-            columns_of(late_ref, at, 5)[...] = (value * LAST_SCALE).astype(jnp.bfloat16)
-            lefts[at * sign] = columns_of(late_ref, at, 5)
-        ready = {place: rows[place] for place in lefts}
-        for at in (3, 4, 5, 6, 7, 1, 0, -1, -2, -3, -4, -5, -6, -7, -8):
+
+        def finish(at):
+            value = jnp.zeros((R, R), jnp.float32)
             if at > -8:
-                value = band_dot(lefts, ready, at * sign)
-            else:
-                value = jnp.zeros((R, R), jnp.float32)
+                value = band_dot(lefts, {place: rows[place] for place in lefts}, at * sign)
             if at <= -4:
                 value = value + columns_of(edge_ref, at * sign + 6 * sign, 2)[...]
             if at >= -2:
                 value = value + columns_of(sum_ref, at * sign, 8)[...]
             columns_of(result_ref, at * sign, 8)[...] = value
             leave(at * sign, result_ref)
+
+        for at in (3, 4, 5, 6, 7):
+            finish(at)
+        for at in range(-5, 0):
+            value = columns_of(rest_ref, at, 5)[...]
+            value = value + band_dot({-3 * sign: columns_of(left_ref, -3 * sign, 4)}, third, at * sign)
+            columns_of(late_ref, at, 5)[...] = (value * LAST_SCALE).astype(jnp.bfloat16)
+            lefts[at * sign] = columns_of(late_ref, at, 5)
+        for at in (1, 0, -1, -2, -3, -4, -5, -6, -7, -8):
+            finish(at)
         for copy in copies:
             copy.wait()
 

time: 56.1 us -> 55.5 us (0.989)
  Pallas kernels: 13.5 us -> 10.3 us
  waiting for transfers between devices: 16.1 us -> 18.8 us
    pallas_call x4, Pallas kernels: 8.51 us -> 5.43 us  [call(): pl.pallas_call(kernel, in_specs=specs, out_specs=[pl.BlockSpec(memory_spa...]
    ppermute x4, waiting for transfers between devices: 14.2 us -> 16 us  [shifted(): lax.ppermute(value, 'blk', [((target + steps) % size, target) for target...]
    ppermute x2, waiting for transfers between devices: 1.93 us -> 2.72 us  [hop(): return lax.ppermute(value, 'blk', pairs)]
  transfers between devices with their start and end apart: 12 -> 12, of which waited for: 3 -> 3; matrix products, arithmetic and copies ran while one was open for 0% -> 0% of each run, Pallas kernels for 15% -> 10%
where the time goes in v5:
time: 55.5 us; the launch traced here: 55.4 us
  starting transfers between devices  26 us (47%)
  waiting for transfers between devices  18.8 us (34%)
  Pallas kernels  10.3 us (19%)
    ppermute x4, waiting for transfers between devices, shifted(): lax.ppermute(value, 'blk', [((target + steps) % size, target) for target...  16 us
    ppermute x4, starting transfers between devices, shifted(): lax.ppermute(value, 'blk', [((target + steps) % size, target) for target...  15.4 us
    ppermute x6, starting transfers between devices, peer(): lax.ppermute(value, 'blk', [(source, source ^ 1) for source in range(size)])  7.27 us
    pallas_call x4, Pallas kernels, call(): pl.pallas_call(kernel, in_specs=specs, out_specs=[pl.BlockSpec(memory_spa...  5.43 us
    ppermute x2, starting transfers between devices, hop(): return lax.ppermute(value, 'blk', pairs)  3.37 us
    pallas_call x1, Pallas kernels, last_call(): pl.pallas_call(last_kernel, in_specs=[pl.BlockSpec(memory_space=pltpu.SME...  2.79 us
    ppermute x2, waiting for transfers between devices, hop(): return lax.ppermute(value, 'blk', pairs)  2.72 us
    pallas_call x1, Pallas kernels, pack(): pl.pallas_call(pack_kernel, in_specs=[hbm, hbm], out_specs=hbm, out_shape...  2.13 us
  transfers between devices with their start and end apart: 12, of which 3 were waited for; matrix products, arithmetic and copies ran while one was open for 0% of the time, Pallas kernels for 10%

profile of v5, /device:TPU:1, one launch (start us, length us, event | category | flops | bytes accessed | tf_op | source)
XLA Modules:
  0.0 55.4 jit_solution(18162647769279551634)
XLA Ops:
  0.0 2.1 %shard_map.28.own = bf16[2064,128]{1,0:T(8,128)(2,1)S(1)} custom-call(s32[256,1280]{1,0:T(8,128)} %adjacency_hbm.1, bf16[256,1280]{1,0:T(8,128)(2,1)} %weight_hbm.1), custom_call_target="tpu_custom_call" | custom-call | flops 1310720 | bytes 2494464 | tf_op jit(solution)/shard_map/pallas_call | solution.py:76
  2.1 3.3 %collective-permute-start = (bf16[2064,128]{1,0:T(8,128)(2,1)S(1)}, bf16[2064,128]{1,0:T(8,128)(2,1)S(1)}, u32[]{:S(2)}, u32[]{:S(2)}) collective-permute-start(bf16[2064,128]{1,0:T(8,128)(2,1)S(1)} %shard_map.28.own), channel_id=1, source_target_pairs={{0,1},{1,0},{2,3},{3,2},{4,5},{5,4},{6,7},{7,6},{8,9},{9,8},{10,11... | collective-permute-start | bytes 1585160 | tf_op jit(solution)/shard_map/ppermute | solution.py:305
  5.5 0.0 collective-permute-start.2
  5.5 8.5 %collective-permute-start.1 = (bf16[2064,128]{1,0:T(8,128)(2,1)S(1)}, bf16[2064,128]{1,0:T(8,128)(2,1)S(1)}, u32[]{:S(2)}, u32[]{:S(2)}) collective-permute-start(bf16[2064,128]{1,0:T(8,128)(2,1)S(1)} %shard_map.28.own), channel_id=1, source_target_pairs={{2,0},{3,1},{4,2},{5,3},{6,4},{7,5},{8,6},{9,7},{10,8},{11,9},{12,... | collective-permute-start | bytes 1585160 | tf_op jit(solution)/shard_map/ppermute | solution.py:302
  14.0 0.0 collective-permute-done.p0
  14.0 0.7 %shard_map.29 = (bf16[256,1280]{1,0:T(8,128)(2,1)S(1)}, f32[256,2304]{1,0:T(8,128)S(1)}) custom-call(s32[1]{0:T(128)} %bitcast.sign_ref, bf16[2064,128]{1,0:T(8,128)(2,1)S(1)} %shard_map.28.own, bf16[2064,128]{1,0:T(8,128)(2,1)S(1)} %collective-permute-done.p0), custom_call_target="tpu_custom_call" | custom-call | bytes 104857 | tf_op jit(solution)/shard_map/pallas_call | solution.py:278
  14.6 0.1 collective-permute-start.5
  14.7 11.5 %collective-permute-done.2.u1 = bf16[2064,128]{1,0:T(8,128)(2,1)S(1)} collective-permute-done((bf16[2064,128]{1,0:T(8,128)(2,1)S(1)}, bf16[2064,128]{1,0:T(8,128)(2,1)S(1)}, u32[]{:S(2)}, u32[]{:S(2)}) %collective-permute-start.2) | collective-permute-done | bytes 528416 | tf_op jit(solution)/shard_map/ppermute | solution.py:302
  26.2 1.0 %collective-permute-start.4 = (bf16[2064,128]{1,0:T(8,128)(2,1)S(1)}, bf16[2064,128]{1,0:T(8,128)(2,1)S(1)}, u32[]{:S(2)}, u32[]{:S(2)}) collective-permute-start(bf16[2064,128]{1,0:T(8,128)(2,1)S(1)} %collective-permute-done.2.u1), channel_id=1, source_target_pairs={{0,1},{1,0},{2,3},{3,2},{4,5},{5,4},{6,7},{7,6},{8,9},{9,8},{10,11... | collective-permute-start | bytes 1585160 | tf_op jit(solution)/shard_map/ppermute | solution.py:305
  27.2 0.0 collective-permute-done.1.v1
  27.2 0.0 collective-permute-start.3
  27.2 0.0 collective-permute-start.6
  27.2 6.9 %collective-permute-start.7 = (bf16[2064,128]{1,0:T(8,128)(2,1)S(1)}, bf16[2064,128]{1,0:T(8,128)(2,1)S(1)}, u32[]{:S(2)}, u32[]{:S(2)}) collective-permute-start(bf16[2064,128]{1,0:T(8,128)(2,1)S(1)} %collective-permute-done.1.v1), channel_id=1, source_target_pairs={{2,0},{3,1},{4,2},{5,3},{6,4},{7,5},{8,6},{9,7},{10,8},{11,9},{12,... | collective-permute-start | bytes 1585160 | tf_op jit(solution)/shard_map/ppermute | solution.py:302
  34.1 0.0 collective-permute-done.5.f3
  34.2 1.1 %collective-permute-start.10 = (bf16[2064,128]{1,0:T(8,128)(2,1)S(1)}, bf16[2064,128]{1,0:T(8,128)(2,1)S(1)}, u32[]{:S(2)}, u32[]{:S(2)}) collective-permute-start(bf16[2064,128]{1,0:T(8,128)(2,1)S(1)} %collective-permute-done.5.f3), channel_id=1, source_target_pairs={{0,1},{1,0},{2,3},{3,2},{4,5},{5,4},{6,7},{7,6},{8,9},{9,8},{10,11... | collective-permute-start | bytes 1585160 | tf_op jit(solution)/shard_map/ppermute | solution.py:305
  35.2 0.0 collective-permute-done.4.xu1
  35.2 0.0 collective-permute-done.3.xv1
  35.2 2.7 %shard_map.30 = (bf16[256,2304]{1,0:T(8,128)(2,1)S(1)}, f32[256,3328]{1,0:T(8,128)S(1)}) custom-call(s32[1]{0:T(128)} %bitcast.sign_ref, bf16[256,1280]{1,0:T(8,128)(2,1)S(1)} %get-tuple-element.21.left_ref, bf16[2064,128]{1,0:T(8,128)(2,1)S(1)} %shard_map.28.own, bf16[2064,128]{1,0:T(8,128)(2,1)S(1)} %collective-permute-done.p0, ...), custom_call_target="tpu_custom_call" | custom-call | bytes 104857 | tf_op jit(solution)/shard_map/pallas_call | solution.py:278
  37.9 3.3 %collective-permute-start.11 = (bf16[2064,128]{1,0:T(8,128)(2,1)S(1)}, bf16[2064,128]{1,0:T(8,128)(2,1)S(1)}, u32[]{:S(2)}, u32[]{:S(2)}) collective-permute-start(bf16[2064,128]{1,0:T(8,128)(2,1)S(1)} %shard_map.28.own), channel_id=1, source_target_pairs={{250,0},{7,1},{252,2},{9,3},{254,4},{11,5},{0,6},{13,7},{2,8},{15,... | collective-permute-start | bytes 1585160 | tf_op jit(solution)/shard_map/ppermute | solution.py:299
  41.2 4.5 %collective-permute-done.6.u2 = bf16[2064,128]{1,0:T(8,128)(2,1)S(1)} collective-permute-done((bf16[2064,128]{1,0:T(8,128)(2,1)S(1)}, bf16[2064,128]{1,0:T(8,128)(2,1)S(1)}, u32[]{:S(2)}, u32[]{:S(2)}) %collective-permute-start.6) | collective-permute-done | bytes 528416 | tf_op jit(solution)/shard_map/ppermute | solution.py:302
  45.7 0.0 collective-permute-done.7.v2
  45.7 1.9 %collective-permute-start.8 = (bf16[2064,128]{1,0:T(8,128)(2,1)S(1)}, bf16[2064,128]{1,0:T(8,128)(2,1)S(1)}, u32[]{:S(2)}, u32[]{:S(2)}) collective-permute-start(bf16[2064,128]{1,0:T(8,128)(2,1)S(1)} %collective-permute-done.7.v2), channel_id=1, source_target_pairs={{0,1},{1,0},{2,3},{3,2},{4,5},{5,4},{6,7},{7,6},{8,9},{9,8},{10,11... | collective-permute-start | bytes 1585160 | tf_op jit(solution)/shard_map/ppermute | solution.py:305
  47.6 0.0 collective-permute-start.9
  47.6 1.7 %shard_map.31 = (bf16[256,3328]{1,0:T(8,128)(2,1)S(1)}, f32[256,1280]{1,0:T(8,128)S(1)}, f32[256,4352]{1,0:T(8,128)S(1)}) custom-call(s32[1]{0:T(128)} %bitcast.sign_ref, bf16[256,2304]{1,0:T(8,128)(2,1)S(1)} %get-tuple-element.26.left_ref, bf16[2064,128]{1,0:T(8,128)(2,1)S(1)} %shard_map.28.own, bf16[2064,128]{1,0:T(8,128)(2,1)S(1)} %collective-permute-done.p0, ...), custom_call_target="tpu_custom_call" | custom-call | bytes 104857 | tf_op jit(solution)/shard_map/pallas_call | solution.py:278
  49.3 2.7 %collective-permute-done.11.b3 = bf16[2064,128]{1,0:T(8,128)(2,1)S(1)} collective-permute-done((bf16[2064,128]{1,0:T(8,128)(2,1)S(1)}, bf16[2064,128]{1,0:T(8,128)(2,1)S(1)}, u32[]{:S(2)}, u32[]{:S(2)}) %collective-permute-start.11) | collective-permute-done | bytes 528416 | tf_op jit(solution)/shard_map/ppermute | solution.py:299
  52.1 0.3 shard_map.32.edge_ref
  52.4 0.0 collective-permute-done.10.xf3
  52.4 0.0 collective-permute-done.8.xv2
  52.4 0.0 collective-permute-done.9.xu2
  52.4 2.8 %shard_map.33 = f32[256,4352]{1,0:T(8,128)} custom-call(s32[1]{0:T(128)} %bitcast.sign_ref, bf16[256,2304]{1,0:T(8,128)(2,1)S(1)} %get-tuple-element.26.left_ref, bf16[2064,128]{1,0:T(8,128)(2,1)S(1)} %collective-permute-done.1.v1, bf16[2064,128]{1,0:T(8,128)(2,1)S(1)} %collective-permute-done.2.u1, bf16[2064,128]{1,0:T(8,128)(2,1)S(1)} %collective-permute-done.3.xv1, ...), custom_call_target="tpu_custom_call" | custom-call | bytes 104857 | tf_op jit(solution)/shard_map/pallas_call | solution.py:257
Async XLA Ops:
  2.1 11.8 %collective-permute-start = (bf16[2064,128]{1,0:T(8,128)(2,1)S(1)}, bf16[2064,128]{1,0:T(8,128)(2,1)S(1)}, u32[]{:S(2)}, u32[]{:S(2)}) collective-permute-start(bf16[2064,128]{1,0:T(8,128)(2,1)S(1)} %shard_map.28.own), channel_id=1, source_target_pairs={{0,1},{1,0},{2,3},{3,2},{4,5},{5,4},{6,7},{7,6},{8,9},{9,8},{10,11... | collective-permute-start | bytes 1585160 | tf_op jit(solution)/shard_map/ppermute | solution.py:305
  5.5 20.8 %collective-permute-start.2 = (bf16[2064,128]{1,0:T(8,128)(2,1)S(1)}, bf16[2064,128]{1,0:T(8,128)(2,1)S(1)}, u32[]{:S(2)}, u32[]{:S(2)}) collective-permute-start(bf16[2064,128]{1,0:T(8,128)(2,1)S(1)} %shard_map.28.own), channel_id=1, source_target_pairs={{254,0},{255,1},{0,2},{1,3},{2,4},{3,5},{4,6},{5,7},{6,8},{7,9},{8... | collective-permute-start | bytes 1585160 | tf_op jit(solution)/shard_map/ppermute | solution.py:302
  5.5 21.8 %collective-permute-start.1 = (bf16[2064,128]{1,0:T(8,128)(2,1)S(1)}, bf16[2064,128]{1,0:T(8,128)(2,1)S(1)}, u32[]{:S(2)}, u32[]{:S(2)}) collective-permute-start(bf16[2064,128]{1,0:T(8,128)(2,1)S(1)} %shard_map.28.own), channel_id=1, source_target_pairs={{2,0},{3,1},{4,2},{5,3},{6,4},{7,5},{8,6},{9,7},{10,8},{11,9},{12,... | collective-permute-start | bytes 1585160 | tf_op jit(solution)/shard_map/ppermute | solution.py:302
  14.6 19.5 %collective-permute-start.5 = (bf16[2064,128]{1,0:T(8,128)(2,1)S(1)}, bf16[2064,128]{1,0:T(8,128)(2,1)S(1)}, u32[]{:S(2)}, u32[]{:S(2)}) collective-permute-start(bf16[2064,128]{1,0:T(8,128)(2,1)S(1)} %shard_map.28.own), channel_id=1, source_target_pairs={{6,0},{251,1},{8,2},{253,3},{10,4},{255,5},{12,6},{1,7},{14,8},{3,... | collective-permute-start | bytes 1585160 | tf_op jit(solution)/shard_map/ppermute | solution.py:299
  26.2 9.0 %collective-permute-start.4 = (bf16[2064,128]{1,0:T(8,128)(2,1)S(1)}, bf16[2064,128]{1,0:T(8,128)(2,1)S(1)}, u32[]{:S(2)}, u32[]{:S(2)}) collective-permute-start(bf16[2064,128]{1,0:T(8,128)(2,1)S(1)} %collective-permute-done.2.u1), channel_id=1, source_target_pairs={{0,1},{1,0},{2,3},{3,2},{4,5},{5,4},{6,7},{7,6},{8,9},{9,8},{10,11... | collective-permute-start | bytes 1585160 | tf_op jit(solution)/shard_map/ppermute | solution.py:305
  27.2 8.0 %collective-permute-start.3 = (bf16[2064,128]{1,0:T(8,128)(2,1)S(1)}, bf16[2064,128]{1,0:T(8,128)(2,1)S(1)}, u32[]{:S(2)}, u32[]{:S(2)}) collective-permute-start(bf16[2064,128]{1,0:T(8,128)(2,1)S(1)} %collective-permute-done.1.v1), channel_id=1, source_target_pairs={{0,1},{1,0},{2,3},{3,2},{4,5},{5,4},{6,7},{7,6},{8,9},{9,8},{10,11... | collective-permute-start | bytes 1585160 | tf_op jit(solution)/shard_map/ppermute | solution.py:305
  27.2 18.5 %collective-permute-start.6 = (bf16[2064,128]{1,0:T(8,128)(2,1)S(1)}, bf16[2064,128]{1,0:T(8,128)(2,1)S(1)}, u32[]{:S(2)}, u32[]{:S(2)}) collective-permute-start(bf16[2064,128]{1,0:T(8,128)(2,1)S(1)} %collective-permute-done.2.u1), channel_id=1, source_target_pairs={{254,0},{255,1},{0,2},{1,3},{2,4},{3,5},{4,6},{5,7},{6,8},{7,9},{8... | collective-permute-start | bytes 1585160 | tf_op jit(solution)/shard_map/ppermute | solution.py:302
  27.2 18.5 %collective-permute-start.7 = (bf16[2064,128]{1,0:T(8,128)(2,1)S(1)}, bf16[2064,128]{1,0:T(8,128)(2,1)S(1)}, u32[]{:S(2)}, u32[]{:S(2)}) collective-permute-start(bf16[2064,128]{1,0:T(8,128)(2,1)S(1)} %collective-permute-done.1.v1), channel_id=1, source_target_pairs={{2,0},{3,1},{4,2},{5,3},{6,4},{7,5},{8,6},{9,7},{10,8},{11,9},{12,... | collective-permute-start | bytes 1585160 | tf_op jit(solution)/shard_map/ppermute | solution.py:302
  34.2 18.3 %collective-permute-start.10 = (bf16[2064,128]{1,0:T(8,128)(2,1)S(1)}, bf16[2064,128]{1,0:T(8,128)(2,1)S(1)}, u32[]{:S(2)}, u32[]{:S(2)}) collective-permute-start(bf16[2064,128]{1,0:T(8,128)(2,1)S(1)} %collective-permute-done.5.f3), channel_id=1, source_target_pairs={{0,1},{1,0},{2,3},{3,2},{4,5},{5,4},{6,7},{7,6},{8,9},{9,8},{10,11... | collective-permute-start | bytes 1585160 | tf_op jit(solution)/shard_map/ppermute | solution.py:305
  37.9 14.1 %collective-permute-start.11 = (bf16[2064,128]{1,0:T(8,128)(2,1)S(1)}, bf16[2064,128]{1,0:T(8,128)(2,1)S(1)}, u32[]{:S(2)}, u32[]{:S(2)}) collective-permute-start(bf16[2064,128]{1,0:T(8,128)(2,1)S(1)} %shard_map.28.own), channel_id=1, source_target_pairs={{250,0},{7,1},{252,2},{9,3},{254,4},{11,5},{0,6},{13,7},{2,8},{15,... | collective-permute-start | bytes 1585160 | tf_op jit(solution)/shard_map/ppermute | solution.py:299
  45.7 6.7 %collective-permute-start.8 = (bf16[2064,128]{1,0:T(8,128)(2,1)S(1)}, bf16[2064,128]{1,0:T(8,128)(2,1)S(1)}, u32[]{:S(2)}, u32[]{:S(2)}) collective-permute-start(bf16[2064,128]{1,0:T(8,128)(2,1)S(1)} %collective-permute-done.7.v2), channel_id=1, source_target_pairs={{0,1},{1,0},{2,3},{3,2},{4,5},{5,4},{6,7},{7,6},{8,9},{9,8},{10,11... | collective-permute-start | bytes 1585160 | tf_op jit(solution)/shard_map/ppermute | solution.py:305
  47.6 4.8 %collective-permute-start.9 = (bf16[2064,128]{1,0:T(8,128)(2,1)S(1)}, bf16[2064,128]{1,0:T(8,128)(2,1)S(1)}, u32[]{:S(2)}, u32[]{:S(2)}) collective-permute-start(bf16[2064,128]{1,0:T(8,128)(2,1)S(1)} %collective-permute-done.6.u2), channel_id=1, source_target_pairs={{0,1},{1,0},{2,3},{3,2},{4,5},{5,4},{6,7},{7,6},{8,9},{9,8},{10,11... | collective-permute-start | bytes 1585160 | tf_op jit(solution)/shard_map/ppermute | solution.py:305

commit v6 on v5

--- a/solution.py
+++ b/solution.py
@@ -216,21 +216,20 @@
         rows[-5 * sign] = xf3
         copies = []
 
-        def leave(at, ref):
+        def leave(at, ref, moved=0, span=8):
             place = columns_of(out_hbm, at, 8)
-            copy = pltpu.make_async_copy(columns_of(ref, at, 8), place, semaphores.at[at + 8])
+            copy = pltpu.make_async_copy(columns_of(ref, at + moved, span), place, semaphores.at[at + 8])
             copy.start()
             copies.append(copy)
 
         for at in (2, 8):
             leave(at * sign, sum_ref)
+        leave(-8 * sign, edge_ref, 6 * sign, 2)
         third = {-3 * sign: rows[-3 * sign]}
         lefts = {5 * sign: columns_of(cube_ref, 5 * sign, 6)}
 
         def finish(at):
-            value = jnp.zeros((R, R), jnp.float32)
-            if at > -8:
-                value = band_dot(lefts, {place: rows[place] for place in lefts}, at * sign)
+            value = band_dot(lefts, {place: rows[place] for place in lefts}, at * sign)
             if at <= -4:
                 value = value + columns_of(edge_ref, at * sign + 6 * sign, 2)[...]
             if at >= -2:
@@ -245,7 +244,7 @@
             value = value + band_dot({-3 * sign: columns_of(left_ref, -3 * sign, 4)}, third, at * sign)
             columns_of(late_ref, at, 5)[...] = (value * LAST_SCALE).astype(jnp.bfloat16)
             lefts[at * sign] = columns_of(late_ref, at, 5)
-        for at in (1, 0, -1, -2, -3, -4, -5, -6, -7, -8):
+        for at in (1, 0, -1, -2, -3, -4, -5, -6, -7):
             finish(at)
         for copy in copies:
             copy.wait()

time: 55.5 us -> 55.4 us (level)
  no operation moved by 1% of the time
where the time goes in v6:
time: 55.4 us; the launch traced here: 55.3 us
  starting transfers between devices  26 us (47%)
  waiting for transfers between devices  18.8 us (34%)
  Pallas kernels  10.3 us (19%)
    ppermute x4, waiting for transfers between devices, shifted(): lax.ppermute(value, 'blk', [((target + steps) % size, target) for target...  16 us
    ppermute x4, starting transfers between devices, shifted(): lax.ppermute(value, 'blk', [((target + steps) % size, target) for target...  15.4 us
    ppermute x6, starting transfers between devices, peer(): lax.ppermute(value, 'blk', [(source, source ^ 1) for source in range(size)])  7.27 us
    pallas_call x4, Pallas kernels, call(): pl.pallas_call(kernel, in_specs=specs, out_specs=[pl.BlockSpec(memory_spa...  5.43 us
    ppermute x2, starting transfers between devices, hop(): return lax.ppermute(value, 'blk', pairs)  3.37 us
    ppermute x2, waiting for transfers between devices, hop(): return lax.ppermute(value, 'blk', pairs)  2.72 us
    pallas_call x1, Pallas kernels, last_call(): pl.pallas_call(last_kernel, in_specs=[pl.BlockSpec(memory_space=pltpu.SME...  2.71 us
    pallas_call x1, Pallas kernels, pack(): pl.pallas_call(pack_kernel, in_specs=[hbm, hbm], out_specs=hbm, out_shape...  2.13 us
  transfers between devices with their start and end apart: 12, of which 3 were waited for; matrix products, arithmetic and copies ran while one was open for 0% of the time, Pallas kernels for 10%

profile of v6, /device:TPU:1, one launch (start us, length us, event | category | flops | bytes accessed | tf_op | source)
XLA Modules:
  0.0 55.3 jit_solution(3249352914855122941)
XLA Ops:
  0.0 2.1 %shard_map.28.own = bf16[2064,128]{1,0:T(8,128)(2,1)S(1)} custom-call(s32[256,1280]{1,0:T(8,128)} %adjacency_hbm.1, bf16[256,1280]{1,0:T(8,128)(2,1)} %weight_hbm.1), custom_call_target="tpu_custom_call" | custom-call | flops 1310720 | bytes 2494464 | tf_op jit(solution)/shard_map/pallas_call | solution.py:76
  2.1 3.3 %collective-permute-start = (bf16[2064,128]{1,0:T(8,128)(2,1)S(1)}, bf16[2064,128]{1,0:T(8,128)(2,1)S(1)}, u32[]{:S(2)}, u32[]{:S(2)}) collective-permute-start(bf16[2064,128]{1,0:T(8,128)(2,1)S(1)} %shard_map.28.own), channel_id=1, source_target_pairs={{0,1},{1,0},{2,3},{3,2},{4,5},{5,4},{6,7},{7,6},{8,9},{9,8},{10,11... | collective-permute-start | bytes 1585160 | tf_op jit(solution)/shard_map/ppermute | solution.py:304
  5.5 0.0 collective-permute-start.2
  5.5 8.5 %collective-permute-start.1 = (bf16[2064,128]{1,0:T(8,128)(2,1)S(1)}, bf16[2064,128]{1,0:T(8,128)(2,1)S(1)}, u32[]{:S(2)}, u32[]{:S(2)}) collective-permute-start(bf16[2064,128]{1,0:T(8,128)(2,1)S(1)} %shard_map.28.own), channel_id=1, source_target_pairs={{2,0},{3,1},{4,2},{5,3},{6,4},{7,5},{8,6},{9,7},{10,8},{11,9},{12,... | collective-permute-start | bytes 1585160 | tf_op jit(solution)/shard_map/ppermute | solution.py:301
  14.0 0.0 collective-permute-done.p0
  14.0 0.7 %shard_map.29 = (bf16[256,1280]{1,0:T(8,128)(2,1)S(1)}, f32[256,2304]{1,0:T(8,128)S(1)}) custom-call(s32[1]{0:T(128)} %bitcast.sign_ref, bf16[2064,128]{1,0:T(8,128)(2,1)S(1)} %shard_map.28.own, bf16[2064,128]{1,0:T(8,128)(2,1)S(1)} %collective-permute-done.p0), custom_call_target="tpu_custom_call" | custom-call | bytes 104857 | tf_op jit(solution)/shard_map/pallas_call | solution.py:277
  14.6 0.1 collective-permute-start.5
  14.7 11.5 %collective-permute-done.2.u1 = bf16[2064,128]{1,0:T(8,128)(2,1)S(1)} collective-permute-done((bf16[2064,128]{1,0:T(8,128)(2,1)S(1)}, bf16[2064,128]{1,0:T(8,128)(2,1)S(1)}, u32[]{:S(2)}, u32[]{:S(2)}) %collective-permute-start.2) | collective-permute-done | bytes 528416 | tf_op jit(solution)/shard_map/ppermute | solution.py:301
  26.2 1.0 %collective-permute-start.4 = (bf16[2064,128]{1,0:T(8,128)(2,1)S(1)}, bf16[2064,128]{1,0:T(8,128)(2,1)S(1)}, u32[]{:S(2)}, u32[]{:S(2)}) collective-permute-start(bf16[2064,128]{1,0:T(8,128)(2,1)S(1)} %collective-permute-done.2.u1), channel_id=1, source_target_pairs={{0,1},{1,0},{2,3},{3,2},{4,5},{5,4},{6,7},{7,6},{8,9},{9,8},{10,11... | collective-permute-start | bytes 1585160 | tf_op jit(solution)/shard_map/ppermute | solution.py:304
  27.2 0.0 collective-permute-done.1.v1
  27.2 0.0 collective-permute-start.3
  27.2 0.0 collective-permute-start.6
  27.2 6.9 %collective-permute-start.7 = (bf16[2064,128]{1,0:T(8,128)(2,1)S(1)}, bf16[2064,128]{1,0:T(8,128)(2,1)S(1)}, u32[]{:S(2)}, u32[]{:S(2)}) collective-permute-start(bf16[2064,128]{1,0:T(8,128)(2,1)S(1)} %collective-permute-done.1.v1), channel_id=1, source_target_pairs={{2,0},{3,1},{4,2},{5,3},{6,4},{7,5},{8,6},{9,7},{10,8},{11,9},{12,... | collective-permute-start | bytes 1585160 | tf_op jit(solution)/shard_map/ppermute | solution.py:301
  34.1 0.0 collective-permute-done.5.f3
  34.2 1.1 %collective-permute-start.10 = (bf16[2064,128]{1,0:T(8,128)(2,1)S(1)}, bf16[2064,128]{1,0:T(8,128)(2,1)S(1)}, u32[]{:S(2)}, u32[]{:S(2)}) collective-permute-start(bf16[2064,128]{1,0:T(8,128)(2,1)S(1)} %collective-permute-done.5.f3), channel_id=1, source_target_pairs={{0,1},{1,0},{2,3},{3,2},{4,5},{5,4},{6,7},{7,6},{8,9},{9,8},{10,11... | collective-permute-start | bytes 1585160 | tf_op jit(solution)/shard_map/ppermute | solution.py:304
  35.2 0.0 collective-permute-done.4.xu1
  35.2 0.0 collective-permute-done.3.xv1
  35.2 2.7 %shard_map.30 = (bf16[256,2304]{1,0:T(8,128)(2,1)S(1)}, f32[256,3328]{1,0:T(8,128)S(1)}) custom-call(s32[1]{0:T(128)} %bitcast.sign_ref, bf16[256,1280]{1,0:T(8,128)(2,1)S(1)} %get-tuple-element.21.left_ref, bf16[2064,128]{1,0:T(8,128)(2,1)S(1)} %shard_map.28.own, bf16[2064,128]{1,0:T(8,128)(2,1)S(1)} %collective-permute-done.p0, ...), custom_call_target="tpu_custom_call" | custom-call | bytes 104857 | tf_op jit(solution)/shard_map/pallas_call | solution.py:277
  37.9 3.3 %collective-permute-start.11 = (bf16[2064,128]{1,0:T(8,128)(2,1)S(1)}, bf16[2064,128]{1,0:T(8,128)(2,1)S(1)}, u32[]{:S(2)}, u32[]{:S(2)}) collective-permute-start(bf16[2064,128]{1,0:T(8,128)(2,1)S(1)} %shard_map.28.own), channel_id=1, source_target_pairs={{250,0},{7,1},{252,2},{9,3},{254,4},{11,5},{0,6},{13,7},{2,8},{15,... | collective-permute-start | bytes 1585160 | tf_op jit(solution)/shard_map/ppermute | solution.py:298
  41.2 4.5 %collective-permute-done.6.u2 = bf16[2064,128]{1,0:T(8,128)(2,1)S(1)} collective-permute-done((bf16[2064,128]{1,0:T(8,128)(2,1)S(1)}, bf16[2064,128]{1,0:T(8,128)(2,1)S(1)}, u32[]{:S(2)}, u32[]{:S(2)}) %collective-permute-start.6) | collective-permute-done | bytes 528416 | tf_op jit(solution)/shard_map/ppermute | solution.py:301
  45.7 0.0 collective-permute-done.7.v2
  45.7 1.9 %collective-permute-start.8 = (bf16[2064,128]{1,0:T(8,128)(2,1)S(1)}, bf16[2064,128]{1,0:T(8,128)(2,1)S(1)}, u32[]{:S(2)}, u32[]{:S(2)}) collective-permute-start(bf16[2064,128]{1,0:T(8,128)(2,1)S(1)} %collective-permute-done.7.v2), channel_id=1, source_target_pairs={{0,1},{1,0},{2,3},{3,2},{4,5},{5,4},{6,7},{7,6},{8,9},{9,8},{10,11... | collective-permute-start | bytes 1585160 | tf_op jit(solution)/shard_map/ppermute | solution.py:304
  47.6 0.0 collective-permute-start.9
  47.6 1.7 %shard_map.31 = (bf16[256,3328]{1,0:T(8,128)(2,1)S(1)}, f32[256,1280]{1,0:T(8,128)S(1)}, f32[256,4352]{1,0:T(8,128)S(1)}) custom-call(s32[1]{0:T(128)} %bitcast.sign_ref, bf16[256,2304]{1,0:T(8,128)(2,1)S(1)} %get-tuple-element.26.left_ref, bf16[2064,128]{1,0:T(8,128)(2,1)S(1)} %shard_map.28.own, bf16[2064,128]{1,0:T(8,128)(2,1)S(1)} %collective-permute-done.p0, ...), custom_call_target="tpu_custom_call" | custom-call | bytes 104857 | tf_op jit(solution)/shard_map/pallas_call | solution.py:277
  49.3 2.7 %collective-permute-done.11.b3 = bf16[2064,128]{1,0:T(8,128)(2,1)S(1)} collective-permute-done((bf16[2064,128]{1,0:T(8,128)(2,1)S(1)}, bf16[2064,128]{1,0:T(8,128)(2,1)S(1)}, u32[]{:S(2)}, u32[]{:S(2)}) %collective-permute-start.11) | collective-permute-done | bytes 528416 | tf_op jit(solution)/shard_map/ppermute | solution.py:298
  52.1 0.3 shard_map.32.edge_ref
  52.4 0.0 collective-permute-done.10.xf3
  52.4 0.0 collective-permute-done.8.xv2
  52.4 0.0 collective-permute-done.9.xu2
  52.4 2.7 %shard_map.33 = f32[256,4352]{1,0:T(8,128)} custom-call(s32[1]{0:T(128)} %bitcast.sign_ref, bf16[256,2304]{1,0:T(8,128)(2,1)S(1)} %get-tuple-element.26.left_ref, bf16[2064,128]{1,0:T(8,128)(2,1)S(1)} %collective-permute-done.1.v1, bf16[2064,128]{1,0:T(8,128)(2,1)S(1)} %collective-permute-done.2.u1, bf16[2064,128]{1,0:T(8,128)(2,1)S(1)} %collective-permute-done.3.xv1, ...), custom_call_target="tpu_custom_call" | custom-call | bytes 104857 | tf_op jit(solution)/shard_map/pallas_call | solution.py:256
Async XLA Ops:
  2.1 11.8 %collective-permute-start = (bf16[2064,128]{1,0:T(8,128)(2,1)S(1)}, bf16[2064,128]{1,0:T(8,128)(2,1)S(1)}, u32[]{:S(2)}, u32[]{:S(2)}) collective-permute-start(bf16[2064,128]{1,0:T(8,128)(2,1)S(1)} %shard_map.28.own), channel_id=1, source_target_pairs={{0,1},{1,0},{2,3},{3,2},{4,5},{5,4},{6,7},{7,6},{8,9},{9,8},{10,11... | collective-permute-start | bytes 1585160 | tf_op jit(solution)/shard_map/ppermute | solution.py:304
  5.5 20.8 %collective-permute-start.2 = (bf16[2064,128]{1,0:T(8,128)(2,1)S(1)}, bf16[2064,128]{1,0:T(8,128)(2,1)S(1)}, u32[]{:S(2)}, u32[]{:S(2)}) collective-permute-start(bf16[2064,128]{1,0:T(8,128)(2,1)S(1)} %shard_map.28.own), channel_id=1, source_target_pairs={{254,0},{255,1},{0,2},{1,3},{2,4},{3,5},{4,6},{5,7},{6,8},{7,9},{8... | collective-permute-start | bytes 1585160 | tf_op jit(solution)/shard_map/ppermute | solution.py:301
  5.5 21.8 %collective-permute-start.1 = (bf16[2064,128]{1,0:T(8,128)(2,1)S(1)}, bf16[2064,128]{1,0:T(8,128)(2,1)S(1)}, u32[]{:S(2)}, u32[]{:S(2)}) collective-permute-start(bf16[2064,128]{1,0:T(8,128)(2,1)S(1)} %shard_map.28.own), channel_id=1, source_target_pairs={{2,0},{3,1},{4,2},{5,3},{6,4},{7,5},{8,6},{9,7},{10,8},{11,9},{12,... | collective-permute-start | bytes 1585160 | tf_op jit(solution)/shard_map/ppermute | solution.py:301
  14.6 19.5 %collective-permute-start.5 = (bf16[2064,128]{1,0:T(8,128)(2,1)S(1)}, bf16[2064,128]{1,0:T(8,128)(2,1)S(1)}, u32[]{:S(2)}, u32[]{:S(2)}) collective-permute-start(bf16[2064,128]{1,0:T(8,128)(2,1)S(1)} %shard_map.28.own), channel_id=1, source_target_pairs={{6,0},{251,1},{8,2},{253,3},{10,4},{255,5},{12,6},{1,7},{14,8},{3,... | collective-permute-start | bytes 1585160 | tf_op jit(solution)/shard_map/ppermute | solution.py:298
  26.2 9.0 %collective-permute-start.4 = (bf16[2064,128]{1,0:T(8,128)(2,1)S(1)}, bf16[2064,128]{1,0:T(8,128)(2,1)S(1)}, u32[]{:S(2)}, u32[]{:S(2)}) collective-permute-start(bf16[2064,128]{1,0:T(8,128)(2,1)S(1)} %collective-permute-done.2.u1), channel_id=1, source_target_pairs={{0,1},{1,0},{2,3},{3,2},{4,5},{5,4},{6,7},{7,6},{8,9},{9,8},{10,11... | collective-permute-start | bytes 1585160 | tf_op jit(solution)/shard_map/ppermute | solution.py:304
  27.2 8.0 %collective-permute-start.3 = (bf16[2064,128]{1,0:T(8,128)(2,1)S(1)}, bf16[2064,128]{1,0:T(8,128)(2,1)S(1)}, u32[]{:S(2)}, u32[]{:S(2)}) collective-permute-start(bf16[2064,128]{1,0:T(8,128)(2,1)S(1)} %collective-permute-done.1.v1), channel_id=1, source_target_pairs={{0,1},{1,0},{2,3},{3,2},{4,5},{5,4},{6,7},{7,6},{8,9},{9,8},{10,11... | collective-permute-start | bytes 1585160 | tf_op jit(solution)/shard_map/ppermute | solution.py:304
  27.2 18.5 %collective-permute-start.6 = (bf16[2064,128]{1,0:T(8,128)(2,1)S(1)}, bf16[2064,128]{1,0:T(8,128)(2,1)S(1)}, u32[]{:S(2)}, u32[]{:S(2)}) collective-permute-start(bf16[2064,128]{1,0:T(8,128)(2,1)S(1)} %collective-permute-done.2.u1), channel_id=1, source_target_pairs={{254,0},{255,1},{0,2},{1,3},{2,4},{3,5},{4,6},{5,7},{6,8},{7,9},{8... | collective-permute-start | bytes 1585160 | tf_op jit(solution)/shard_map/ppermute | solution.py:301
  27.2 18.5 %collective-permute-start.7 = (bf16[2064,128]{1,0:T(8,128)(2,1)S(1)}, bf16[2064,128]{1,0:T(8,128)(2,1)S(1)}, u32[]{:S(2)}, u32[]{:S(2)}) collective-permute-start(bf16[2064,128]{1,0:T(8,128)(2,1)S(1)} %collective-permute-done.1.v1), channel_id=1, source_target_pairs={{2,0},{3,1},{4,2},{5,3},{6,4},{7,5},{8,6},{9,7},{10,8},{11,9},{12,... | collective-permute-start | bytes 1585160 | tf_op jit(solution)/shard_map/ppermute | solution.py:301
  34.2 18.3 %collective-permute-start.10 = (bf16[2064,128]{1,0:T(8,128)(2,1)S(1)}, bf16[2064,128]{1,0:T(8,128)(2,1)S(1)}, u32[]{:S(2)}, u32[]{:S(2)}) collective-permute-start(bf16[2064,128]{1,0:T(8,128)(2,1)S(1)} %collective-permute-done.5.f3), channel_id=1, source_target_pairs={{0,1},{1,0},{2,3},{3,2},{4,5},{5,4},{6,7},{7,6},{8,9},{9,8},{10,11... | collective-permute-start | bytes 1585160 | tf_op jit(solution)/shard_map/ppermute | solution.py:304
  37.9 14.1 %collective-permute-start.11 = (bf16[2064,128]{1,0:T(8,128)(2,1)S(1)}, bf16[2064,128]{1,0:T(8,128)(2,1)S(1)}, u32[]{:S(2)}, u32[]{:S(2)}) collective-permute-start(bf16[2064,128]{1,0:T(8,128)(2,1)S(1)} %shard_map.28.own), channel_id=1, source_target_pairs={{250,0},{7,1},{252,2},{9,3},{254,4},{11,5},{0,6},{13,7},{2,8},{15,... | collective-permute-start | bytes 1585160 | tf_op jit(solution)/shard_map/ppermute | solution.py:298
  45.7 6.7 %collective-permute-start.8 = (bf16[2064,128]{1,0:T(8,128)(2,1)S(1)}, bf16[2064,128]{1,0:T(8,128)(2,1)S(1)}, u32[]{:S(2)}, u32[]{:S(2)}) collective-permute-start(bf16[2064,128]{1,0:T(8,128)(2,1)S(1)} %collective-permute-done.7.v2), channel_id=1, source_target_pairs={{0,1},{1,0},{2,3},{3,2},{4,5},{5,4},{6,7},{7,6},{8,9},{9,8},{10,11... | collective-permute-start | bytes 1585160 | tf_op jit(solution)/shard_map/ppermute | solution.py:304
  47.6 4.8 %collective-permute-start.9 = (bf16[2064,128]{1,0:T(8,128)(2,1)S(1)}, bf16[2064,128]{1,0:T(8,128)(2,1)S(1)}, u32[]{:S(2)}, u32[]{:S(2)}) collective-permute-start(bf16[2064,128]{1,0:T(8,128)(2,1)S(1)} %collective-permute-done.6.u2), channel_id=1, source_target_pairs={{0,1},{1,0},{2,3},{3,2},{4,5},{5,4},{6,7},{7,6},{8,9},{9,8},{10,11... | collective-permute-start | bytes 1585160 | tf_op jit(solution)/shard_map/ppermute | solution.py:304
